TPU v7x, 512 devices: a whole 4x8x8 slice. The times are simulated.
512 devices in a mesh: seq: 128 (over z, y, core), head: 4 (over x).
Axes of the slice: x: 4, y: 8, z: 8, core: 2. Of those that a mesh axis runs over, the one named last changes fastest.
Arguments:
- hidden_states: bfloat16 [32768, 1536], P('seq', 'head'), may hold values from -60 to 60
- feature_q: bfloat16 [1536, 384], P(None, 'head'), may hold values from -0.15625 to 0.15625
- feature_k: bfloat16 [1536, 384], P(None, 'head'), may hold values from -0.15625 to 0.15625
- value_w: bfloat16 [1536, 1536], P(None, 'head'), may hold values from -0.15625 to 0.15625
- window_q: bfloat16 [1536, 1536], P(None, 'head'), may hold values from -0.15625 to 0.15625
- window_k: bfloat16 [1536, 1536], P(None, 'head'), may hold values from -0.15625 to 0.15625
- norm_gain: float32 [1536], P('head'), may hold values from 0.5 to 1.5
Outputs:
- mixed: bfloat16 [32768, 1536], P('seq', 'head')
All inputs are finite; a program needn't handle non-finite values.
Results may differ from a plain program's by a relative error of at most 0.007.
Values may be sent and summed in bfloat16 or wider, within the bound.
No kernel may reach another device: no remote copies, remote signals or barrier semaphores. Data moves between devices by JAX's collectives and lax.ppermute only.
A program may use at most 128 MiB of HBM per device.

v0:
```python
import jax
import jax.numpy as jnp
import numpy as np
from jax import lax
from jax.sharding import Mesh
from jax.sharding import PartitionSpec as P

FK = 16
HV = 64
WINDOW_HEAD_SIZE = 64
WIN = 64
SEQ = ("seq_0", "seq_1", "seq_2")


HIGH_ACCURACY = lax.Precision.HIGHEST


def in_order(blocks, dim):
    blocks = jnp.moveaxis(blocks, 0, dim)
    lengths = blocks.shape
    return blocks.reshape(*lengths[:dim], lengths[dim] * lengths[dim + 1], *lengths[dim + 2 :])


def copy_for_each(shard, axis):
    copies = jnp.broadcast_to(shard, (lax.axis_size(axis), *shard.shape))
    return lax.all_to_all(copies, axis, split_axis=0, concat_axis=0, tiled=True)


def collect(shard, axis, dim):
    return in_order(copy_for_each(shard, axis), dim)


def from_behind(shard, axis, by):
    devices = lax.axis_size(axis)
    pairs = [(i, i + by) for i in range(devices) if 0 <= i + by < devices]
    return lax.ppermute(shard, axis, pairs)


def filled_with(shard, identity):
    return jnp.broadcast_to(jnp.asarray(identity, shard.dtype), shard.shape)


def carried_in(shard, axes, combine, identity):
    before = start = filled_with(shard, identity)
    so_far = shard
    for axis in reversed(axes):
        devices, place = (lax.axis_size(axis), lax.axis_index(axis))
        pieces = lax.all_gather(so_far, axis)
        inside, so_far = (start, start)
        for k in range(devices):
            passed = k < place
            so_far = combine(so_far, pieces[k])
            inside = jnp.where(passed, so_far, inside)
        before = combine(inside, before)
    return before


def expand(x):
    lead = x.shape[:-1]
    width = x.shape[-1]
    ones = jnp.ones(lead + (1,), jnp.float32)
    upper, lower = np.triu_indices(width)
    weight = np.where(upper == lower, 0.5**0.5, 1.0).astype(np.float32)
    quad = x[..., upper] * x[..., lower] * weight
    return jnp.concatenate([ones, x, quad], axis=-1)


def add_states(earlier, later):
    return earlier + later


def body(hidden_states, feature_q, feature_k, value_w, window_q, window_k, norm_gain):
    rows = hidden_states.shape[0]
    heads = feature_q.shape[1] // FK
    offset = lax.axis_index(SEQ) * rows
    whole = collect(hidden_states, "head", 1)
    query = (jnp.dot(whole, feature_q, preferred_element_type=jnp.float32) * FK ** (-0.25)).reshape(
        rows, heads, FK
    )
    key = (jnp.dot(whole, feature_k, preferred_element_type=jnp.float32) * FK ** (-0.25)).reshape(
        rows, heads, FK
    )
    wquery = jnp.dot(whole, window_q, preferred_element_type=jnp.float32).astype(jnp.bfloat16)
    wkey = jnp.dot(whole, window_k, preferred_element_type=jnp.float32).astype(jnp.bfloat16)
    values_ext = jnp.dot(whole, value_w, preferred_element_type=jnp.float32).astype(jnp.bfloat16)
    prev_keys, prev_values = from_behind((wkey[rows - WIN :], values_ext[rows - WIN :]), SEQ, 1)
    key_rows_full = jnp.concatenate([prev_keys, wkey], axis=0)
    values_all = jnp.concatenate([prev_values, values_ext], axis=0)
    value3 = values_ext.reshape(rows, heads, HV)
    phi_q = expand(query)
    phi_k = expand(key)
    width = phi_k.shape[-1]
    local_state = jnp.einsum(
        "lhf,lhv->fhv", phi_k, value3.astype(jnp.float32), precision=HIGH_ACCURACY
    ).reshape(width, heads * HV)
    prefix = carried_in(local_state, SEQ, add_states, jnp.zeros_like(local_state))
    inner = jnp.einsum("lhf,mhf->hlm", query, key, precision=HIGH_ACCURACY)
    kernel = 1.0 + inner + 0.5 * inner * inner
    index_rows = jnp.arange(rows, dtype=jnp.int32)
    causal = index_rows[:, None] >= index_rows[None, :]
    kernel = jnp.where(causal[None], kernel, 0.0).astype(jnp.bfloat16)
    intra = jnp.einsum("hlm,mhv->lhv", kernel, value3, preferred_element_type=jnp.float32)
    cross = jnp.einsum(
        "lhf,fhv->lhv", phi_q, prefix.reshape(width, heads, HV), precision=HIGH_ACCURACY
    )
    linear = intra + cross
    scale = lax.rsqrt(jnp.mean(linear * linear, axis=-1, keepdims=True) + 1e-05)
    normed = linear * scale * norm_gain.reshape(heads, HV)
    query_weight3 = wquery.reshape(rows, heads, WINDOW_HEAD_SIZE)
    key_tensor3 = key_rows_full.reshape(rows + WIN, heads, WINDOW_HEAD_SIZE)
    window_logits = jnp.einsum(
        "qxo,bxo->xqb", query_weight3, key_tensor3, preferred_element_type=jnp.float32
    ) * WINDOW_HEAD_SIZE ** (-0.5)
    query_pos = offset + index_rows[:, None]
    key_pos = offset - WIN + jnp.arange(rows + WIN, dtype=jnp.int32)[None, :]
    valid = (key_pos <= query_pos) & (key_pos > query_pos - WIN) & (key_pos >= 0)
    window_logits = jnp.where(valid[None], window_logits, -1e30)
    top = jnp.max(window_logits, axis=-1, keepdims=True)
    expw = jnp.exp(window_logits - top)
    weights = (expw / jnp.sum(expw, axis=-1, keepdims=True)).astype(jnp.bfloat16)
    window = jnp.einsum(
        "hlm,mhv->lhv",
        weights,
        values_all.reshape(rows + WIN, heads, HV),
        preferred_element_type=jnp.float32,
    )
    return (normed + window).astype(jnp.bfloat16).reshape(rows, heads * HV)


def solution(mesh):
    split = Mesh(
        mesh.devices.reshape(8, 8, 2, mesh.shape["head"]), ("seq_0", "seq_1", "seq_2", "head")
    )
    placed = (
        P(SEQ, "head"),
        P(None, "head"),
        P(None, "head"),
        P(None, "head"),
        P(None, "head"),
        P(None, "head"),
        P("head"),
    )
    return jax.shard_map(
        body, mesh=split, in_specs=placed, out_specs=P(SEQ, "head"), check_vma=False
    )
```

profile of v0, /device:TPU:2, one launch (start us, length us, event | category | flops | bytes accessed | tf_op | source)
XLA Modules:
  0.0 175.3 jit_solution(3891422970781210131)
XLA Ops:
  6.5 1.2 copy.54
  8.7 9.5 %all-to-all-start = ((bf16[4,256,384]{1,2,0:T(8,128)(2,1)}), bf16[4,256,384]{1,2,0:T(8,128)(2,1)S(1)}, u32[]{:S(2)}, u32[]{:S(2)}) async-start(bf16[4,256,384]{1,2,0:T(8,128)(2,1)} %broadcast_in_dim.53), calls=%async_computation | async-start | bytes 1572864 | tf_op jit(solution)/shard_map/all_to_all | solution.py:26
  18.2 8.0 %all-to-all-done = bf16[4,256,384]{1,2,0:T(8,128)(2,1)S(1)} async-done(((bf16[4,256,384]{1,2,0:T(8,128)(2,1)}), bf16[4,256,384]{1,2,0:T(8,128)(2,1)S(1)}, u32[]{:S(2)}, u32[]{:S(2)}) %all-to-all-start) | async-done | bytes 786464 | tf_op jit(solution)/shard_map/all_to_all | solution.py:26
  27.7 1.8 %gather_fusion.2 = f32[136,256,6]{1,2,0:T(8,128)} fusion(f32[256,6,16]{0,1,2:T(8,128)S(1)} %copy.81, s32[1024]{0:T(1024)S(1)} %pad_clamp_fusion.1), kind=kCustom, calls=%fused_computation.2 | custom fusion | bytes 1671712 | tf_op jit(solution)/shard_map/gather | solution.py:64
  29.5 1.8 %gather_fusion = f32[136,256,6]{1,2,0:T(8,128)} fusion(f32[256,6,16]{0,1,2:T(8,128)S(1)} %copy.56, s32[1024]{0:T(1024)S(1)} %pad_clamp_fusion.1), kind=kCustom, calls=%fused_computation | custom fusion | bytes 1671712 | tf_op jit(solution)/shard_map/gather | solution.py:64
  31.3 1.8 %gather_fusion.1 = f32[136,256,6]{1,2,0:T(8,128)} fusion(f32[256,6,16]{0,1,2:T(8,128)S(1)} %copy.56, s32[1024]{0:T(1024)S(1)} %pad_clamp_fusion), kind=kCustom, calls=%fused_computation.1 | custom fusion | bytes 1671712 | tf_op jit(solution)/shard_map/gather | solution.py:64
  33.9 3.8 %fusion.21 = (f32[256,6,136]{0,2,1:T(8,128)}, f32[256,6,136]{0,2,1:T(8,128)S(1)}) fusion(f32[136,256,6]{1,2,0:T(8,128)S(1)} %gather_fusion.3, f32[136,256,6]{1,2,0:T(8,128)} %gather_fusion.2, f32[136]{0:T(256)S(1)} %copy-done.25, f32[136,256,6]{1,2,0:T(8,128)} %gather_fusion.1, f32[136,256,6]{1,2,0:T(8,128)} %gather_fusion), kind=kLoop, calls=%fused_computation.37 | loop fusion | flops 835584 | bytes 5014048 | tf_op jit(solution)/shard_map/mul | solution.py:64
  38.7 2.2 %all_gather.11 = f32[2,153,384]{2,1,0:T(8,128)S(1)} all-gather(f32[1,153,384]{2,1,0:T(8,128)S(1)} %copy.60), channel_id=1, replica_groups=mesh['seq_0'=8,'seq_1'=8,'seq_2'=2,'head'=4] {'seq_2'}, dimensions={0}, use_global_device_ids=true | all-gather | bytes 705024 | tf_op jit(solution)/shard_map/all_gather | solution.py:48
  42.3 45.5 %all-gather.3.cloned.1.call-done = f32[8,153,384]{2,1,0:T(8,128)} async-done(((f32[1,153,384]{2,1,0:T(8,128)}), f32[8,153,384]{2,1,0:T(8,128)}) %all-gather.3.cloned.1.call-update) | async-done | bytes 1880080 | tf_op jit(solution)/shard_map/all_gather | solution.py:48
  87.7 2.7 %fusion.33 = (f32[1,153,384]{2,1,0:T(8,128)}, f32[1,153,384]{2,1,0:T(8,128)S(1)}, f32[1,153,384]{2,1,0:T(8,128)S(1)}, f32[1,153,384]{2,1,0:T(8,128)}, f32[1,153,...) fusion(f32[8,153,384]{2,1,0:T(8,128)} %all-gather.3.cloned.1.call-done), kind=kLoop, calls=%fused_computation.63 | loop fusion | bytes 3760128 | tf_op jit(solution)/shard_map/slice | solution.py:52
  93.1 1.9 %copy.94 = f32[1,153,384]{1,2,0:T(8,128)} copy(f32[1,153,384]{2,1,0:T(8,128)} %get-tuple-element.17) | data formatting | bytes 470016
  94.9 1.9 %copy.93 = f32[1,153,384]{1,2,0:T(8,128)} copy(f32[1,153,384]{2,1,0:T(8,128)} %get-tuple-element.18) | data formatting | bytes 470016
  96.8 1.9 %copy.91 = f32[1,153,384]{1,2,0:T(8,128)} copy(f32[1,153,384]{2,1,0:T(8,128)} %get-tuple-element.19) | data formatting | bytes 470016
  98.7 1.9 %copy.98 = f32[1,153,384]{1,2,0:T(8,128)} copy(f32[1,153,384]{2,1,0:T(8,128)} %get-tuple-element.20) | data formatting | bytes 470016
  100.5 2.3 %add_add_fusion.1 = f32[1,153,384]{1,2,0:T(8,128)} fusion(f32[1,153,384]{1,2,0:T(8,128)} %copy.98, f32[1,153,384]{1,2,0:T(8,128)S(1)} %copy.97, f32[1,153,384]{1,2,0:T(8,128)S(1)} %copy.96, f32[1,153,384]{1,2,0:T(8,128)S(1)} %copy.95, f32[1,153,384]{1,2,0:T(8,128)} %copy.94, f32[1,153,384]{1,2,0:T(8,128)} %copy.93, f32[1,153,384]{1,2,0:T(8,128)} %copy.91, ...), kind=kLoop, calls=%fused_computation.50 | loop fusion | flops 411264 | bytes 2115072 | tf_op jit(solution)/shard_map/add | solution.py:69
  102.9 1.8 %copy.72 = f32[1,153,384]{2,1,0:T(8,128)} copy(f32[1,153,384]{1,2,0:T(8,128)} %add_add_fusion.1) | data formatting | bytes 470016 | tf_op jit(solution)/shard_map/add | solution.py:69
  105.7 1.4 slice.106
  107.1 1.9 %collective-permute-start = (bf16[64,384]{1,0:T(8,128)(2,1)}, bf16[64,384]{1,0:T(8,128)(2,1)}, u32[]{:S(2)}, u32[]{:S(2)}) collective-permute-start(bf16[64,384]{1,0:T(8,128)(2,1)} %slice.106), channel_id=1, source_target_pairs={{0,4},{4,8},{8,12},{12,16},{16,20},{20,24},{24,28},{28,32},{32,36}... | collective-permute-start | bytes 147464 | tf_op jit(solution)/shard_map/ppermute | solution.py:36
  109.0 1.9 %convolution_convert_fusion = bf16[256,384]{1,0:T(8,128)(2,1)S(1)} fusion(bf16[256,1536]{0,1:T(8,128)(2,1)S(1)} %bitcast.49, bf16[1536,384]{1,0:T(8,128)(2,1)} %param.22), kind=kOutput, calls=%fused_computation.17 | convolution fusion | flops 302088192 | bytes 2162688 | tf_op jit(solution)/shard_map/dot_general | solution.py:84
  112.2 3.7 %collective-permute-start.1 = (bf16[64,384]{1,0:T(8,128)(2,1)}, bf16[64,384]{1,0:T(8,128)(2,1)}, u32[]{:S(2)}, u32[]{:S(2)}) collective-permute-start(bf16[64,384]{1,0:T(8,128)(2,1)} %slice.107), channel_id=1, source_target_pairs={{0,4},{4,8},{8,12},{12,16},{16,20},{20,24},{24,28},{28,32},{32,36}... | collective-permute-start | bytes 147464 | tf_op jit(solution)/shard_map/ppermute | solution.py:36
  116.0 1.7 fusion.4
  117.6 1.3 convolution_convert_fusion.1
  120.0 1.8 %copy.86 = bf16[256,384]{0,1:T(8,128)(2,1)} copy(bf16[256,384]{1,0:T(8,128)(2,1)} %convolution_convert_fusion.1) | data formatting | bytes 393216 | tf_op jit(solution)/shard_map/convert_element_type | solution.py:83
  125.3 3.8 %fusion.35 = (f32[6,256]{1,0:T(8,128)}, f32[6,256,320]{1,2,0:T(8,128)}) fusion(pred[256,320]{0,1:T(8,128)(4,1)S(1)} %copy-done.23, bf16[256,6,64]{0,2,1:T(8,128)(2,1)} %bitcast.63, bf16[320,6,64]{0,2,1:T(8,128)(2,1)} %bitcast.62), kind=kOutput, calls=%fused_computation.65 | convolution fusion | flops 64880960 | bytes 2496512 | tf_op jit(solution)/shard_map/sub | solution.py:119
  129.1 19.4 %all-gather.5.cloned.1.call-done = f32[8,153,384]{2,1,0:T(8,128)} async-done(((f32[1,153,384]{2,1,0:T(8,128)}), f32[8,153,384]{2,1,0:T(8,128)}) %all-gather.5.cloned.1.call-update) | async-done | bytes 1880080 | tf_op jit(solution)/shard_map/all_gather | solution.py:48
  148.5 2.7 %fusion.32 = (f32[1,153,384]{2,1,0:T(8,128)S(1)}, f32[1,153,384]{2,1,0:T(8,128)S(1)}, f32[1,153,384]{2,1,0:T(8,128)S(1)}, f32[1,153,384]{2,1,0:T(8,128)}, f32[1,...) fusion(f32[8,153,384]{2,1,0:T(8,128)} %all-gather.5.cloned.1.call-done), kind=kLoop, calls=%fused_computation.62 | loop fusion | bytes 3760128 | tf_op jit(solution)/shard_map/slice | solution.py:52
  154.0 1.9 %copy.103 = f32[1,153,384]{1,2,0:T(8,128)} copy(f32[1,153,384]{2,1,0:T(8,128)} %get-tuple-element.8) | data formatting | bytes 470016
  155.9 1.9 %copy.102 = f32[1,153,384]{1,2,0:T(8,128)} copy(f32[1,153,384]{2,1,0:T(8,128)} %get-tuple-element.9) | data formatting | bytes 470016
  157.8 1.9 %copy.101 = f32[1,153,384]{1,2,0:T(8,128)} copy(f32[1,153,384]{2,1,0:T(8,128)} %get-tuple-element.10) | data formatting | bytes 470016
  159.7 1.9 %copy.99 = f32[1,153,384]{1,2,0:T(8,128)} copy(f32[1,153,384]{2,1,0:T(8,128)} %get-tuple-element.11) | data formatting | bytes 470016
  161.6 1.9 %copy.106 = f32[1,153,384]{1,2,0:T(8,128)} copy(f32[1,153,384]{2,1,0:T(8,128)} %get-tuple-element.12) | data formatting | bytes 470016
  163.5 2.7 %add_add_fusion = f32[1,153,384]{1,2,0:T(8,128)S(1)} fusion(f32[1,153,384]{1,2,0:T(8,128)} %copy.106, f32[1,153,384]{1,2,0:T(8,128)} %copy.105, f32[1,153,384]{1,2,0:T(8,128)} %copy.104, f32[1,153,384]{1,2,0:T(8,128)} %copy-done.4, f32[1,153,384]{1,2,0:T(8,128)} %copy-done.3, f32[1,153,384]{1,2,0:T(8,128)} %copy.91, f32[1,153,384]{1,2,0:T(8,128)} %copy.99, ...), kind=kLoop, calls=%fused_computation.43 | loop fusion | flops 1997568 | bytes 4465170 | tf_op jit(solution)/shard_map/add | solution.py:69
  (107 shorter events, 19.9 us)
Async XLA Ops:
  6.5 26.5 %copy-start = (bf16[1536,384]{1,0:T(8,128)(2,1)S(1)}, bf16[1536,384]{1,0:T(8,128)(2,1)}, u32[]{:S(2)}) copy-start(bf16[1536,384]{1,0:T(8,128)(2,1)} %param.20) | copy-start | bytes 3538948
  6.5 11.6 %copy-start.27 = (s32[136]{0:T(256)S(1)}, s32[136]{0:T(256)}, u32[]{:S(2)}) copy-start(s32[136]{0:T(256)} %constant.76) | copy-start | bytes 1636
  6.5 11.7 %copy-start.26 = (s32[136]{0:T(256)S(1)}, s32[136]{0:T(256)}, u32[]{:S(2)}) copy-start(s32[136]{0:T(256)} %constant.77) | copy-start | bytes 1636
  6.5 19.7 %copy-start.21 = (bf16[1536,96]{0,1:T(8,128)(2,1)S(1)}, bf16[1536,96]{0,1:T(8,128)(2,1)}, u32[]{:S(2)}) copy-start(bf16[1536,96]{0,1:T(8,128)(2,1)} %param.18) | copy-start | bytes 884740
  8.7 17.8 %copy-start.22 = (bf16[1536,96]{0,1:T(8,128)(2,1)S(1)}, bf16[1536,96]{0,1:T(8,128)(2,1)}, u32[]{:S(2)}) copy-start(bf16[1536,96]{0,1:T(8,128)(2,1)} %param.19) | copy-start | bytes 884740
  8.7 17.5 %all-to-all-start = ((bf16[4,256,384]{1,2,0:T(8,128)(2,1)}), bf16[4,256,384]{1,2,0:T(8,128)(2,1)S(1)}, u32[]{:S(2)}, u32[]{:S(2)}) async-start(bf16[4,256,384]{1,2,0:T(8,128)(2,1)} %broadcast_in_dim.53), calls=%async_computation | async-start | bytes 1572864 | tf_op jit(solution)/shard_map/all_to_all | solution.py:26
  18.2 69.6 %all-gather.3.cloned.1.call-start = ((), (), s32[]{:S(2)}) async-start(), calls=%async_computation.1 | async-start | bytes 2211840 | tf_op jit(solution)/shard_map/all_gather | solution.py:48
  26.5 1.2 copy-start.14
  33.7 4.0 %copy-start.6 = (bf16[256,384]{1,0:T(8,128)(2,1)}, bf16[256,384]{1,0:T(8,128)(2,1)S(1)}, u32[]{:S(2)}) copy-start(bf16[256,384]{1,0:T(8,128)(2,1)S(1)} %convolution_convert_fusion.2) | copy-start | bytes 589828
  33.8 3.9 %copy-start.8 = (bf16[256,384]{0,1:T(8,128)(2,1)}, bf16[256,384]{0,1:T(8,128)(2,1)S(1)}, u32[]{:S(2)}) copy-start(bf16[256,384]{0,1:T(8,128)(2,1)S(1)} %copy.55) | copy-start | bytes 589828
  33.8 3.9 %copy-start.18 = (f32[256,96]{0,1:T(8,128)S(1)}, f32[256,96]{0,1:T(8,128)}, u32[]{:S(2)}) copy-start(f32[256,96]{0,1:T(8,128)} %copy-done.17) | copy-start | bytes 294916
  41.2 49.3 %copy-start.3 = (f32[1,153,384]{1,2,0:T(8,128)}, f32[1,153,384]{1,2,0:T(8,128)S(1)}, u32[]{:S(2)}) copy-start(f32[1,153,384]{1,2,0:T(8,128)S(1)} %copy.89) | copy-start | bytes 705028
  41.3 49.2 %copy-start.4 = (f32[1,153,384]{1,2,0:T(8,128)}, f32[1,153,384]{1,2,0:T(8,128)S(1)}, u32[]{:S(2)}) copy-start(f32[1,153,384]{1,2,0:T(8,128)S(1)} %add.182) | copy-start | bytes 705028
  42.2 106.3 %all-gather.5.cloned.1.call-start = ((), (), s32[]{:S(2)}) async-start(), calls=%async_computation.2 | async-start | bytes 2211840 | tf_op jit(solution)/shard_map/all_gather | solution.py:48
  100.5 4.2 %copy-start.24 = (f32[384]{0:T(512)S(1)}, f32[384]{0:T(512)}, u32[]{:S(2)}) copy-start(f32[384]{0:T(512)} %param.23) | copy-start | bytes 4612
  104.9 11.1 %copy-start.15 = (f32[256,96]{0,1:T(8,128)S(1)}, f32[256,96]{0,1:T(8,128)}, u32[]{:S(2)}) copy-start(f32[256,96]{0,1:T(8,128)} %copy-done.14) | copy-start | bytes 294916
  104.9 11.1 %copy-start.19 = (f32[256,96]{0,1:T(8,128)S(1)}, f32[256,96]{0,1:T(8,128)}, u32[]{:S(2)}) copy-start(f32[256,96]{0,1:T(8,128)} %copy-done.17) | copy-start | bytes 294916
  107.1 16.4 %collective-permute-start = (bf16[64,384]{1,0:T(8,128)(2,1)}, bf16[64,384]{1,0:T(8,128)(2,1)}, u32[]{:S(2)}, u32[]{:S(2)}) collective-permute-start(bf16[64,384]{1,0:T(8,128)(2,1)} %slice.106), channel_id=1, source_target_pairs={{0,4},{4,8},{8,12},{12,16},{16,20},{20,24},{24,28},{28,32},{32,36}... | collective-permute-start | bytes 147464 | tf_op jit(solution)/shard_map/ppermute | solution.py:36
  111.6 6.0 %copy-start.11 = (bf16[1536,384]{1,0:T(8,128)(2,1)S(1)}, bf16[1536,384]{1,0:T(8,128)(2,1)}, u32[]{:S(2)}) copy-start(bf16[1536,384]{1,0:T(8,128)(2,1)} %param.21) | copy-start | bytes 3538948
  112.2 9.6 %collective-permute-start.1 = (bf16[64,384]{1,0:T(8,128)(2,1)}, bf16[64,384]{1,0:T(8,128)(2,1)}, u32[]{:S(2)}, u32[]{:S(2)}) collective-permute-start(bf16[64,384]{1,0:T(8,128)(2,1)} %slice.107), channel_id=1, source_target_pairs={{0,4},{4,8},{8,12},{12,16},{16,20},{20,24},{24,28},{28,32},{32,36}... | collective-permute-start | bytes 147464 | tf_op jit(solution)/shard_map/ppermute | solution.py:36
  117.6 1.3 copy-start.9
  118.9 2.9 %copy-start.13 = (bf16[256,384]{1,0:T(8,128)(2,1)S(1)}, bf16[256,384]{1,0:T(8,128)(2,1)}, u32[]{:S(2)}) copy-start(bf16[256,384]{1,0:T(8,128)(2,1)} %copy-done.12) | copy-start | bytes 589828
  118.9 4.7 %copy-start.7 = (bf16[256,384]{1,0:T(8,128)(2,1)S(1)}, bf16[256,384]{1,0:T(8,128)(2,1)}, u32[]{:S(2)}) copy-start(bf16[256,384]{1,0:T(8,128)(2,1)} %copy-done.6) | copy-start | bytes 589828
  120.0 5.3 %copy-start.23 = (pred[256,320]{0,1:T(8,128)(4,1)S(1)}, pred[256,320]{0,1:T(8,128)(4,1)}, u32[]{:S(2)}) copy-start(pred[256,320]{0,1:T(8,128)(4,1)} %and_and_fusion) | copy-start | bytes 245764
  154.0 9.5 %copy-start.1 = (f32[1,153,384]{1,2,0:T(8,128)S(1)}, f32[1,153,384]{1,2,0:T(8,128)}, u32[]{:S(2)}) copy-start(f32[1,153,384]{1,2,0:T(8,128)} %copy.94) | copy-start | bytes 705028
  154.0 9.5 %copy-start.2 = (f32[1,153,384]{1,2,0:T(8,128)S(1)}, f32[1,153,384]{1,2,0:T(8,128)}, u32[]{:S(2)}) copy-start(f32[1,153,384]{1,2,0:T(8,128)} %copy.93) | copy-start | bytes 705028
  163.5 2.8 %copy-start.5 = (f32[256,6,136]{0,2,1:T(8,128)S(1)}, f32[256,6,136]{0,2,1:T(8,128)}, u32[]{:S(2)}) copy-start(f32[256,6,136]{0,2,1:T(8,128)} %get-tuple-element.23) | copy-start | bytes 2506756
  163.5 2.8 %copy-start.10 = (f32[6,64,256]{2,1,0:T(8,128)S(1)}, f32[6,64,256]{2,1,0:T(8,128)}, u32[]{:S(2)}) copy-start(f32[6,64,256]{2,1,0:T(8,128)} %fusion.36) | copy-start | bytes 1179652
  163.5 2.8 %copy-start.16 = (f32[256,96]{0,1:T(8,128)S(1)}, f32[256,96]{0,1:T(8,128)}, u32[]{:S(2)}) copy-start(f32[256,96]{0,1:T(8,128)} %copy-done.14) | copy-start | bytes 294916
  163.5 3.7 %copy-start.28 = (f32[6,256,320]{1,2,0:T(8,128)S(1)}, f32[6,256,320]{1,2,0:T(8,128)}, u32[]{:S(2)}) copy-start(f32[6,256,320]{1,2,0:T(8,128)} %get-tuple-element.26) | copy-start | bytes 5898244
  166.3 1.1 copy-start.20
  166.3 1.0 copy-start.29
  (3 other events, 2.4 us)
Sparse Core Ops, SparseCore 0:
  42.3 45.3 all-gather.2
  104.9 43.5 all-gather.4
where the time goes:
time: 176 us; the launch traced here: 175 us
  waiting for transfers between devices  72.9 us (41%)
  local copies, waits for them, and re-layouts  46.9 us (27%)
  starting transfers between devices  15.2 us (9%)
  between operations  13.9 us (8%)
  matrix products  12.9 us (7%)
  other arithmetic  11.5 us (7%)
  blocking collectives  2.16 us (1%)
    all_gather x2, waiting for transfers between devices, carried_in(): pieces = lax.all_gather(so_far, axis)  64.9 us
    unnamed x79, local copies, waits for them, and re-layouts  24.7 us
    all_to_all x1, starting transfers between devices, copy_for_each(): return lax.all_to_all(copies, axis, split_axis=0, concat_axis=0, tiled=True)  9.5 us
    all_to_all x1, waiting for transfers between devices, copy_for_each(): return lax.all_to_all(copies, axis, split_axis=0, concat_axis=0, tiled=True)  7.98 us
    gather x4, local copies, waits for them, and re-layouts, expand(): quad = x[..., upper] * x[..., lower] * weight  6.11 us
    ppermute x2, starting transfers between devices, from_behind(): return lax.ppermute(shard, axis, pairs)  5.62 us
    slice x3, local copies, waits for them, and re-layouts, carried_in(): so_far = combine(so_far, pieces[k])  5.46 us
    add x3, other arithmetic, add_states(): return earlier + later  5.12 us
  transfers between devices with their start and end apart: 5, of which 3 were waited for; matrix products, arithmetic and copies ran while one was open for 10% of the time, Pallas kernels for 0%

commit v1 on v0

v1 whole, which is shorter than its diff:
```python
import functools

import jax
import jax.numpy as jnp
from jax import lax
from jax.experimental import pallas as pl
from jax.experimental.pallas import tpu as pltpu
from jax.sharding import Mesh
from jax.sharding import PartitionSpec as P

FK = 16
HV = 64
WIN = 64
ROLLS = 8
BLOCKS = ROLLS + 2
PAIR_ROWS = BLOCKS * FK
SEQ = ("seq_0", "seq_1", "seq_2")
PLANE = ("seq_1", "seq_2")
F32 = jnp.float32
BF16 = jnp.bfloat16
NT = (((1,), (1,)), ((), ()))
VMEM_BYTES = 40 << 20


def dot(a, b):
    return jnp.dot(a, b, preferred_element_type=F32)


def project_transposed(w_ref, x_ref, rows, chunks):
    depth = x_ref.shape[1]
    total = None
    for c in range(chunks):
        part = lax.dot_general(
            w_ref[:, c * depth : (c + 1) * depth],
            x_ref[c * rows : (c + 1) * rows, :],
            NT,
            preferred_element_type=F32,
        )
        total = part if total is None else total + part
    return total * FK ** (-0.25)


def project(x_ref, w_ref, rows, chunks):
    depth = x_ref.shape[1]
    total = None
    for c in range(chunks):
        part = dot(x_ref[c * rows : (c + 1) * rows, :], w_ref[c * depth : (c + 1) * depth, :])
        total = part if total is None else total + part
    return total


def features(xt, weight, one):
    total, tokens = xt.shape
    x3 = xt.reshape(total // FK, FK, tokens)
    blocks = [(xt * xt * weight).astype(BF16)]
    for d in range(1, ROLLS):
        rolled = jnp.concatenate([x3[:, d:], x3[:, :d]], axis=1)
        blocks.append((x3 * rolled).reshape(total, tokens).astype(BF16))
    blocks.append(xt.astype(BF16))
    half = x3[:, : FK // 2] * x3[:, FK // 2 :]
    mixed = jnp.concatenate([half, jnp.full_like(half, one)], axis=1)
    blocks.append(mixed.reshape(total, tokens).astype(BF16))
    return blocks


def low_half(shape):
    return lax.broadcasted_iota(jnp.int32, shape, len(shape) - 1) < HV


def state_kernel(rows, chunks, x_ref, wk_ref, wv_ref, state_ref, kt_ref, v_ref):
    v = project(x_ref, wv_ref, rows, chunks).astype(BF16)
    v_ref[...] = v
    kt = project_transposed(wk_ref, x_ref, rows, chunks)
    kt_ref[...] = kt
    blocks = features(kt, 1.0, 1.0)
    pairs = v.shape[1] // 128
    for p in range(pairs):
        left = jnp.concatenate([b[32 * p : 32 * p + 32] for b in blocks], axis=0)
        both = dot(left, v[:, 128 * p : 128 * p + 128]).reshape(BLOCKS, 2, FK, 128)
        one = jnp.where(low_half((BLOCKS, FK, 128)), both[:, 0], both[:, 1])
        state_ref[PAIR_ROWS * p : PAIR_ROWS * (p + 1), :] = one.reshape(PAIR_ROWS, 128).astype(BF16)
    used = PAIR_ROWS * pairs
    state_ref[used:, :] = jnp.zeros((state_ref.shape[0] - used, 128), BF16)


def window_project_kernel(rows, chunks, x_ref, wq_ref, wk_ref, v_ref, oq_ref, ok_ref, halo_ref):
    oq_ref[...] = project(x_ref, wq_ref, rows, chunks).astype(BF16)
    keys = project(x_ref, wk_ref, rows, chunks).astype(BF16)
    ok_ref[...] = keys
    width = keys.shape[1]
    halo_ref[:, :width] = keys[rows - WIN :]
    halo_ref[:, width:] = v_ref[rows - WIN :, :]


def intra_kernel(rows, chunks, x_ref, wq_ref, kt_ref, v_ref, intra_ref, phi_ref):
    qt = project_transposed(wq_ref, x_ref, rows, chunks)
    blocks = features(qt, 0.5, 1.0 / (FK // 2))
    heads = qt.shape[0] // FK
    pad = jnp.zeros((384 - 2 * PAIR_ROWS, rows), F32)
    kt = kt_ref[...]
    q_hi = qt.astype(BF16).astype(F32)
    q_lo = qt - q_hi
    k_hi = kt.astype(BF16).astype(F32)
    k_lo = kt - k_hi
    zero = jnp.zeros((128 - 3 * FK, rows), F32)
    t = lax.broadcasted_iota(jnp.int32, (rows, rows), 0)
    s = lax.broadcasted_iota(jnp.int32, (rows, rows), 1)
    causal = t >= s
    for p in range(heads // 2):
        phi = jnp.concatenate([b[32 * p : 32 * p + 32].astype(F32) for b in blocks] + [pad], axis=0)
        phi_ref[:, 384 * p : 384 * (p + 1)] = phi.T.astype(BF16)
        vp = v_ref[:, 128 * p : 128 * p + 128]
        outs = []
        for h in (2 * p, 2 * p + 1):
            at = slice(FK * h, FK * (h + 1))
            left = jnp.concatenate([q_hi[at], q_hi[at], q_lo[at], zero], axis=0).T.astype(BF16)
            right = jnp.concatenate([k_hi[at], k_lo[at], k_hi[at], zero], axis=0).astype(BF16)
            a = dot(left, right)
            kern = jnp.where(causal, 1.0 + a + 0.5 * a * a, 0.0).astype(BF16)
            outs.append(dot(kern, vp))
        intra_ref[:, 128 * p : 128 * p + 128] = jnp.where(low_half((rows, 128)), outs[0], outs[1])


def window_kernel(rows, first_ref, q_ref, k_ref, v_ref, halo_ref, out_ref):
    width = k_ref.shape[1]
    first = first_ref[0]
    row = lax.broadcasted_iota(jnp.int32, (2 * WIN, 2 * WIN), 0) % WIN
    col = lax.broadcasted_iota(jnp.int32, (2 * WIN, 2 * WIN), 1)
    band = (col <= row + WIN) & (col > row)
    for t in range(rows // WIN):
        valid = band & ((col >= WIN) | (first == 0)) if t == 0 else band
        for p in range(width // 128):
            at = slice(128 * p, 128 * p + 128)
            if t == 0:
                keys = jnp.concatenate([halo_ref[:, at], k_ref[:WIN, at]], axis=0)
                vals = jnp.concatenate(
                    [halo_ref[:, width + 128 * p : width + 128 * p + 128], v_ref[:WIN, at]], axis=0
                )
            else:
                keys = k_ref[WIN * (t - 1) : WIN * (t + 1), at]
                vals = v_ref[WIN * (t - 1) : WIN * (t + 1), at]
            q = q_ref[WIN * t : WIN * (t + 1), at]
            low = low_half((WIN, 128))
            none = jnp.zeros_like(q)
            both = jnp.concatenate([jnp.where(low, q, none), jnp.where(low, none, q)], axis=0)
            logits = lax.dot_general(both, keys, NT, preferred_element_type=F32) * HV ** (-0.5)
            logits = jnp.where(valid, logits, -1e30)
            top = jnp.max(logits, axis=-1, keepdims=True)
            expw = jnp.exp(logits - top)
            weights = (expw / jnp.sum(expw, axis=-1, keepdims=True)).astype(BF16)
            mixed = dot(weights, vals)
            out_ref[WIN * t : WIN * (t + 1), at] = jnp.where(low, mixed[:WIN], mixed[WIN:])


def prefix_kernel(plane_ref, slices_ref, totals_ref, out_ref):
    plane = plane_ref[0]
    run = jnp.zeros(totals_ref.shape[1:], F32)
    for z in range(totals_ref.shape[0]):
        run = run + jnp.where(z < plane, totals_ref[z], 0.0)
    for i in range(slices_ref.shape[0]):
        out_ref[i] = run.astype(BF16)
        run = run + slices_ref[i].astype(F32)


def final_kernel(rows, state_ref, phi_ref, intra_ref, window_ref, gain_ref, out_ref):
    low_state = low_half((BLOCKS, FK, 128))
    i = lax.broadcasted_iota(jnp.int32, (256, 128), 0) % 128
    j = lax.broadcasted_iota(jnp.int32, (256, 128), 1)
    ones = jnp.where((i < HV) == (j < HV), 1.0 / HV, 0.0).astype(BF16)
    for p in range(intra_ref.shape[1] // 128):
        at = slice(128 * p, 128 * p + 128)
        state = state_ref[PAIR_ROWS * p : PAIR_ROWS * (p + 1), :].reshape(BLOCKS, FK, 128)
        none = jnp.zeros_like(state)
        even = jnp.where(low_state, state, none)[:, None]
        odd = jnp.where(low_state, none, state)[:, None]
        right = jnp.concatenate([even, odd], axis=1).reshape(2 * PAIR_ROWS, 128)
        right = jnp.concatenate([right, jnp.zeros((384 - 2 * PAIR_ROWS, 128), BF16)], axis=0)
        linear = intra_ref[:, at] + dot(phi_ref[:, 384 * p : 384 * (p + 1)], right)
        square = linear * linear
        hi = square.astype(BF16)
        lo = (square - hi.astype(F32)).astype(BF16)
        mean = dot(jnp.concatenate([hi, lo], axis=1), ones)
        normed = linear * lax.rsqrt(mean + 1e-5) * gain_ref[:, at]
        out_ref[:, at] = (normed + window_ref[:, at]).astype(BF16)


def call(kernel, outs, args, flops, scalars=0):
    outs = [jax.ShapeDtypeStruct(s, d) for s, d in outs]
    size = sum(a.size * a.dtype.itemsize for a in list(args) + outs)
    specs = [pl.BlockSpec(memory_space=pltpu.SMEM)] * scalars
    specs += [pl.BlockSpec(memory_space=pltpu.VMEM)] * (len(args) - scalars)
    return pl.pallas_call(
        kernel,
        out_shape=outs,
        in_specs=specs,
        out_specs=[pl.BlockSpec(memory_space=pltpu.VMEM)] * len(outs),
        compiler_params=pltpu.CompilerParams(vmem_limit_bytes=VMEM_BYTES),
        cost_estimate=pl.CostEstimate(flops=flops, bytes_accessed=size, transcendentals=0),
    )(*args)


def exchange(x, axis):
    return lax.all_to_all(x, axis, split_axis=0, concat_axis=0, tiled=True)


def body(hidden_states, feature_q, feature_k, value_w, window_q, window_k, norm_gain):
    rows = hidden_states.shape[0]
    chunks = lax.axis_size("head")
    width = value_w.shape[1]
    model = value_w.shape[0]
    few = feature_k.shape[1]
    planes, members = lax.axis_size("seq_0"), lax.axis_size("seq_1") * lax.axis_size("seq_2")
    plane = lax.axis_index("seq_0").astype(jnp.int32).reshape(1)
    first = (lax.axis_index(SEQ) == 0).astype(jnp.int32).reshape(1)
    piece = FK * members
    held = -(-PAIR_ROWS * width // (128 * piece)) * piece

    whole = lax.all_gather(hidden_states, "head", tiled=True)
    state, kt, v = call(
        functools.partial(state_kernel, rows, chunks),
        [((held, 128), BF16), ((few, rows), F32), ((rows, width), BF16)],
        [whole, feature_k.T, value_w],
        2 * rows * model * (few + width),
    )
    slices = exchange(state.reshape(members, held // members, 128), PLANE)
    wq, wk, halo = call(
        functools.partial(window_project_kernel, rows, chunks),
        [((rows, width), BF16), ((rows, width), BF16), ((WIN, 2 * width), BF16)],
        [whole, window_q, window_k, v],
        4 * rows * model * width,
    )
    devices = lax.axis_size(SEQ)
    halo = lax.ppermute(halo, SEQ, [(i, i + 1) for i in range(devices - 1)])
    total = jnp.sum(slices.astype(F32), axis=0)
    totals = exchange(jnp.broadcast_to(total, (planes, *total.shape)), "seq_0")
    intra, phi = call(
        functools.partial(intra_kernel, rows, chunks),
        [((rows, width), F32), ((rows, 3 * width), BF16)],
        [whole, feature_q.T, kt, v],
        2 * rows * model * few + 8 * rows * rows * width,
    )
    (before,) = call(
        prefix_kernel, [(slices.shape, BF16)], [plane, slices, totals], 10 * slices.size, 1
    )
    prefix = exchange(before, PLANE).reshape(held, 128)
    (window,) = call(
        functools.partial(window_kernel, rows),
        [((rows, width), F32)],
        [first, wq, wk, v, halo],
        16 * rows * WIN * width,
        1,
    )
    (mixed,) = call(
        functools.partial(final_kernel, rows),
        [((rows, width), BF16)],
        [prefix, phi, intra, window, norm_gain.reshape(1, width)],
        4 * rows * 384 * width,
    )
    return mixed


def solution(mesh):
    split = Mesh(
        mesh.devices.reshape(8, 8, 2, mesh.shape["head"]), ("seq_0", "seq_1", "seq_2", "head")
    )
    placed = (
        P(SEQ, "head"),
        P(None, "head"),
        P(None, "head"),
        P(None, "head"),
        P(None, "head"),
        P(None, "head"),
        P("head"),
    )
    return jax.shard_map(
        body, mesh=split, in_specs=placed, out_specs=P(SEQ, "head"), check_vma=False
    )
```

time: 176 us -> 76.9 us (0.44)
  the two profiles are of different devices: /device:TPU:2 before, /device:TPU:1 now
where the time goes in v1:
time: 76.9 us; the launch traced here: 75.9 us
  blocking collectives  32.3 us (42%)
  starting transfers between devices  16.8 us (22%)
  Pallas kernels  11.2 us (15%)
  waiting for transfers between devices  9.62 us (13%)
  local copies, waits for them, and re-layouts  5.83 us (8%)
    all_to_all x1, blocking collectives, exchange(): return lax.all_to_all(x, axis, split_axis=0, concat_axis=0, tiled=True)  20.3 us
    all_to_all x2, starting transfers between devices, exchange(): return lax.all_to_all(x, axis, split_axis=0, concat_axis=0, tiled=True)  13.3 us
    all_gather x1, blocking collectives, body(): whole = lax.all_gather(hidden_states, 'head', tiled=True)  11.9 us
    pallas_call x6, Pallas kernels, call(): pl.pallas_call(kernel, out_shape=outs, in_specs=specs, out_specs=[pl.Bloc...  11.2 us
    all_to_all x2, waiting for transfers between devices, exchange(): return lax.all_to_all(x, axis, split_axis=0, concat_axis=0, tiled=True)  9.62 us
    unnamed x26, local copies, waits for them, and re-layouts  5.16 us
    ppermute x1, starting transfers between devices, body(): halo = lax.ppermute(halo, SEQ, [(i, i + 1) for i in range(devices - 1)])  3.53 us
  transfers between devices with their start and end apart: 3, of which 1 were waited for; matrix products, arithmetic and copies ran while one was open for 0% of the time, Pallas kernels for 10%

profile of v1, /device:TPU:1, one launch (start us, length us, event | category | flops | bytes accessed | tf_op | source)
XLA Modules:
  0.0 75.9 jit_solution(5750157452725701324)
XLA Ops:
  0.0 11.9 %all_gather.3.x_ref = bf16[1024,384]{1,0:T(8,128)(2,1)S(1)} all-gather(bf16[256,384]{1,0:T(8,128)(2,1)} %param.7), channel_id=1, replica_groups=mesh['seq_0'=8,'seq_1'=8,'seq_2'=2,'head'=4] {'head'}, dimensions={0}, use_global_device_ids=true | all-gather | bytes 983040 | tf_op jit(solution)/shard_map/all_gather | solution.py:218
  11.9 0.0 copy-done.4
  11.9 1.3 %copy-done.2 = bf16[1536,384]{1,0:T(8,128)(2,1)S(1)} copy-done((bf16[1536,384]{1,0:T(8,128)(2,1)S(1)}, bf16[1536,384]{1,0:T(8,128)(2,1)}, u32[]{:S(2)}) %copy-start.2) | copy-done | bytes 1179672
  13.2 1.3 %shard_map.73 = (bf16[512,128]{1,0:T(8,128)(2,1)S(1)}, f32[96,256]{1,0:T(8,128)S(1)}, bf16[256,384]{1,0:T(8,128)(2,1)S(1)}) custom-call(bf16[1024,384]{1,0:T(8,128)(2,1)S(1)} %all_gather.3.x_ref, bf16[96,1536]{1,0:T(8,128)(2,1)S(1)} %bitcast.7, bf16[1536,384]{1,0:T(8,128)(2,1)S(1)} %copy-done.2), custom_call_target="tpu_custom_call" | custom-call | flops 377487360 | bytes 2686976 | tf_op jit(solution)/shard_map/pallas_call | solution.py:192
  14.5 0.0 copy-start.10
  14.5 0.0 copy-start
  14.6 20.3 %all_to_all.15.slices_ref = bf16[16,32,128]{2,1,0:T(8,128)(2,1)S(1)} all-to-all(bf16[16,32,128]{2,1,0:T(8,128)(2,1)S(1)} %bitcast.9), channel_id=1, replica_groups=mesh['seq_0'=8,'seq_1'=8,'seq_2'=2,'head'=4] {'seq_1','seq_2'}, dimensions={0} | all-to-all | bytes 262144 | tf_op jit(solution)/shard_map/all_to_all | solution.py:203
  34.9 0.0 copy-done.10
  34.9 0.7 broadcast_in_dim.3
  35.6 9.5 %all-to-all-start.1 = ((f32[8,32,128]{2,1,0:T(8,128)}), f32[8,32,128]{2,1,0:T(8,128)}, u32[]{:S(2)}, u32[]{:S(2)}) async-start(f32[8,32,128]{2,1,0:T(8,128)} %broadcast_in_dim.3), calls=%async_computation.1 | async-start | bytes 262144 | tf_op jit(solution)/shard_map/all_to_all | solution.py:203
  45.1 9.6 %all-to-all-done.1.totals_ref = f32[8,32,128]{2,1,0:T(8,128)} async-done(((f32[8,32,128]{2,1,0:T(8,128)}), f32[8,32,128]{2,1,0:T(8,128)}, u32[]{:S(2)}, u32[]{:S(2)}) %all-to-all-start.1) | async-done | bytes 131104 | tf_op jit(solution)/shard_map/all_to_all | solution.py:203
  54.7 0.9 %shard_map.74 = bf16[16,32,128]{2,1,0:T(8,128)(2,1)S(1)} custom-call(s32[1]{0:T(128)} %bitcast.plane_ref, bf16[16,32,128]{2,1,0:T(8,128)(2,1)S(1)} %all_to_all.15.slices_ref, f32[8,32,128]{2,1,0:T(8,128)} %all-to-all-done.1.totals_ref), custom_call_target="tpu_custom_call" | custom-call | flops 655360 | bytes 393220 | tf_op jit(solution)/shard_map/pallas_call | solution.py:192
  55.6 0.6 copy-done.3
  56.3 3.8 %all-to-all-start.2 = ((bf16[16,32,128]{2,1,0:T(8,128)(2,1)}), bf16[16,32,128]{2,1,0:T(8,128)(2,1)S(1)}, u32[]{:S(2)}, u32[]{:S(2)}) async-start(bf16[16,32,128]{2,1,0:T(8,128)(2,1)} %copy-done.3), calls=%async_computation.2 | async-start | bytes 262144 | tf_op jit(solution)/shard_map/all_to_all | solution.py:203
  60.1 0.0 copy-done.1
  60.1 0.0 copy-done
  60.1 0.0 copy-start.12
  60.1 1.7 %shard_map.76 = (bf16[256,384]{1,0:T(8,128)(2,1)S(1)}, bf16[256,384]{1,0:T(8,128)(2,1)S(1)}, bf16[64,768]{1,0:T(8,128)(2,1)}) custom-call(bf16[1024,384]{1,0:T(8,128)(2,1)S(1)} %all_gather.3.x_ref, bf16[1536,384]{1,0:T(8,128)(2,1)S(1)} %copy-done, bf16[1536,384]{1,0:T(8,128)(2,1)S(1)} %copy-done.1, bf16[256,384]{1,0:T(8,128)(2,1)S(1)} %get-tuple-element.15.v_ref), custom_call_target="tpu_custom_call" | custom-call | flops 603979776 | bytes 3833856 | tf_op jit(solution)/shard_map/pallas_call | solution.py:192
  61.8 0.7 copy-done.6
  62.5 0.7 copy-done.8
  63.2 3.5 %collective-permute-start = (bf16[64,768]{1,0:T(8,128)(2,1)}, bf16[64,768]{1,0:T(8,128)(2,1)S(1)}, u32[]{:S(2)}, u32[]{:S(2)}) collective-permute-start(bf16[64,768]{1,0:T(8,128)(2,1)} %get-tuple-element.20), channel_id=1, source_target_pairs={{0,4},{4,8},{8,12},{12,16},{16,20},{20,24},{24,28},{28,32},{32,36}... | collective-permute-start | bytes 294920 | tf_op jit(solution)/shard_map/ppermute | solution.py:233
  66.8 0.0 copy-done.12
  66.8 0.0 copy-start.5
  66.8 1.0 %copy-done.5 = bf16[1536,96]{0,1:T(8,128)(2,1)S(1)} copy-done((bf16[1536,96]{0,1:T(8,128)(2,1)S(1)}, bf16[1536,96]{0,1:T(8,128)(2,1)}, u32[]{:S(2)}) %copy-start.5) | copy-done | bytes 294936
  67.7 0.9 %copy-done.11 = f32[96,256]{1,0:T(8,128)S(1)} copy-done((f32[96,256]{1,0:T(8,128)S(1)}, f32[96,256]{1,0:T(8,128)}, u32[]{:S(2)}) %copy-start.11) | copy-done | bytes 98328
  68.6 1.7 %shard_map.75 = (f32[256,384]{1,0:T(8,128)S(1)}, bf16[256,1152]{1,0:T(8,128)(2,1)S(1)}) custom-call(bf16[1024,384]{1,0:T(8,128)(2,1)S(1)} %all_gather.3.x_ref, bf16[96,1536]{1,0:T(8,128)(2,1)S(1)} %bitcast.8, f32[96,256]{1,0:T(8,128)S(1)} %copy-done.11, bf16[256,384]{1,0:T(8,128)(2,1)S(1)} %get-tuple-element.15.v_ref), custom_call_target="tpu_custom_call" | custom-call | flops 276824064 | bytes 2359296 | tf_op jit(solution)/shard_map/pallas_call | solution.py:192
  70.4 0.0 collective-permute-done.halo_ref
  70.4 0.0 copy-done.7
  70.4 0.0 copy-done.9
  70.4 4.0 %shard_map.77.window_ref = f32[256,384]{1,0:T(8,128)S(1)} custom-call(s32[1]{0:T(128)} %bitcast.5.first_ref, bf16[256,384]{1,0:T(8,128)(2,1)S(1)} %copy-done.7, bf16[256,384]{1,0:T(8,128)(2,1)S(1)} %copy-done.9, bf16[256,384]{1,0:T(8,128)(2,1)S(1)} %get-tuple-element.15.v_ref, bf16[64,768]{1,0:T(8,128)(2,1)S(1)} %collective-permute-done.halo_ref), custom_call_target="tpu_custom_call" | custom-call | flops 100663296 | bytes 1081348 | tf_op jit(solution)/shard_map/pallas_call | solution.py:192
  74.4 0.0 all-to-all-done.2
  74.4 1.5 %shard_map.78 = bf16[256,384]{1,0:T(8,128)(2,1)} custom-call(bf16[512,128]{1,0:T(8,128)(2,1)S(1)} %bitcast.6, bf16[256,1152]{1,0:T(8,128)(2,1)S(1)} %get-tuple-element.16.phi_ref, f32[256,384]{1,0:T(8,128)S(1)} %get-tuple-element.17.intra_ref, f32[256,384]{1,0:T(8,128)S(1)} %shard_map.77.window_ref, f32[1,384]{1,0:T(1,128)S(1)} %reshape.22.gain_ref), custom_call_target="tpu_custom_call" | custom-call | flops 150994944 | bytes 1705472 | tf_op jit(solution)/shard_map/pallas_call | solution.py:192
  (11 shorter events, 0.0 us)
Async XLA Ops:
  0.0 11.9 %copy-start.4 = (bf16[1536,96]{0,1:T(8,128)(2,1)S(1)}, bf16[1536,96]{0,1:T(8,128)(2,1)}, u32[]{:S(2)}) copy-start(bf16[1536,96]{0,1:T(8,128)(2,1)} %param.9) | copy-start | bytes 884740
  11.9 1.3 %copy-start.2 = (bf16[1536,384]{1,0:T(8,128)(2,1)S(1)}, bf16[1536,384]{1,0:T(8,128)(2,1)}, u32[]{:S(2)}) copy-start(bf16[1536,384]{1,0:T(8,128)(2,1)} %wv_ref.1) | copy-start | bytes 3538948
  13.2 46.9 %copy-start.1 = (bf16[1536,384]{1,0:T(8,128)(2,1)S(1)}, bf16[1536,384]{1,0:T(8,128)(2,1)}, u32[]{:S(2)}) copy-start(bf16[1536,384]{1,0:T(8,128)(2,1)} %wk_ref.1) | copy-start | bytes 3538948
  14.5 20.4 %copy-start.10 = (f32[96,256]{1,0:T(8,128)}, f32[96,256]{1,0:T(8,128)S(1)}, u32[]{:S(2)}) copy-start(f32[96,256]{1,0:T(8,128)S(1)} %get-tuple-element.14.kt_ref) | copy-start | bytes 294916
  14.5 45.5 %copy-start = (bf16[1536,384]{1,0:T(8,128)(2,1)S(1)}, bf16[1536,384]{1,0:T(8,128)(2,1)}, u32[]{:S(2)}) copy-start(bf16[1536,384]{1,0:T(8,128)(2,1)} %wq_ref.1) | copy-start | bytes 3538948
  35.6 19.1 %all-to-all-start.1 = ((f32[8,32,128]{2,1,0:T(8,128)}), f32[8,32,128]{2,1,0:T(8,128)}, u32[]{:S(2)}, u32[]{:S(2)}) async-start(f32[8,32,128]{2,1,0:T(8,128)} %broadcast_in_dim.3), calls=%async_computation.1 | async-start | bytes 262144 | tf_op jit(solution)/shard_map/all_to_all | solution.py:203
  55.6 0.7 copy-start.3
  56.3 18.1 %all-to-all-start.2 = ((bf16[16,32,128]{2,1,0:T(8,128)(2,1)}), bf16[16,32,128]{2,1,0:T(8,128)(2,1)S(1)}, u32[]{:S(2)}, u32[]{:S(2)}) async-start(bf16[16,32,128]{2,1,0:T(8,128)(2,1)} %copy-done.3), calls=%async_computation.2 | async-start | bytes 262144 | tf_op jit(solution)/shard_map/all_to_all | solution.py:203
  60.1 6.7 %copy-start.12 = (f32[384]{0:T(512)S(1)}, f32[384]{0:T(512)}, u32[]{:S(2)}) copy-start(f32[384]{0:T(512)} %param.13) | copy-start | bytes 4612
  61.8 0.7 copy-start.6
  62.5 0.7 copy-start.8
  63.2 7.2 %collective-permute-start = (bf16[64,768]{1,0:T(8,128)(2,1)}, bf16[64,768]{1,0:T(8,128)(2,1)S(1)}, u32[]{:S(2)}, u32[]{:S(2)}) collective-permute-start(bf16[64,768]{1,0:T(8,128)(2,1)} %get-tuple-element.20), channel_id=1, source_target_pairs={{0,4},{4,8},{8,12},{12,16},{16,20},{20,24},{24,28},{28,32},{32,36}... | collective-permute-start | bytes 294920 | tf_op jit(solution)/shard_map/ppermute | solution.py:233
  66.8 1.0 %copy-start.5 = (bf16[1536,96]{0,1:T(8,128)(2,1)S(1)}, bf16[1536,96]{0,1:T(8,128)(2,1)}, u32[]{:S(2)}) copy-start(bf16[1536,96]{0,1:T(8,128)(2,1)} %param.8) | copy-start | bytes 884740
  67.7 0.9 %copy-start.11 = (f32[96,256]{1,0:T(8,128)S(1)}, f32[96,256]{1,0:T(8,128)}, u32[]{:S(2)}) copy-start(f32[96,256]{1,0:T(8,128)} %copy-done.10) | copy-start | bytes 294916
  68.6 1.8 %copy-start.7 = (bf16[256,384]{1,0:T(8,128)(2,1)S(1)}, bf16[256,384]{1,0:T(8,128)(2,1)}, u32[]{:S(2)}) copy-start(bf16[256,384]{1,0:T(8,128)(2,1)} %copy-done.6) | copy-start | bytes 589828
  68.6 1.8 %copy-start.9 = (bf16[256,384]{1,0:T(8,128)(2,1)S(1)}, bf16[256,384]{1,0:T(8,128)(2,1)}, u32[]{:S(2)}) copy-start(bf16[256,384]{1,0:T(8,128)(2,1)} %copy-done.8) | copy-start | bytes 589828

commit v2 on v1

--- a/solution.py
+++ b/solution.py
@@ -19,7 +19,6 @@
 F32 = jnp.float32
 BF16 = jnp.bfloat16
 NT = (((1,), (1,)), ((), ()))
-VMEM_BYTES = 40 << 20
 
 
 def dot(a, b):
@@ -67,37 +66,94 @@
     return lax.broadcasted_iota(jnp.int32, shape, len(shape) - 1) < HV
 
 
-def state_kernel(rows, chunks, x_ref, wk_ref, wv_ref, state_ref, kt_ref, v_ref):
-    v = project(x_ref, wv_ref, rows, chunks).astype(BF16)
+def state_kernel(rows, chunks, x_ref, wk_ref, wv_hbm, state_hbm, v_hbm, wv_ref, state_ref, v_ref, wv_sem, out_sem):
+    depth = x_ref.shape[1]
+    loads = []
+    for c in range(chunks):
+        at = pl.ds(c * depth, depth)
+        loads.append(pltpu.make_async_copy(wv_hbm.at[at], wv_ref.at[at], wv_sem.at[c]))
+        loads[c].start()
+    blocks = features(project_transposed(wk_ref, x_ref, rows, chunks), 1.0, 1.0)
+    total = None
+    for c in range(chunks):
+        loads[c].wait()
+        part = dot(x_ref[c * rows : (c + 1) * rows, :], wv_ref[c * depth : (c + 1) * depth, :])
+        total = part if total is None else total + part
+    v = total.astype(BF16)
     v_ref[...] = v
-    kt = project_transposed(wk_ref, x_ref, rows, chunks)
-    kt_ref[...] = kt
-    blocks = features(kt, 1.0, 1.0)
+    stores = [pltpu.make_async_copy(v_ref, v_hbm, out_sem.at[0])]
+    stores[0].start()
     pairs = v.shape[1] // 128
+    used = PAIR_ROWS * pairs
+    state_ref[used:, :] = jnp.zeros((state_ref.shape[0] - used, 128), BF16)
     for p in range(pairs):
         left = jnp.concatenate([b[32 * p : 32 * p + 32] for b in blocks], axis=0)
         both = dot(left, v[:, 128 * p : 128 * p + 128]).reshape(BLOCKS, 2, FK, 128)
         one = jnp.where(low_half((BLOCKS, FK, 128)), both[:, 0], both[:, 1])
         state_ref[PAIR_ROWS * p : PAIR_ROWS * (p + 1), :] = one.reshape(PAIR_ROWS, 128).astype(BF16)
-    used = PAIR_ROWS * pairs
-    state_ref[used:, :] = jnp.zeros((state_ref.shape[0] - used, 128), BF16)
-
-
-def window_project_kernel(rows, chunks, x_ref, wq_ref, wk_ref, v_ref, oq_ref, ok_ref, halo_ref):
-    oq_ref[...] = project(x_ref, wq_ref, rows, chunks).astype(BF16)
+        size = PAIR_ROWS if p + 1 < pairs else state_ref.shape[0] - PAIR_ROWS * p
+        at = pl.ds(PAIR_ROWS * p, size)
+        stores.append(pltpu.make_async_copy(state_ref.at[at], state_hbm.at[at], out_sem.at[p + 1]))
+        stores[p + 1].start()
+    for store in stores:
+        store.wait()
+
+
+def window_band():
+    row = lax.broadcasted_iota(jnp.int32, (2 * WIN, 2 * WIN), 0) % WIN
+    col = lax.broadcasted_iota(jnp.int32, (2 * WIN, 2 * WIN), 1)
+    return (col <= row + WIN) & (col > row), col
+
+
+def window_tile(q, keys, vals, valid):
+    low = low_half((WIN, 128))
+    none = jnp.zeros_like(q)
+    both = jnp.concatenate([jnp.where(low, q, none), jnp.where(low, none, q)], axis=0)
+    logits = lax.dot_general(both, keys, NT, preferred_element_type=F32) * HV ** (-0.5)
+    logits = jnp.where(valid, logits, -1e30)
+    top = jnp.max(logits, axis=-1, keepdims=True)
+    expw = jnp.exp(logits - top)
+    weights = (expw / jnp.sum(expw, axis=-1, keepdims=True)).astype(BF16)
+    mixed = dot(weights, vals)
+    return jnp.where(low, mixed[:WIN], mixed[WIN:])
+
+
+def window_kernel(rows, chunks, x_ref, wq_ref, wk_ref, v_ref, out_ref, head_ref, halo_ref):
+    queries = project(x_ref, wq_ref, rows, chunks).astype(BF16)
     keys = project(x_ref, wk_ref, rows, chunks).astype(BF16)
-    ok_ref[...] = keys
     width = keys.shape[1]
     halo_ref[:, :width] = keys[rows - WIN :]
     halo_ref[:, width:] = v_ref[rows - WIN :, :]
-
-
-def intra_kernel(rows, chunks, x_ref, wq_ref, kt_ref, v_ref, intra_ref, phi_ref):
+    head_ref[:, :width] = queries[:WIN]
+    head_ref[:, width : 2 * width] = keys[:WIN]
+    head_ref[:, 2 * width :] = v_ref[:WIN, :]
+    band, _ = window_band()
+    for t in range(1, rows // WIN):
+        for p in range(width // 128):
+            at = slice(128 * p, 128 * p + 128)
+            seen = slice(WIN * (t - 1), WIN * (t + 1))
+            out_ref[WIN * (t - 1) : WIN * t, at] = window_tile(
+                queries[WIN * t : WIN * (t + 1), at], keys[seen, at], v_ref[seen, at], band
+            )
+
+
+def first_window_kernel(first_ref, head_ref, halo_ref, out_ref):
+    width = out_ref.shape[1]
+    band, col = window_band()
+    valid = band & ((col >= WIN) | (first_ref[0] == 0))
+    for p in range(width // 128):
+        at, at2, at3 = (slice(n * width + 128 * p, n * width + 128 * p + 128) for n in range(3))
+        keys = jnp.concatenate([halo_ref[:, at], head_ref[:, at2]], axis=0)
+        vals = jnp.concatenate([halo_ref[:, at2], head_ref[:, at3]], axis=0)
+        out_ref[:, at] = window_tile(head_ref[:, at], keys, vals, valid)
+
+
+def intra_kernel(rows, chunks, x_ref, wq_ref, wk_ref, v_ref, intra_ref, phi_ref):
     qt = project_transposed(wq_ref, x_ref, rows, chunks)
+    kt = project_transposed(wk_ref, x_ref, rows, chunks)
     blocks = features(qt, 0.5, 1.0 / (FK // 2))
     heads = qt.shape[0] // FK
     pad = jnp.zeros((384 - 2 * PAIR_ROWS, rows), F32)
-    kt = kt_ref[...]
     q_hi = qt.astype(BF16).astype(F32)
     q_lo = qt - q_hi
     k_hi = kt.astype(BF16).astype(F32)
@@ -121,35 +177,12 @@
         intra_ref[:, 128 * p : 128 * p + 128] = jnp.where(low_half((rows, 128)), outs[0], outs[1])
 
 
-def window_kernel(rows, first_ref, q_ref, k_ref, v_ref, halo_ref, out_ref):
-    width = k_ref.shape[1]
-    first = first_ref[0]
-    row = lax.broadcasted_iota(jnp.int32, (2 * WIN, 2 * WIN), 0) % WIN
-    col = lax.broadcasted_iota(jnp.int32, (2 * WIN, 2 * WIN), 1)
-    band = (col <= row + WIN) & (col > row)
-    for t in range(rows // WIN):
-        valid = band & ((col >= WIN) | (first == 0)) if t == 0 else band
-        for p in range(width // 128):
-            at = slice(128 * p, 128 * p + 128)
-            if t == 0:
-                keys = jnp.concatenate([halo_ref[:, at], k_ref[:WIN, at]], axis=0)
-                vals = jnp.concatenate(
-                    [halo_ref[:, width + 128 * p : width + 128 * p + 128], v_ref[:WIN, at]], axis=0
-                )
-            else:
-                keys = k_ref[WIN * (t - 1) : WIN * (t + 1), at]
-                vals = v_ref[WIN * (t - 1) : WIN * (t + 1), at]
-            q = q_ref[WIN * t : WIN * (t + 1), at]
-            low = low_half((WIN, 128))
-            none = jnp.zeros_like(q)
-            both = jnp.concatenate([jnp.where(low, q, none), jnp.where(low, none, q)], axis=0)
-            logits = lax.dot_general(both, keys, NT, preferred_element_type=F32) * HV ** (-0.5)
-            logits = jnp.where(valid, logits, -1e30)
-            top = jnp.max(logits, axis=-1, keepdims=True)
-            expw = jnp.exp(logits - top)
-            weights = (expw / jnp.sum(expw, axis=-1, keepdims=True)).astype(BF16)
-            mixed = dot(weights, vals)
-            out_ref[WIN * t : WIN * (t + 1), at] = jnp.where(low, mixed[:WIN], mixed[WIN:])
+def total_kernel(slices_ref, out_ref):
+    total = slices_ref[0].astype(F32)
+    for i in range(1, slices_ref.shape[0]):
+        total = total + slices_ref[i].astype(F32)
+    for z in range(out_ref.shape[0]):
+        out_ref[z] = total
 
 
 def prefix_kernel(plane_ref, slices_ref, totals_ref, out_ref):
@@ -162,7 +195,7 @@
         run = run + slices_ref[i].astype(F32)
 
 
-def final_kernel(rows, state_ref, phi_ref, intra_ref, window_ref, gain_ref, out_ref):
+def final_kernel(rows, state_ref, phi_ref, intra_ref, first_ref, window_ref, gain_ref, out_ref):
     low_state = low_half((BLOCKS, FK, 128))
     i = lax.broadcasted_iota(jnp.int32, (256, 128), 0) % 128
     j = lax.broadcasted_iota(jnp.int32, (256, 128), 1)
@@ -181,22 +214,26 @@
         lo = (square - hi.astype(F32)).astype(BF16)
         mean = dot(jnp.concatenate([hi, lo], axis=1), ones)
         normed = linear * lax.rsqrt(mean + 1e-5) * gain_ref[:, at]
-        out_ref[:, at] = (normed + window_ref[:, at]).astype(BF16)
-
-
-def call(kernel, outs, args, flops, scalars=0):
-    outs = [jax.ShapeDtypeStruct(s, d) for s, d in outs]
-    size = sum(a.size * a.dtype.itemsize for a in list(args) + outs)
-    specs = [pl.BlockSpec(memory_space=pltpu.SMEM)] * scalars
-    specs += [pl.BlockSpec(memory_space=pltpu.VMEM)] * (len(args) - scalars)
+        out_ref[:WIN, at] = (normed[:WIN] + first_ref[:, at]).astype(BF16)
+        out_ref[WIN:, at] = (normed[WIN:] + window_ref[:, at]).astype(BF16)
+
+
+def call(kernel, outs, args, flops, scratch=(), vmem=12):
+    arrays = [a if space is pltpu.SMEM else pltpu.with_memory_space_constraint(a, space) for a, space in args]
+    size = sum(a.size * a.dtype.itemsize for a in arrays)
+
+    def spec(space):
+        return pl.BlockSpec(memory_space=pltpu.VMEM if space is pltpu.HBM and not scratch else space)
+
     return pl.pallas_call(
         kernel,
-        out_shape=outs,
-        in_specs=specs,
-        out_specs=[pl.BlockSpec(memory_space=pltpu.VMEM)] * len(outs),
-        compiler_params=pltpu.CompilerParams(vmem_limit_bytes=VMEM_BYTES),
+        out_shape=[space(shape, dtype) for shape, dtype, space in outs],
+        in_specs=[spec(space) for _, space in args],
+        out_specs=[spec(space) for _, _, space in outs],
+        scratch_shapes=list(scratch),
+        compiler_params=pltpu.CompilerParams(vmem_limit_bytes=vmem << 20),
         cost_estimate=pl.CostEstimate(flops=flops, bytes_accessed=size, transcendentals=0),
-    )(*args)
+    )(*arrays)
 
 
 def exchange(x, axis):
@@ -215,45 +252,62 @@
     piece = FK * members
     held = -(-PAIR_ROWS * width // (128 * piece)) * piece
 
+    pairs = width // 128
+    vmem, hbm, smem = pltpu.VMEM, pltpu.HBM, pltpu.SMEM
+
     whole = lax.all_gather(hidden_states, "head", tiled=True)
-    state, kt, v = call(
+    state, v = call(
         functools.partial(state_kernel, rows, chunks),
-        [((held, 128), BF16), ((few, rows), F32), ((rows, width), BF16)],
-        [whole, feature_k.T, value_w],
+        [((held, 128), BF16, hbm), ((rows, width), BF16, hbm)],
+        [(whole, vmem), (feature_k.T, vmem), (value_w, hbm)],
         2 * rows * model * (few + width),
+        scratch=[
+            pltpu.VMEM((model, width), BF16),
+            pltpu.VMEM((held, 128), BF16),
+            pltpu.VMEM((rows, width), BF16),
+            pltpu.SemaphoreType.DMA((chunks,)),
+            pltpu.SemaphoreType.DMA((pairs + 1,)),
+        ],
     )
     slices = exchange(state.reshape(members, held // members, 128), PLANE)
-    wq, wk, halo = call(
-        functools.partial(window_project_kernel, rows, chunks),
-        [((rows, width), BF16), ((rows, width), BF16), ((WIN, 2 * width), BF16)],
-        [whole, window_q, window_k, v],
-        4 * rows * model * width,
-    )
+    window, head, halo = call(
+        functools.partial(window_kernel, rows, chunks),
+        [((rows - WIN, width), F32, hbm), ((WIN, 3 * width), BF16, hbm), ((WIN, 2 * width), BF16, hbm)],
+        [(whole, vmem), (window_q, vmem), (window_k, vmem), (v, hbm)],
+        4 * rows * model * width + 12 * rows * WIN * width,
+    )
+    slices, window, head, halo = lax.optimization_barrier((slices, window, head, halo))
     devices = lax.axis_size(SEQ)
     halo = lax.ppermute(halo, SEQ, [(i, i + 1) for i in range(devices - 1)])
-    total = jnp.sum(slices.astype(F32), axis=0)
-    totals = exchange(jnp.broadcast_to(total, (planes, *total.shape)), "seq_0")
+    (totals,) = call(
+        total_kernel, [((planes, *slices.shape[1:]), F32, hbm)], [(slices, vmem)], slices.size
+    )
+    totals = exchange(totals, "seq_0")
     intra, phi = call(
         functools.partial(intra_kernel, rows, chunks),
-        [((rows, width), F32), ((rows, 3 * width), BF16)],
-        [whole, feature_q.T, kt, v],
-        2 * rows * model * few + 8 * rows * rows * width,
-    )
+        [((rows, width), F32, vmem), ((rows, 3 * width), BF16, vmem)],
+        [(whole, vmem), (feature_q.T, vmem), (feature_k.T, vmem), (v, hbm)],
+        4 * rows * model * few + 8 * rows * rows * width,
+    )
+    totals, intra, phi = lax.optimization_barrier((totals, intra, phi))
     (before,) = call(
-        prefix_kernel, [(slices.shape, BF16)], [plane, slices, totals], 10 * slices.size, 1
+        prefix_kernel,
+        [(slices.shape, BF16, hbm)],
+        [(plane, smem), (slices, vmem), (totals, vmem)],
+        10 * slices.size,
     )
     prefix = exchange(before, PLANE).reshape(held, 128)
-    (window,) = call(
-        functools.partial(window_kernel, rows),
-        [((rows, width), F32)],
-        [first, wq, wk, v, halo],
-        16 * rows * WIN * width,
-        1,
-    )
+    (early,) = call(
+        first_window_kernel,
+        [((WIN, width), F32, vmem)],
+        [(first, smem), (head, vmem), (halo, vmem)],
+        4 * WIN * WIN * width,
+    )
+    gain = norm_gain.reshape(1, width)
     (mixed,) = call(
         functools.partial(final_kernel, rows),
-        [((rows, width), BF16)],
-        [prefix, phi, intra, window, norm_gain.reshape(1, width)],
+        [((rows, width), BF16, hbm)],
+        [(a, vmem) for a in (prefix, phi, intra, early, window, gain)],
         4 * rows * 384 * width,
     )
     return mixed

time: 76.9 us -> 73.5 us (0.956)
  blocking collectives: 32.3 us -> 11.9 us
  starting transfers between devices: 16.8 us -> 28.2 us
  Pallas kernels: 11.2 us -> 16.9 us
  waiting for transfers between devices: 9.62 us -> 14.9 us
  local copies, waits for them, and re-layouts: 5.83 us -> 0.99 us
    all_to_all x1 -> x0, blocking collectives: 20.3 us -> none  [exchange(): return lax.all_to_all(x, axis, split_axis=0, concat_axis=0, tiled=True)]
    all_to_all x2 -> x3, starting transfers between devices: 13.3 us -> 24.6 us  [exchange(): return lax.all_to_all(x, axis, split_axis=0, concat_axis=0, tiled=True)]
    pallas_call x6 -> x7, Pallas kernels: 11.2 us -> 16.9 us  [call(): pl.pallas_call(kernel, out_shape=[space(shape, dtype) for shape, dtype, s...]
    unnamed x26 -> x16, local copies, waits for them, and re-layouts: 5.16 us -> 0.98 us
    all_to_all x2 -> x3, waiting for transfers between devices: 9.62 us -> 12.8 us  [exchange(): return lax.all_to_all(x, axis, split_axis=0, concat_axis=0, tiled=True)]
    ppermute x1, waiting for transfers between devices: 0.01 us -> 2.09 us  [body(): halo = lax.ppermute(halo, SEQ, [(i, i + 1) for i in range(devices - 1)])]
  transfers between devices with their start and end apart: 3 -> 4, of which waited for: 1 -> 4; matrix products, arithmetic and copies ran while one was open for 0% -> 0% of each run, Pallas kernels for 10% -> 12%
where the time goes in v2:
time: 73.5 us; the launch traced here: 73 us
  starting transfers between devices  28.2 us (38%)
  Pallas kernels  16.9 us (23%)
  waiting for transfers between devices  14.9 us (20%)
  blocking collectives  11.9 us (16%)
  local copies, waits for them, and re-layouts  0.99 us (1%)
    all_to_all x3, starting transfers between devices, exchange(): return lax.all_to_all(x, axis, split_axis=0, concat_axis=0, tiled=True)  24.6 us
    pallas_call x7, Pallas kernels, call(): pl.pallas_call(kernel, out_shape=[space(shape, dtype) for shape, dtype, s...  16.9 us
    all_to_all x3, waiting for transfers between devices, exchange(): return lax.all_to_all(x, axis, split_axis=0, concat_axis=0, tiled=True)  12.8 us
    all_gather x1, blocking collectives, body(): whole = lax.all_gather(hidden_states, 'head', tiled=True)  11.9 us
    ppermute x1, starting transfers between devices, body(): halo = lax.ppermute(halo, SEQ, [(i, i + 1) for i in range(devices - 1)])  3.55 us
    ppermute x1, waiting for transfers between devices, body(): halo = lax.ppermute(halo, SEQ, [(i, i + 1) for i in range(devices - 1)])  2.09 us
  transfers between devices with their start and end apart: 4, of which 4 were waited for; matrix products, arithmetic and copies ran while one was open for 0% of the time, Pallas kernels for 12%

profile of v2, /device:TPU:1, one launch (start us, length us, event | category | flops | bytes accessed | tf_op | source)
XLA Modules:
  0.0 73.0 jit_solution(668433414624355938)
XLA Ops:
  0.0 0.0 copy-start.2
  0.0 11.9 %all_gather.3.x_ref = bf16[1024,384]{1,0:T(8,128)(2,1)S(1)} all-gather(bf16[256,384]{1,0:T(8,128)(2,1)} %param.7), channel_id=1, replica_groups=mesh['seq_0'=8,'seq_1'=8,'seq_2'=2,'head'=4] {'head'}, dimensions={0}, use_global_device_ids=true | all-gather | bytes 983040 | tf_op jit(solution)/shard_map/all_gather | solution.py:258
  11.9 0.0 copy-done.2
  11.9 0.0 copy-start
  11.9 0.0 copy-start.1
  11.9 3.7 %shard_map.73 = (bf16[512,128]{1,0:T(8,128)(2,1)}, bf16[256,384]{1,0:T(8,128)(2,1)}) custom-call(bf16[1024,384]{1,0:T(8,128)(2,1)S(1)} %all_gather.3.x_ref, bf16[96,1536]{1,0:T(8,128)(2,1)S(1)} %bitcast.6, bf16[1536,384]{1,0:T(8,128)(2,1)} %wv_hbm.1), custom_call_target="tpu_custom_call" | custom-call | flops 377487360 | bytes 2260992 | tf_op jit(solution)/shard_map/pallas_call | solution.py:228
  15.6 12.5 %all-to-all-start = ((bf16[16,32,128]{2,1,0:T(8,128)(2,1)}), bf16[16,32,128]{2,1,0:T(8,128)(2,1)}, u32[]{:S(2)}, u32[]{:S(2)}) async-start(bf16[16,32,128]{2,1,0:T(8,128)(2,1)} %bitcast.10), calls=%async_computation | async-start | bytes 262144 | tf_op jit(solution)/shard_map/all_to_all | solution.py:240
  28.1 0.0 copy-done
  28.1 0.0 copy-done.1
  28.1 5.2 %shard_map.74 = (f32[192,384]{1,0:T(8,128)}, bf16[64,1152]{1,0:T(8,128)(2,1)}, bf16[64,768]{1,0:T(8,128)(2,1)}) custom-call(bf16[1024,384]{1,0:T(8,128)(2,1)S(1)} %all_gather.3.x_ref, bf16[1536,384]{1,0:T(8,128)(2,1)S(1)} %copy-done, bf16[1536,384]{1,0:T(8,128)(2,1)S(1)} %copy-done.1, bf16[256,384]{1,0:T(8,128)(2,1)} %get-tuple-element.20.v_ref), custom_call_target="tpu_custom_call" | custom-call | flops 679477248 | bytes 3342336 | tf_op jit(solution)/shard_map/pallas_call | solution.py:228
  33.3 4.1 %all-to-all-done.slices_ref = bf16[16,32,128]{2,1,0:T(8,128)(2,1)} async-done(((bf16[16,32,128]{2,1,0:T(8,128)(2,1)}), bf16[16,32,128]{2,1,0:T(8,128)(2,1)}, u32[]{:S(2)}, u32[]{:S(2)}) %all-to-all-start) | async-done | bytes 131104 | tf_op jit(solution)/shard_map/all_to_all | solution.py:240
  37.4 1.6 %shard_map.75 = f32[8,32,128]{2,1,0:T(8,128)} custom-call(bf16[16,32,128]{2,1,0:T(8,128)(2,1)} %all-to-all-done.slices_ref), custom_call_target="tpu_custom_call" | custom-call | flops 65536 | bytes 131072 | tf_op jit(solution)/shard_map/pallas_call | solution.py:228
  39.0 0.0 copy-start.7
  39.0 0.0 copy-start.5
  39.0 8.3 %all-to-all-start.1 = ((f32[8,32,128]{2,1,0:T(8,128)}), f32[8,32,128]{2,1,0:T(8,128)S(1)}, u32[]{:S(2)}, u32[]{:S(2)}) async-start(f32[8,32,128]{2,1,0:T(8,128)} %shard_map.75), calls=%async_computation.1 | async-start | bytes 262144 | tf_op jit(solution)/shard_map/all_to_all | solution.py:240
  47.3 0.0 copy-start.6
  47.4 0.0 copy-start.3
  47.4 1.0 %copy-done.3 = bf16[1536,96]{0,1:T(8,128)(2,1)S(1)} copy-done((bf16[1536,96]{0,1:T(8,128)(2,1)S(1)}, bf16[1536,96]{0,1:T(8,128)(2,1)}, u32[]{:S(2)}) %copy-start.3) | copy-done | bytes 294936
  48.3 0.0 copy-start.4
  48.3 2.3 %shard_map.76 = (f32[256,384]{1,0:T(8,128)S(1)}, bf16[256,1152]{1,0:T(8,128)(2,1)S(1)}) custom-call(bf16[1024,384]{1,0:T(8,128)(2,1)S(1)} %all_gather.3.x_ref, bf16[96,1536]{1,0:T(8,128)(2,1)S(1)} %bitcast.9, bf16[96,1536]{1,0:T(8,128)(2,1)S(1)} %bitcast.7, bf16[256,384]{1,0:T(8,128)(2,1)} %get-tuple-element.20.v_ref), custom_call_target="tpu_custom_call" | custom-call | flops 352321536 | bytes 1572864 | tf_op jit(solution)/shard_map/pallas_call | solution.py:228
  50.6 6.2 %all-to-all-done.1.totals_ref = f32[8,32,128]{2,1,0:T(8,128)S(1)} async-done(((f32[8,32,128]{2,1,0:T(8,128)}), f32[8,32,128]{2,1,0:T(8,128)S(1)}, u32[]{:S(2)}, u32[]{:S(2)}) %all-to-all-start.1) | async-done | bytes 131104 | tf_op jit(solution)/shard_map/all_to_all | solution.py:240
  56.9 1.6 %shard_map.77 = bf16[16,32,128]{2,1,0:T(8,128)(2,1)} custom-call(s32[1]{0:T(128)} %bitcast.plane_ref, bf16[16,32,128]{2,1,0:T(8,128)(2,1)} %all-to-all-done.slices_ref, f32[8,32,128]{2,1,0:T(8,128)S(1)} %all-to-all-done.1.totals_ref), custom_call_target="tpu_custom_call" | custom-call | flops 655360 | bytes 262148 | tf_op jit(solution)/shard_map/pallas_call | solution.py:228
  58.5 3.8 %all-to-all-start.2 = ((bf16[16,32,128]{2,1,0:T(8,128)(2,1)}), bf16[16,32,128]{2,1,0:T(8,128)(2,1)S(1)}, u32[]{:S(2)}, u32[]{:S(2)}) async-start(bf16[16,32,128]{2,1,0:T(8,128)(2,1)} %shard_map.77), calls=%async_computation.2 | async-start | bytes 262144 | tf_op jit(solution)/shard_map/all_to_all | solution.py:240
  62.3 0.0 copy-done.7
  62.3 3.5 %collective-permute-start = (bf16[64,768]{1,0:T(8,128)(2,1)S(1)}, bf16[64,768]{1,0:T(8,128)(2,1)S(1)}, u32[]{:S(2)}, u32[]{:S(2)}) collective-permute-start(bf16[64,768]{1,0:T(8,128)(2,1)S(1)} %copy-done.7), channel_id=1, source_target_pairs={{0,4},{4,8},{8,12},{12,16},{16,20},{20,24},{24,28},{28,32},{32,36}... | collective-permute-start | bytes 294920 | tf_op jit(solution)/shard_map/ppermute | solution.py:281
  65.8 0.0 copy-done.6
  65.9 2.1 %collective-permute-done.halo_ref = bf16[64,768]{1,0:T(8,128)(2,1)S(1)} collective-permute-done((bf16[64,768]{1,0:T(8,128)(2,1)S(1)}, bf16[64,768]{1,0:T(8,128)(2,1)S(1)}, u32[]{:S(2)}, u32[]{:S(2)}) %collective-permute-start) | collective-permute-done | bytes 98336 | tf_op jit(solution)/shard_map/ppermute | solution.py:281
  67.9 0.0 copy-done.5
  68.0 1.1 %shard_map.78.first_ref = f32[64,384]{1,0:T(8,128)S(1)} custom-call(s32[1]{0:T(128)} %bitcast.5.first_ref, bf16[64,1152]{1,0:T(8,128)(2,1)S(1)} %copy-done.5, bf16[64,768]{1,0:T(8,128)(2,1)S(1)} %collective-permute-done.halo_ref), custom_call_target="tpu_custom_call" | custom-call | flops 6291456 | bytes 245764 | tf_op jit(solution)/shard_map/pallas_call | solution.py:228
  69.0 2.5 %all-to-all-done.2 = bf16[16,32,128]{2,1,0:T(8,128)(2,1)S(1)} async-done(((bf16[16,32,128]{2,1,0:T(8,128)(2,1)}), bf16[16,32,128]{2,1,0:T(8,128)(2,1)S(1)}, u32[]{:S(2)}, u32[]{:S(2)}) %all-to-all-start.2) | async-done | bytes 131104 | tf_op jit(solution)/shard_map/all_to_all | solution.py:240
  71.5 0.0 copy-done.4
  71.5 1.5 %shard_map.79 = bf16[256,384]{1,0:T(8,128)(2,1)} custom-call(bf16[512,128]{1,0:T(8,128)(2,1)S(1)} %bitcast.8, bf16[256,1152]{1,0:T(8,128)(2,1)S(1)} %get-tuple-element.28.phi_ref, f32[256,384]{1,0:T(8,128)S(1)} %get-tuple-element.29.intra_ref, f32[64,384]{1,0:T(8,128)S(1)} %shard_map.78.first_ref, f32[192,384]{1,0:T(8,128)S(1)} %copy-done.4, ...), custom_call_target="tpu_custom_call" | custom-call | flops 150994944 | bytes 1508864 | tf_op jit(solution)/shard_map/pallas_call | solution.py:228
  (1 shorter events, 0.0 us)
Async XLA Ops:
  0.0 11.9 %copy-start.2 = (bf16[1536,96]{0,1:T(8,128)(2,1)S(1)}, bf16[1536,96]{0,1:T(8,128)(2,1)}, u32[]{:S(2)}) copy-start(bf16[1536,96]{0,1:T(8,128)(2,1)} %param.9) | copy-start | bytes 884740
  11.9 16.2 %copy-start = (bf16[1536,384]{1,0:T(8,128)(2,1)S(1)}, bf16[1536,384]{1,0:T(8,128)(2,1)}, u32[]{:S(2)}) copy-start(bf16[1536,384]{1,0:T(8,128)(2,1)} %wq_ref.1) | copy-start | bytes 3538948
  11.9 16.2 %copy-start.1 = (bf16[1536,384]{1,0:T(8,128)(2,1)S(1)}, bf16[1536,384]{1,0:T(8,128)(2,1)}, u32[]{:S(2)}) copy-start(bf16[1536,384]{1,0:T(8,128)(2,1)} %wk_ref.1) | copy-start | bytes 3538948
  15.6 21.8 %all-to-all-start = ((bf16[16,32,128]{2,1,0:T(8,128)(2,1)}), bf16[16,32,128]{2,1,0:T(8,128)(2,1)}, u32[]{:S(2)}, u32[]{:S(2)}) async-start(bf16[16,32,128]{2,1,0:T(8,128)(2,1)} %bitcast.10), calls=%async_computation | async-start | bytes 262144 | tf_op jit(solution)/shard_map/all_to_all | solution.py:240
  39.0 23.2 %copy-start.7 = (bf16[64,768]{1,0:T(8,128)(2,1)S(1)}, bf16[64,768]{1,0:T(8,128)(2,1)}, u32[]{:S(2)}) copy-start(bf16[64,768]{1,0:T(8,128)(2,1)} %get-tuple-element.31) | copy-start | bytes 294916
  39.0 28.9 %copy-start.5 = (bf16[64,1152]{1,0:T(8,128)(2,1)S(1)}, bf16[64,1152]{1,0:T(8,128)(2,1)}, u32[]{:S(2)}) copy-start(bf16[64,1152]{1,0:T(8,128)(2,1)} %get-tuple-element.30.head_ref) | copy-start | bytes 442372
  39.0 17.8 %all-to-all-start.1 = ((f32[8,32,128]{2,1,0:T(8,128)}), f32[8,32,128]{2,1,0:T(8,128)S(1)}, u32[]{:S(2)}, u32[]{:S(2)}) async-start(f32[8,32,128]{2,1,0:T(8,128)} %shard_map.75), calls=%async_computation.1 | async-start | bytes 262144 | tf_op jit(solution)/shard_map/all_to_all | solution.py:240
  47.3 18.5 %copy-start.6 = (f32[384]{0:T(512)S(1)}, f32[384]{0:T(512)}, u32[]{:S(2)}) copy-start(f32[384]{0:T(512)} %param.13) | copy-start | bytes 4612
  47.4 1.0 %copy-start.3 = (bf16[1536,96]{0,1:T(8,128)(2,1)S(1)}, bf16[1536,96]{0,1:T(8,128)(2,1)}, u32[]{:S(2)}) copy-start(bf16[1536,96]{0,1:T(8,128)(2,1)} %param.8) | copy-start | bytes 884740
  48.3 23.2 %copy-start.4 = (f32[192,384]{1,0:T(8,128)S(1)}, f32[192,384]{1,0:T(8,128)}, u32[]{:S(2)}) copy-start(f32[192,384]{1,0:T(8,128)} %get-tuple-element.32.window_ref) | copy-start | bytes 884740
  58.5 13.1 %all-to-all-start.2 = ((bf16[16,32,128]{2,1,0:T(8,128)(2,1)}), bf16[16,32,128]{2,1,0:T(8,128)(2,1)S(1)}, u32[]{:S(2)}, u32[]{:S(2)}) async-start(bf16[16,32,128]{2,1,0:T(8,128)(2,1)} %shard_map.77), calls=%async_computation.2 | async-start | bytes 262144 | tf_op jit(solution)/shard_map/all_to_all | solution.py:240
  62.3 5.7 %collective-permute-start = (bf16[64,768]{1,0:T(8,128)(2,1)S(1)}, bf16[64,768]{1,0:T(8,128)(2,1)S(1)}, u32[]{:S(2)}, u32[]{:S(2)}) collective-permute-start(bf16[64,768]{1,0:T(8,128)(2,1)S(1)} %copy-done.7), channel_id=1, source_target_pairs={{0,4},{4,8},{8,12},{12,16},{16,20},{20,24},{24,28},{28,32},{32,36}... | collective-permute-start | bytes 294920 | tf_op jit(solution)/shard_map/ppermute | solution.py:281

commit v3 on v1

--- a/solution.py
+++ b/solution.py
@@ -18,8 +18,8 @@
 PLANE = ("seq_1", "seq_2")
 F32 = jnp.float32
 BF16 = jnp.bfloat16
+FLOPS_PER_NS = 1_000_000
 NT = (((1,), (1,)), ((), ()))
-VMEM_BYTES = 40 << 20
 
 
 def dot(a, b):
@@ -67,16 +67,19 @@
     return lax.broadcasted_iota(jnp.int32, shape, len(shape) - 1) < HV
 
 
-def state_kernel(rows, chunks, x_ref, wk_ref, wv_ref, state_ref, kt_ref, v_ref):
+def feature_kernel(rows, chunks, x_ref, wk_ref, left_ref):
+    blocks = features(project_transposed(wk_ref, x_ref, rows, chunks), 1.0, 1.0)
+    for p in range(left_ref.shape[0]):
+        for n, block in enumerate(blocks):
+            left_ref[p, 32 * n : 32 * (n + 1), :] = block[32 * p : 32 * p + 32]
+
+
+def state_kernel(rows, chunks, x_ref, wv_ref, left_ref, state_ref, v_ref):
     v = project(x_ref, wv_ref, rows, chunks).astype(BF16)
     v_ref[...] = v
-    kt = project_transposed(wk_ref, x_ref, rows, chunks)
-    kt_ref[...] = kt
-    blocks = features(kt, 1.0, 1.0)
     pairs = v.shape[1] // 128
     for p in range(pairs):
-        left = jnp.concatenate([b[32 * p : 32 * p + 32] for b in blocks], axis=0)
-        both = dot(left, v[:, 128 * p : 128 * p + 128]).reshape(BLOCKS, 2, FK, 128)
+        both = dot(left_ref[p], v[:, 128 * p : 128 * p + 128]).reshape(BLOCKS, 2, FK, 128)
         one = jnp.where(low_half((BLOCKS, FK, 128)), both[:, 0], both[:, 1])
         state_ref[PAIR_ROWS * p : PAIR_ROWS * (p + 1), :] = one.reshape(PAIR_ROWS, 128).astype(BF16)
     used = PAIR_ROWS * pairs
@@ -92,12 +95,44 @@
     halo_ref[:, width:] = v_ref[rows - WIN :, :]
 
 
-def intra_kernel(rows, chunks, x_ref, wq_ref, kt_ref, v_ref, intra_ref, phi_ref):
+def window_kernel(rows, first_ref, q_ref, k_ref, v_ref, halo_ref, out_ref):
+    width = k_ref.shape[1]
+    row = lax.broadcasted_iota(jnp.int32, (2 * WIN, 2 * WIN), 0) % WIN
+    col = lax.broadcasted_iota(jnp.int32, (2 * WIN, 2 * WIN), 1)
+    band = (col <= row + WIN) & (col > row)
+    low = low_half((WIN, 128))
+    tiles = [(t, p) for t in range(rows // WIN) for p in range(width // 128)]
+
+    def seen(ref, t, p, shift):
+        at = slice(128 * p, 128 * p + 128)
+        if t > 0:
+            return ref[WIN * (t - 1) : WIN * (t + 1), at]
+        return jnp.concatenate(
+            [halo_ref[:, shift + 128 * p : shift + 128 * p + 128], ref[:WIN, at]], axis=0
+        )
+
+    logits = []
+    for t, p in tiles:
+        q = q_ref[WIN * t : WIN * (t + 1), 128 * p : 128 * p + 128]
+        none = jnp.zeros_like(q)
+        both = jnp.concatenate([jnp.where(low, q, none), jnp.where(low, none, q)], axis=0)
+        score = lax.dot_general(both, seen(k_ref, t, p, 0), NT, preferred_element_type=F32)
+        valid = band & ((col >= WIN) | (first_ref[0] == 0)) if t == 0 else band
+        logits.append(jnp.where(valid, score * HV ** (-0.5), -1e30))
+    logits = jnp.concatenate(logits, axis=0)
+    expw = jnp.exp(logits - jnp.max(logits, axis=-1, keepdims=True))
+    weights = (expw / jnp.sum(expw, axis=-1, keepdims=True)).astype(BF16)
+    for n, (t, p) in enumerate(tiles):
+        mixed = dot(weights[2 * WIN * n : 2 * WIN * (n + 1)], seen(v_ref, t, p, width))
+        out_ref[WIN * t : WIN * (t + 1), 128 * p : 128 * p + 128] = jnp.where(low, mixed[:WIN], mixed[WIN:])
+
+
+def intra_kernel(rows, chunks, x_ref, wq_ref, wk_ref, v_ref, intra_ref, phi_ref):
     qt = project_transposed(wq_ref, x_ref, rows, chunks)
+    kt = project_transposed(wk_ref, x_ref, rows, chunks)
     blocks = features(qt, 0.5, 1.0 / (FK // 2))
     heads = qt.shape[0] // FK
     pad = jnp.zeros((384 - 2 * PAIR_ROWS, rows), F32)
-    kt = kt_ref[...]
     q_hi = qt.astype(BF16).astype(F32)
     q_lo = qt - q_hi
     k_hi = kt.astype(BF16).astype(F32)
@@ -121,37 +156,6 @@
         intra_ref[:, 128 * p : 128 * p + 128] = jnp.where(low_half((rows, 128)), outs[0], outs[1])
 
 
-def window_kernel(rows, first_ref, q_ref, k_ref, v_ref, halo_ref, out_ref):
-    width = k_ref.shape[1]
-    first = first_ref[0]
-    row = lax.broadcasted_iota(jnp.int32, (2 * WIN, 2 * WIN), 0) % WIN
-    col = lax.broadcasted_iota(jnp.int32, (2 * WIN, 2 * WIN), 1)
-    band = (col <= row + WIN) & (col > row)
-    for t in range(rows // WIN):
-        valid = band & ((col >= WIN) | (first == 0)) if t == 0 else band
-        for p in range(width // 128):
-            at = slice(128 * p, 128 * p + 128)
-            if t == 0:
-                keys = jnp.concatenate([halo_ref[:, at], k_ref[:WIN, at]], axis=0)
-                vals = jnp.concatenate(
-                    [halo_ref[:, width + 128 * p : width + 128 * p + 128], v_ref[:WIN, at]], axis=0
-                )
-            else:
-                keys = k_ref[WIN * (t - 1) : WIN * (t + 1), at]
-                vals = v_ref[WIN * (t - 1) : WIN * (t + 1), at]
-            q = q_ref[WIN * t : WIN * (t + 1), at]
-            low = low_half((WIN, 128))
-            none = jnp.zeros_like(q)
-            both = jnp.concatenate([jnp.where(low, q, none), jnp.where(low, none, q)], axis=0)
-            logits = lax.dot_general(both, keys, NT, preferred_element_type=F32) * HV ** (-0.5)
-            logits = jnp.where(valid, logits, -1e30)
-            top = jnp.max(logits, axis=-1, keepdims=True)
-            expw = jnp.exp(logits - top)
-            weights = (expw / jnp.sum(expw, axis=-1, keepdims=True)).astype(BF16)
-            mixed = dot(weights, vals)
-            out_ref[WIN * t : WIN * (t + 1), at] = jnp.where(low, mixed[:WIN], mixed[WIN:])
-
-
 def prefix_kernel(plane_ref, slices_ref, totals_ref, out_ref):
     plane = plane_ref[0]
     run = jnp.zeros(totals_ref.shape[1:], F32)
@@ -180,23 +184,27 @@
         hi = square.astype(BF16)
         lo = (square - hi.astype(F32)).astype(BF16)
         mean = dot(jnp.concatenate([hi, lo], axis=1), ones)
-        normed = linear * lax.rsqrt(mean + 1e-5) * gain_ref[:, at]
+        normed = linear * lax.rsqrt(mean + 1e-5) * gain_ref[at].reshape(1, 128)
         out_ref[:, at] = (normed + window_ref[:, at]).astype(BF16)
 
 
-def call(kernel, outs, args, flops, scalars=0):
-    outs = [jax.ShapeDtypeStruct(s, d) for s, d in outs]
-    size = sum(a.size * a.dtype.itemsize for a in list(args) + outs)
-    specs = [pl.BlockSpec(memory_space=pltpu.SMEM)] * scalars
-    specs += [pl.BlockSpec(memory_space=pltpu.VMEM)] * (len(args) - scalars)
+def call(kernel, outs, args, nanoseconds, vmem=12):
+    arrays = [a if space is pltpu.SMEM else pltpu.with_memory_space_constraint(a, space) for a, space in args]
+    spaces = [space for _, space in args]
+
+    def spec(space):
+        return pl.BlockSpec(memory_space=pltpu.SMEM if space is pltpu.SMEM else pltpu.VMEM)
+
     return pl.pallas_call(
         kernel,
-        out_shape=outs,
-        in_specs=specs,
-        out_specs=[pl.BlockSpec(memory_space=pltpu.VMEM)] * len(outs),
-        compiler_params=pltpu.CompilerParams(vmem_limit_bytes=VMEM_BYTES),
-        cost_estimate=pl.CostEstimate(flops=flops, bytes_accessed=size, transcendentals=0),
-    )(*args)
+        out_shape=[space(shape, dtype) for shape, dtype, space in outs],
+        in_specs=[spec(space) for space in spaces],
+        out_specs=[spec(space) for _, _, space in outs],
+        compiler_params=pltpu.CompilerParams(vmem_limit_bytes=vmem << 20),
+        cost_estimate=pl.CostEstimate(
+            flops=nanoseconds * FLOPS_PER_NS, bytes_accessed=0, transcendentals=0
+        ),
+    )(*arrays)
 
 
 def exchange(x, axis):
@@ -215,46 +223,60 @@
     piece = FK * members
     held = -(-PAIR_ROWS * width // (128 * piece)) * piece
 
+    pairs = width // 128
+    vmem, hbm, smem = pltpu.VMEM, pltpu.HBM, pltpu.SMEM
+
     whole = lax.all_gather(hidden_states, "head", tiled=True)
-    state, kt, v = call(
+    whole, plane, first = lax.optimization_barrier((whole, plane, first))
+    (left,) = call(
+        functools.partial(feature_kernel, rows, chunks),
+        [((pairs, 2 * PAIR_ROWS, rows), BF16, vmem)],
+        [(whole, vmem), (feature_k.T, vmem)],
+        900,
+    )
+    state, v = call(
         functools.partial(state_kernel, rows, chunks),
-        [((held, 128), BF16), ((few, rows), F32), ((rows, width), BF16)],
-        [whole, feature_k.T, value_w],
-        2 * rows * model * (few + width),
+        [((held, 128), BF16, vmem), ((rows, width), BF16, hbm)],
+        [(whole, vmem), (value_w, vmem), (left, vmem)],
+        1000,
     )
     slices = exchange(state.reshape(members, held // members, 128), PLANE)
+    slices, v = lax.optimization_barrier((slices, v))
+    total = jnp.sum(slices.astype(F32), axis=0)
+    totals = exchange(jnp.broadcast_to(total, (planes, *total.shape)), "seq_0")
     wq, wk, halo = call(
         functools.partial(window_project_kernel, rows, chunks),
-        [((rows, width), BF16), ((rows, width), BF16), ((WIN, 2 * width), BF16)],
-        [whole, window_q, window_k, v],
-        4 * rows * model * width,
+        [((rows, width), BF16, hbm), ((rows, width), BF16, hbm), ((WIN, 2 * width), BF16, hbm)],
+        [(whole, vmem), (window_q, vmem), (window_k, vmem), (v, hbm)],
+        1700,
     )
     devices = lax.axis_size(SEQ)
     halo = lax.ppermute(halo, SEQ, [(i, i + 1) for i in range(devices - 1)])
-    total = jnp.sum(slices.astype(F32), axis=0)
-    totals = exchange(jnp.broadcast_to(total, (planes, *total.shape)), "seq_0")
     intra, phi = call(
         functools.partial(intra_kernel, rows, chunks),
-        [((rows, width), F32), ((rows, 3 * width), BF16)],
-        [whole, feature_q.T, kt, v],
-        2 * rows * model * few + 8 * rows * rows * width,
-    )
+        [((rows, width), F32, vmem), ((rows, 3 * width), BF16, vmem)],
+        [(whole, vmem), (feature_q.T, hbm), (feature_k.T, hbm), (v, hbm)],
+        2200,
+    )
+    totals, wq, wk, halo, intra, phi = lax.optimization_barrier((totals, wq, wk, halo, intra, phi))
     (before,) = call(
-        prefix_kernel, [(slices.shape, BF16)], [plane, slices, totals], 10 * slices.size, 1
+        prefix_kernel,
+        [(slices.shape, BF16, hbm)],
+        [(plane, smem), (slices, vmem), (totals, vmem)],
+        1000,
     )
     prefix = exchange(before, PLANE).reshape(held, 128)
     (window,) = call(
         functools.partial(window_kernel, rows),
-        [((rows, width), F32)],
-        [first, wq, wk, v, halo],
-        16 * rows * WIN * width,
-        1,
+        [((rows, width), F32, vmem)],
+        [(first, smem), (wq, hbm), (wk, hbm), (v, hbm), (halo, vmem)],
+        3000,
     )
     (mixed,) = call(
         functools.partial(final_kernel, rows),
-        [((rows, width), BF16)],
-        [prefix, phi, intra, window, norm_gain.reshape(1, width)],
-        4 * rows * 384 * width,
+        [((rows, width), BF16, hbm)],
+        [(a, vmem) for a in (prefix, phi, intra, window, norm_gain)],
+        1400,
     )
     return mixed
 

time: 76.9 us -> 71.1 us (0.925)
  local copies, waits for them, and re-layouts: 5.83 us -> 2.46 us
  starting transfers between devices: 16.8 us -> 15.3 us
    unnamed x26 -> x10, local copies, waits for them, and re-layouts: 5.16 us -> 1.8 us
    ppermute x1, starting transfers between devices: 3.53 us -> 2 us  [body(): halo = lax.ppermute(halo, SEQ, [(i, i + 1) for i in range(devices - 1)])]
    pallas_call x6 -> x7, Pallas kernels: 11.2 us -> 11.1 us  [call(): pl.pallas_call(kernel, out_shape=[space(shape, dtype) for shape, dtype, s...]
  transfers between devices with their start and end apart: 3 -> 3, of which waited for: 1 -> 2; matrix products, arithmetic and copies ran while one was open for 0% -> 0% of each run, Pallas kernels for 10% -> 10%
where the time goes in v3:
time: 71.1 us; the launch traced here: 70.4 us
  blocking collectives  32 us (45%)
  starting transfers between devices  15.3 us (22%)
  Pallas kernels  11.1 us (16%)
  waiting for transfers between devices  9.55 us (13%)
  local copies, waits for them, and re-layouts  2.46 us (3%)
    all_to_all x1, blocking collectives, exchange(): return lax.all_to_all(x, axis, split_axis=0, concat_axis=0, tiled=True)  20.2 us
    all_to_all x2, starting transfers between devices, exchange(): return lax.all_to_all(x, axis, split_axis=0, concat_axis=0, tiled=True)  13.3 us
    all_gather x1, blocking collectives, body(): whole = lax.all_gather(hidden_states, 'head', tiled=True)  11.8 us
    pallas_call x7, Pallas kernels, call(): pl.pallas_call(kernel, out_shape=[space(shape, dtype) for shape, dtype, s...  11.1 us
    all_to_all x2, waiting for transfers between devices, exchange(): return lax.all_to_all(x, axis, split_axis=0, concat_axis=0, tiled=True)  9.55 us
    ppermute x1, starting transfers between devices, body(): halo = lax.ppermute(halo, SEQ, [(i, i + 1) for i in range(devices - 1)])  2 us
    unnamed x10, local copies, waits for them, and re-layouts  1.8 us
  transfers between devices with their start and end apart: 3, of which 2 were waited for; matrix products, arithmetic and copies ran while one was open for 0% of the time, Pallas kernels for 10%

profile of v3, /device:TPU:1, one launch (start us, length us, event | category | flops | bytes accessed | tf_op | source)
XLA Modules:
  0.0 70.4 jit_solution(9156087379709979078)
XLA Ops:
  0.0 11.8 %all_gather.3.x_ref = bf16[1024,384]{1,0:T(8,128)(2,1)S(1)} all-gather(bf16[256,384]{1,0:T(8,128)(2,1)} %param.7), channel_id=1, replica_groups=mesh['seq_0'=8,'seq_1'=8,'seq_2'=2,'head'=4] {'head'}, dimensions={0}, use_global_device_ids=true | all-gather | bytes 983040 | tf_op jit(solution)/shard_map/all_gather | solution.py:229
  11.8 0.0 copy-start.3
  11.8 1.0 %copy-done.3 = bf16[1536,96]{0,1:T(8,128)(2,1)S(1)} copy-done((bf16[1536,96]{0,1:T(8,128)(2,1)S(1)}, bf16[1536,96]{0,1:T(8,128)(2,1)}, u32[]{:S(2)}) %copy-start.3) | copy-done | bytes 294936
  12.8 0.0 copy-start
  12.8 0.4 shard_map.73.left_ref
  13.2 0.8 %copy-done = bf16[1536,384]{1,0:T(8,128)(2,1)S(1)} copy-done((bf16[1536,384]{1,0:T(8,128)(2,1)S(1)}, bf16[1536,384]{1,0:T(8,128)(2,1)}, u32[]{:S(2)}) %copy-start) | copy-done | bytes 1179672
  14.0 0.0 copy-start.1
  14.0 0.0 copy-start.2
  14.0 1.4 %shard_map.74 = (bf16[512,128]{1,0:T(8,128)(2,1)S(1)}, bf16[256,384]{1,0:T(8,128)(2,1)}) custom-call(bf16[1024,384]{1,0:T(8,128)(2,1)S(1)} %all_gather.3.x_ref, bf16[1536,384]{1,0:T(8,128)(2,1)S(1)} %copy-done, bf16[3,320,256]{2,1,0:T(8,128)(2,1)S(1)} %shard_map.73.left_ref), custom_call_target="tpu_custom_call" | custom-call | flops 1000000000 | tf_op jit(solution)/shard_map/pallas_call | solution.py:198
  15.4 20.2 %all_to_all.15.slices_ref = bf16[16,32,128]{2,1,0:T(8,128)(2,1)S(1)} all-to-all(bf16[16,32,128]{2,1,0:T(8,128)(2,1)S(1)} %bitcast.7), channel_id=1, replica_groups=mesh['seq_0'=8,'seq_1'=8,'seq_2'=2,'head'=4] {'seq_1','seq_2'}, dimensions={0} | all-to-all | bytes 262144 | tf_op jit(solution)/shard_map/all_to_all | solution.py:211
  35.6 0.7 broadcast_in_dim.3
  36.3 9.5 %all-to-all-start.1 = ((f32[8,32,128]{2,1,0:T(8,128)}), f32[8,32,128]{2,1,0:T(8,128)S(1)}, u32[]{:S(2)}, u32[]{:S(2)}) async-start(f32[8,32,128]{2,1,0:T(8,128)} %broadcast_in_dim.3), calls=%async_computation.1 | async-start | bytes 262144 | tf_op jit(solution)/shard_map/all_to_all | solution.py:211
  45.7 0.0 copy-done.1
  45.7 0.0 copy-done.2
  45.8 2.7 %shard_map.75 = (bf16[256,384]{1,0:T(8,128)(2,1)}, bf16[256,384]{1,0:T(8,128)(2,1)}, bf16[64,768]{1,0:T(8,128)(2,1)}) custom-call(bf16[1024,384]{1,0:T(8,128)(2,1)S(1)} %all_gather.3.x_ref, bf16[1536,384]{1,0:T(8,128)(2,1)S(1)} %copy-done.1, bf16[1536,384]{1,0:T(8,128)(2,1)S(1)} %copy-done.2, bf16[256,384]{1,0:T(8,128)(2,1)} %get-tuple-element.28.v_ref), custom_call_target="tpu_custom_call" | custom-call | flops 1700000000 | tf_op jit(solution)/shard_map/pallas_call | solution.py:198
  48.5 2.0 %collective-permute-start = (bf16[64,768]{1,0:T(8,128)(2,1)}, bf16[64,768]{1,0:T(8,128)(2,1)S(1)}, u32[]{:S(2)}, u32[]{:S(2)}) collective-permute-start(bf16[64,768]{1,0:T(8,128)(2,1)} %get-tuple-element.31), channel_id=1, source_target_pairs={{0,4},{4,8},{8,12},{12,16},{16,20},{20,24},{24,28},{28,32},{32,36}... | collective-permute-start | bytes 294920 | tf_op jit(solution)/shard_map/ppermute | solution.py:254
  50.5 2.4 %shard_map.76 = (f32[256,384]{1,0:T(8,128)S(1)}, bf16[256,1152]{1,0:T(8,128)(2,1)S(1)}) custom-call(bf16[1024,384]{1,0:T(8,128)(2,1)S(1)} %all_gather.3.x_ref, bf16[96,1536]{1,0:T(8,128)(2,1)} %bitcast.10, bf16[96,1536]{1,0:T(8,128)(2,1)} %bitcast.8, bf16[256,384]{1,0:T(8,128)(2,1)} %get-tuple-element.28.v_ref), custom_call_target="tpu_custom_call" | custom-call | flops 2200000000 | tf_op jit(solution)/shard_map/pallas_call | solution.py:198
  52.9 0.0 collective-permute-done.halo_ref
  53.0 2.3 %all-to-all-done.1.totals_ref = f32[8,32,128]{2,1,0:T(8,128)S(1)} async-done(((f32[8,32,128]{2,1,0:T(8,128)}), f32[8,32,128]{2,1,0:T(8,128)S(1)}, u32[]{:S(2)}, u32[]{:S(2)}) %all-to-all-start.1) | async-done | bytes 131104 | tf_op jit(solution)/shard_map/all_to_all | solution.py:211
  55.2 0.7 shard_map.77
  55.9 3.8 %all-to-all-start.2 = ((bf16[16,32,128]{2,1,0:T(8,128)(2,1)}), bf16[16,32,128]{2,1,0:T(8,128)(2,1)S(1)}, u32[]{:S(2)}, u32[]{:S(2)}) async-start(bf16[16,32,128]{2,1,0:T(8,128)(2,1)} %shard_map.77), calls=%async_computation.2 | async-start | bytes 262144 | tf_op jit(solution)/shard_map/all_to_all | solution.py:211
  59.7 0.0 copy-start.4
  59.7 1.9 %shard_map.78.window_ref = f32[256,384]{1,0:T(8,128)S(1)} custom-call(s32[1]{0:T(128)} %bitcast.1.first_ref, bf16[256,384]{1,0:T(8,128)(2,1)} %get-tuple-element.38.q_ref, bf16[256,384]{1,0:T(8,128)(2,1)} %get-tuple-element.39.k_ref, bf16[256,384]{1,0:T(8,128)(2,1)} %get-tuple-element.28.v_ref, bf16[64,768]{1,0:T(8,128)(2,1)S(1)} %collective-permute-done.halo_ref), custom_call_target="tpu_custom_call" | custom-call | flops 3000000000 | tf_op jit(solution)/shard_map/pallas_call | solution.py:198
  61.7 7.2 %all-to-all-done.2 = bf16[16,32,128]{2,1,0:T(8,128)(2,1)S(1)} async-done(((bf16[16,32,128]{2,1,0:T(8,128)(2,1)}), bf16[16,32,128]{2,1,0:T(8,128)(2,1)S(1)}, u32[]{:S(2)}, u32[]{:S(2)}) %all-to-all-start.2) | async-done | bytes 131104 | tf_op jit(solution)/shard_map/all_to_all | solution.py:211
  69.0 0.0 copy-done.4
  69.0 1.5 %shard_map.79 = bf16[256,384]{1,0:T(8,128)(2,1)} custom-call(bf16[512,128]{1,0:T(8,128)(2,1)S(1)} %bitcast.6, bf16[256,1152]{1,0:T(8,128)(2,1)S(1)} %get-tuple-element.35.phi_ref, f32[256,384]{1,0:T(8,128)S(1)} %get-tuple-element.36.intra_ref, f32[256,384]{1,0:T(8,128)S(1)} %shard_map.78.window_ref, f32[384]{0:T(512)S(1)} %copy-done.4), custom_call_target="tpu_custom_call" | custom-call | flops 1400000000 | tf_op jit(solution)/shard_map/pallas_call | solution.py:198
  (1 shorter events, 0.0 us)
Async XLA Ops:
  11.8 1.0 %copy-start.3 = (bf16[1536,96]{0,1:T(8,128)(2,1)S(1)}, bf16[1536,96]{0,1:T(8,128)(2,1)}, u32[]{:S(2)}) copy-start(bf16[1536,96]{0,1:T(8,128)(2,1)} %param.9) | copy-start | bytes 884740
  12.8 1.3 %copy-start = (bf16[1536,384]{1,0:T(8,128)(2,1)S(1)}, bf16[1536,384]{1,0:T(8,128)(2,1)}, u32[]{:S(2)}) copy-start(bf16[1536,384]{1,0:T(8,128)(2,1)} %wv_ref.1) | copy-start | bytes 3538948
  14.0 31.7 %copy-start.1 = (bf16[1536,384]{1,0:T(8,128)(2,1)S(1)}, bf16[1536,384]{1,0:T(8,128)(2,1)}, u32[]{:S(2)}) copy-start(bf16[1536,384]{1,0:T(8,128)(2,1)} %wq_ref.1) | copy-start | bytes 3538948
  14.0 31.7 %copy-start.2 = (bf16[1536,384]{1,0:T(8,128)(2,1)S(1)}, bf16[1536,384]{1,0:T(8,128)(2,1)}, u32[]{:S(2)}) copy-start(bf16[1536,384]{1,0:T(8,128)(2,1)} %wk_ref.1) | copy-start | bytes 3538948
  36.3 19.0 %all-to-all-start.1 = ((f32[8,32,128]{2,1,0:T(8,128)}), f32[8,32,128]{2,1,0:T(8,128)S(1)}, u32[]{:S(2)}, u32[]{:S(2)}) async-start(f32[8,32,128]{2,1,0:T(8,128)} %broadcast_in_dim.3), calls=%async_computation.1 | async-start | bytes 262144 | tf_op jit(solution)/shard_map/all_to_all | solution.py:211
  48.5 4.5 %collective-permute-start = (bf16[64,768]{1,0:T(8,128)(2,1)}, bf16[64,768]{1,0:T(8,128)(2,1)S(1)}, u32[]{:S(2)}, u32[]{:S(2)}) collective-permute-start(bf16[64,768]{1,0:T(8,128)(2,1)} %get-tuple-element.31), channel_id=1, source_target_pairs={{0,4},{4,8},{8,12},{12,16},{16,20},{20,24},{24,28},{28,32},{32,36}... | collective-permute-start | bytes 294920 | tf_op jit(solution)/shard_map/ppermute | solution.py:254
  55.9 13.0 %all-to-all-start.2 = ((bf16[16,32,128]{2,1,0:T(8,128)(2,1)}), bf16[16,32,128]{2,1,0:T(8,128)(2,1)S(1)}, u32[]{:S(2)}, u32[]{:S(2)}) async-start(bf16[16,32,128]{2,1,0:T(8,128)(2,1)} %shard_map.77), calls=%async_computation.2 | async-start | bytes 262144 | tf_op jit(solution)/shard_map/all_to_all | solution.py:211
  59.7 9.2 %copy-start.4 = (f32[384]{0:T(512)S(1)}, f32[384]{0:T(512)}, u32[]{:S(2)}) copy-start(f32[384]{0:T(512)} %gain_ref.1) | copy-start | bytes 4612

commit v4 on v3

--- a/solution.py
+++ b/solution.py
@@ -67,32 +67,52 @@
     return lax.broadcasted_iota(jnp.int32, shape, len(shape) - 1) < HV
 
 
-def feature_kernel(rows, chunks, x_ref, wk_ref, left_ref):
+def state_kernel(
+    rows, chunks, x_ref, wk_hbm, wv_hbm, state_ref, v_hbm, wk_ref, wv_ref, v_ref, wk_sem, wv_sem, v_sem
+):
+    load = pltpu.make_async_copy(wk_hbm, wk_ref, wk_sem)
+    load.start()
+    parts = wv_sem.shape[0]
+    piece = wv_ref.shape[0] // parts
+    loads = []
+    for n in range(parts):
+        at = pl.ds(n * piece, piece)
+        loads.append(pltpu.make_async_copy(wv_hbm.at[at], wv_ref.at[at], wv_sem.at[n]))
+        loads[n].start()
+    load.wait()
     blocks = features(project_transposed(wk_ref, x_ref, rows, chunks), 1.0, 1.0)
-    for p in range(left_ref.shape[0]):
-        for n, block in enumerate(blocks):
-            left_ref[p, 32 * n : 32 * (n + 1), :] = block[32 * p : 32 * p + 32]
-
-
-def state_kernel(rows, chunks, x_ref, wv_ref, left_ref, state_ref, v_ref):
-    v = project(x_ref, wv_ref, rows, chunks).astype(BF16)
+    depth = x_ref.shape[1]
+    total = None
+    for c in range(chunks):
+        for n in range(c * parts // chunks, (c + 1) * parts // chunks):
+            loads[n].wait()
+        part = dot(x_ref[c * rows : (c + 1) * rows, :], wv_ref[c * depth : (c + 1) * depth, :])
+        total = part if total is None else total + part
+    v = total.astype(BF16)
     v_ref[...] = v
+    store = pltpu.make_async_copy(v_ref, v_hbm, v_sem)
+    store.start()
     pairs = v.shape[1] // 128
     for p in range(pairs):
-        both = dot(left_ref[p], v[:, 128 * p : 128 * p + 128]).reshape(BLOCKS, 2, FK, 128)
+        left = jnp.concatenate([b[32 * p : 32 * p + 32] for b in blocks], axis=0)
+        both = dot(left, v[:, 128 * p : 128 * p + 128]).reshape(BLOCKS, 2, FK, 128)
         one = jnp.where(low_half((BLOCKS, FK, 128)), both[:, 0], both[:, 1])
         state_ref[PAIR_ROWS * p : PAIR_ROWS * (p + 1), :] = one.reshape(PAIR_ROWS, 128).astype(BF16)
     used = PAIR_ROWS * pairs
     state_ref[used:, :] = jnp.zeros((state_ref.shape[0] - used, 128), BF16)
-
-
-def window_project_kernel(rows, chunks, x_ref, wq_ref, wk_ref, v_ref, oq_ref, ok_ref, halo_ref):
-    oq_ref[...] = project(x_ref, wq_ref, rows, chunks).astype(BF16)
-    keys = project(x_ref, wk_ref, rows, chunks).astype(BF16)
-    ok_ref[...] = keys
+    store.wait()
+
+
+def window_key_kernel(rows, chunks, x_ref, w_ref, v_ref, out_ref, halo_ref):
+    keys = project(x_ref, w_ref, rows, chunks).astype(BF16)
+    out_ref[...] = keys
     width = keys.shape[1]
     halo_ref[:, :width] = keys[rows - WIN :]
     halo_ref[:, width:] = v_ref[rows - WIN :, :]
+
+
+def window_query_kernel(rows, chunks, x_ref, w_ref, out_ref):
+    out_ref[...] = project(x_ref, w_ref, rows, chunks).astype(BF16)
 
 
 def window_kernel(rows, first_ref, q_ref, k_ref, v_ref, halo_ref, out_ref):
@@ -188,21 +208,23 @@
         out_ref[:, at] = (normed + window_ref[:, at]).astype(BF16)
 
 
-def call(kernel, outs, args, nanoseconds, vmem=12):
+def call(kernel, outs, args, nanoseconds, scratch=(), vmem=12):
     arrays = [a if space is pltpu.SMEM else pltpu.with_memory_space_constraint(a, space) for a, space in args]
     spaces = [space for _, space in args]
+    size = sum(a.size * a.dtype.itemsize for a in arrays)
 
     def spec(space):
-        return pl.BlockSpec(memory_space=pltpu.SMEM if space is pltpu.SMEM else pltpu.VMEM)
+        return pl.BlockSpec(memory_space=pltpu.VMEM if space is pltpu.HBM and not scratch else space)
 
     return pl.pallas_call(
         kernel,
         out_shape=[space(shape, dtype) for shape, dtype, space in outs],
         in_specs=[spec(space) for space in spaces],
         out_specs=[spec(space) for _, _, space in outs],
+        scratch_shapes=list(scratch),
         compiler_params=pltpu.CompilerParams(vmem_limit_bytes=vmem << 20),
         cost_estimate=pl.CostEstimate(
-            flops=nanoseconds * FLOPS_PER_NS, bytes_accessed=0, transcendentals=0
+            flops=nanoseconds * FLOPS_PER_NS, bytes_accessed=size, transcendentals=0
         ),
     )(*arrays)
 
@@ -223,49 +245,56 @@
     piece = FK * members
     held = -(-PAIR_ROWS * width // (128 * piece)) * piece
 
-    pairs = width // 128
     vmem, hbm, smem = pltpu.VMEM, pltpu.HBM, pltpu.SMEM
 
     whole = lax.all_gather(hidden_states, "head", tiled=True)
     whole, plane, first = lax.optimization_barrier((whole, plane, first))
-    (left,) = call(
-        functools.partial(feature_kernel, rows, chunks),
-        [((pairs, 2 * PAIR_ROWS, rows), BF16, vmem)],
-        [(whole, vmem), (feature_k.T, vmem)],
-        900,
-    )
     state, v = call(
         functools.partial(state_kernel, rows, chunks),
         [((held, 128), BF16, vmem), ((rows, width), BF16, hbm)],
-        [(whole, vmem), (value_w, vmem), (left, vmem)],
-        1000,
+        [(whole, vmem), (feature_k.T, hbm), (value_w, hbm)],
+        2200,
+        scratch=[
+            pltpu.VMEM((few, model), BF16),
+            pltpu.VMEM((model, width), BF16),
+            pltpu.VMEM((rows, width), BF16),
+            pltpu.SemaphoreType.DMA(()),
+            pltpu.SemaphoreType.DMA((2 * chunks,)),
+            pltpu.SemaphoreType.DMA(()),
+        ],
     )
     slices = exchange(state.reshape(members, held // members, 128), PLANE)
     slices, v = lax.optimization_barrier((slices, v))
     total = jnp.sum(slices.astype(F32), axis=0)
     totals = exchange(jnp.broadcast_to(total, (planes, *total.shape)), "seq_0")
-    wq, wk, halo = call(
-        functools.partial(window_project_kernel, rows, chunks),
-        [((rows, width), BF16, hbm), ((rows, width), BF16, hbm), ((WIN, 2 * width), BF16, hbm)],
-        [(whole, vmem), (window_q, vmem), (window_k, vmem), (v, hbm)],
-        1700,
+    wk, halo = call(
+        functools.partial(window_key_kernel, rows, chunks),
+        [((rows, width), BF16, hbm), ((WIN, 2 * width), BF16, hbm)],
+        [(whole, vmem), (window_k, vmem), (v, hbm)],
+        1500,
     )
     devices = lax.axis_size(SEQ)
     halo = lax.ppermute(halo, SEQ, [(i, i + 1) for i in range(devices - 1)])
+    (wq,) = call(
+        functools.partial(window_query_kernel, rows, chunks),
+        [((rows, width), BF16, hbm)],
+        [(whole, vmem), (window_q, vmem)],
+        1200,
+    )
+    totals, wq, wk, halo, v = lax.optimization_barrier((totals, wq, wk, halo, v))
+    (before,) = call(
+        prefix_kernel,
+        [(slices.shape, BF16, hbm)],
+        [(plane, smem), (slices, vmem), (totals, vmem)],
+        1000,
+    )
+    prefix = exchange(before, PLANE).reshape(held, 128)
     intra, phi = call(
         functools.partial(intra_kernel, rows, chunks),
         [((rows, width), F32, vmem), ((rows, 3 * width), BF16, vmem)],
         [(whole, vmem), (feature_q.T, hbm), (feature_k.T, hbm), (v, hbm)],
         2200,
     )
-    totals, wq, wk, halo, intra, phi = lax.optimization_barrier((totals, wq, wk, halo, intra, phi))
-    (before,) = call(
-        prefix_kernel,
-        [(slices.shape, BF16, hbm)],
-        [(plane, smem), (slices, vmem), (totals, vmem)],
-        1000,
-    )
-    prefix = exchange(before, PLANE).reshape(held, 128)
     (window,) = call(
         functools.partial(window_kernel, rows),
         [((rows, width), F32, vmem)],

time: 71.1 us -> 71.3 us (level)
  Pallas kernels: 11.1 us -> 14.2 us
  local copies, waits for them, and re-layouts: 2.46 us -> 0.68 us
  waiting for transfers between devices: 9.55 us -> 8.62 us
    pallas_call x7, Pallas kernels: 11.1 us -> 14.2 us  [call(): pl.pallas_call(kernel, out_shape=[space(shape, dtype) for shape, dtype, s...]
    unnamed x10 -> x6, local copies, waits for them, and re-layouts: 1.8 us -> 0.02 us
    all_to_all x2, waiting for transfers between devices: 9.55 us -> 8 us  [exchange(): return lax.all_to_all(x, axis, split_axis=0, concat_axis=0, tiled=True)]
  transfers between devices with their start and end apart: 3 -> 3, of which waited for: 2 -> 3; matrix products, arithmetic and copies ran while one was open for 0% -> 0% of each run, Pallas kernels for 10% -> 11%
where the time goes in v4:
time: 71.3 us; the launch traced here: 70.9 us
  blocking collectives  32 us (45%)
  starting transfers between devices  15.3 us (21%)
  Pallas kernels  14.2 us (20%)
  waiting for transfers between devices  8.62 us (12%)
    all_to_all x1, blocking collectives, exchange(): return lax.all_to_all(x, axis, split_axis=0, concat_axis=0, tiled=True)  20.2 us
    pallas_call x7, Pallas kernels, call(): pl.pallas_call(kernel, out_shape=[space(shape, dtype) for shape, dtype, s...  14.2 us
    all_to_all x2, starting transfers between devices, exchange(): return lax.all_to_all(x, axis, split_axis=0, concat_axis=0, tiled=True)  13.3 us
    all_gather x1, blocking collectives, body(): whole = lax.all_gather(hidden_states, 'head', tiled=True)  11.8 us
    all_to_all x2, waiting for transfers between devices, exchange(): return lax.all_to_all(x, axis, split_axis=0, concat_axis=0, tiled=True)  8 us
    ppermute x1, starting transfers between devices, body(): halo = lax.ppermute(halo, SEQ, [(i, i + 1) for i in range(devices - 1)])  2.01 us
  transfers between devices with their start and end apart: 3, of which 3 were waited for; matrix products, arithmetic and copies ran while one was open for 0% of the time, Pallas kernels for 11%

profile of v4, /device:TPU:1, one launch (start us, length us, event | category | flops | bytes accessed | tf_op | source)
XLA Modules:
  0.0 70.9 jit_solution(4631214307225338060)
XLA Ops:
  0.0 11.8 %all_gather.3.x_ref = bf16[1024,384]{1,0:T(8,128)(2,1)S(1)} all-gather(bf16[256,384]{1,0:T(8,128)(2,1)} %param.7), channel_id=1, replica_groups=mesh['seq_0'=8,'seq_1'=8,'seq_2'=2,'head'=4] {'head'}, dimensions={0}, use_global_device_ids=true | all-gather | bytes 983040 | tf_op jit(solution)/shard_map/all_gather | solution.py:250
  11.8 0.0 copy-start
  11.8 4.1 %shard_map.73 = (bf16[512,128]{1,0:T(8,128)(2,1)S(1)}, bf16[256,384]{1,0:T(8,128)(2,1)}) custom-call(bf16[1024,384]{1,0:T(8,128)(2,1)S(1)} %all_gather.3.x_ref, bf16[96,1536]{1,0:T(8,128)(2,1)} %bitcast.8, bf16[1536,384]{1,0:T(8,128)(2,1)} %wv_hbm.1), custom_call_target="tpu_custom_call" | custom-call | flops 2200000000 | bytes 2260992 | tf_op jit(solution)/shard_map/pallas_call | solution.py:219
  15.9 20.2 %all_to_all.15.slices_ref = bf16[16,32,128]{2,1,0:T(8,128)(2,1)S(1)} all-to-all(bf16[16,32,128]{2,1,0:T(8,128)(2,1)S(1)} %bitcast.7), channel_id=1, replica_groups=mesh['seq_0'=8,'seq_1'=8,'seq_2'=2,'head'=4] {'seq_1','seq_2'}, dimensions={0} | all-to-all | bytes 262144 | tf_op jit(solution)/shard_map/all_to_all | solution.py:233
  36.1 0.7 broadcast_in_dim.3
  36.8 9.5 %all-to-all-start.1 = ((f32[8,32,128]{2,1,0:T(8,128)}), f32[8,32,128]{2,1,0:T(8,128)S(1)}, u32[]{:S(2)}, u32[]{:S(2)}) async-start(f32[8,32,128]{2,1,0:T(8,128)} %broadcast_in_dim.3), calls=%async_computation.1 | async-start | bytes 262144 | tf_op jit(solution)/shard_map/all_to_all | solution.py:233
  46.2 0.0 copy-done
  46.2 0.0 copy-start.1
  46.3 2.3 %shard_map.75 = (bf16[256,384]{1,0:T(8,128)(2,1)}, bf16[64,768]{1,0:T(8,128)(2,1)}) custom-call(bf16[1024,384]{1,0:T(8,128)(2,1)S(1)} %all_gather.3.x_ref, bf16[1536,384]{1,0:T(8,128)(2,1)S(1)} %copy-done, bf16[256,384]{1,0:T(8,128)(2,1)} %get-tuple-element.30.v_ref), custom_call_target="tpu_custom_call" | custom-call | flops 1500000000 | bytes 2162688 | tf_op jit(solution)/shard_map/pallas_call | solution.py:219
  48.6 2.0 %collective-permute-start = (bf16[64,768]{1,0:T(8,128)(2,1)}, bf16[64,768]{1,0:T(8,128)(2,1)S(1)}, u32[]{:S(2)}, u32[]{:S(2)}) collective-permute-start(bf16[64,768]{1,0:T(8,128)(2,1)} %get-tuple-element.28), channel_id=1, source_target_pairs={{0,4},{4,8},{8,12},{12,16},{16,20},{20,24},{24,28},{28,32},{32,36}... | collective-permute-start | bytes 294920 | tf_op jit(solution)/shard_map/ppermute | solution.py:277
  50.6 0.0 copy-done.1
  50.6 1.3 %shard_map.74.q_ref = bf16[256,384]{1,0:T(8,128)(2,1)} custom-call(bf16[1024,384]{1,0:T(8,128)(2,1)S(1)} %all_gather.3.x_ref, bf16[1536,384]{1,0:T(8,128)(2,1)S(1)} %copy-done.1), custom_call_target="tpu_custom_call" | custom-call | flops 1200000000 | bytes 1966080 | tf_op jit(solution)/shard_map/pallas_call | solution.py:219
  51.9 0.6 collective-permute-done.halo_ref
  52.6 3.2 %all-to-all-done.1.totals_ref = f32[8,32,128]{2,1,0:T(8,128)S(1)} async-done(((f32[8,32,128]{2,1,0:T(8,128)}), f32[8,32,128]{2,1,0:T(8,128)S(1)}, u32[]{:S(2)}, u32[]{:S(2)}) %all-to-all-start.1) | async-done | bytes 131104 | tf_op jit(solution)/shard_map/all_to_all | solution.py:233
  55.8 0.7 shard_map.76
  56.4 3.8 %all-to-all-start.2 = ((bf16[16,32,128]{2,1,0:T(8,128)(2,1)}), bf16[16,32,128]{2,1,0:T(8,128)(2,1)S(1)}, u32[]{:S(2)}, u32[]{:S(2)}) async-start(bf16[16,32,128]{2,1,0:T(8,128)(2,1)} %shard_map.76), calls=%async_computation.2 | async-start | bytes 262144 | tf_op jit(solution)/shard_map/all_to_all | solution.py:233
  60.2 2.4 %shard_map.77 = (f32[256,384]{1,0:T(8,128)S(1)}, bf16[256,1152]{1,0:T(8,128)(2,1)S(1)}) custom-call(bf16[1024,384]{1,0:T(8,128)(2,1)S(1)} %all_gather.3.x_ref, bf16[96,1536]{1,0:T(8,128)(2,1)} %bitcast.10, bf16[96,1536]{1,0:T(8,128)(2,1)} %bitcast.9, bf16[256,384]{1,0:T(8,128)(2,1)} %get-tuple-element.30.v_ref), custom_call_target="tpu_custom_call" | custom-call | flops 2200000000 | bytes 1572864 | tf_op jit(solution)/shard_map/pallas_call | solution.py:219
  62.7 0.0 copy-start.2
  62.7 2.0 %shard_map.78.window_ref = f32[256,384]{1,0:T(8,128)S(1)} custom-call(s32[1]{0:T(128)} %bitcast.1.first_ref, bf16[256,384]{1,0:T(8,128)(2,1)} %shard_map.74.q_ref, bf16[256,384]{1,0:T(8,128)(2,1)} %get-tuple-element.35.k_ref, bf16[256,384]{1,0:T(8,128)(2,1)} %get-tuple-element.30.v_ref, bf16[64,768]{1,0:T(8,128)(2,1)S(1)} %collective-permute-done.halo_ref), custom_call_target="tpu_custom_call" | custom-call | flops 3000000000 | bytes 688132 | tf_op jit(solution)/shard_map/pallas_call | solution.py:219
  64.7 4.8 %all-to-all-done.2 = bf16[16,32,128]{2,1,0:T(8,128)(2,1)S(1)} async-done(((bf16[16,32,128]{2,1,0:T(8,128)(2,1)}), bf16[16,32,128]{2,1,0:T(8,128)(2,1)S(1)}, u32[]{:S(2)}, u32[]{:S(2)}) %all-to-all-start.2) | async-done | bytes 131104 | tf_op jit(solution)/shard_map/all_to_all | solution.py:233
  69.5 0.0 copy-done.2
  69.5 1.5 %shard_map.79 = bf16[256,384]{1,0:T(8,128)(2,1)} custom-call(bf16[512,128]{1,0:T(8,128)(2,1)S(1)} %bitcast.6, bf16[256,1152]{1,0:T(8,128)(2,1)S(1)} %get-tuple-element.31.phi_ref, f32[256,384]{1,0:T(8,128)S(1)} %get-tuple-element.32.intra_ref, f32[256,384]{1,0:T(8,128)S(1)} %shard_map.78.window_ref, f32[384]{0:T(512)S(1)} %copy-done.2), custom_call_target="tpu_custom_call" | custom-call | flops 1400000000 | bytes 1508864 | tf_op jit(solution)/shard_map/pallas_call | solution.py:219
  (1 shorter events, 0.0 us)
Async XLA Ops:
  11.8 34.4 %copy-start = (bf16[1536,384]{1,0:T(8,128)(2,1)S(1)}, bf16[1536,384]{1,0:T(8,128)(2,1)}, u32[]{:S(2)}) copy-start(bf16[1536,384]{1,0:T(8,128)(2,1)} %w_ref.3) | copy-start | bytes 3538948
  36.8 19.0 %all-to-all-start.1 = ((f32[8,32,128]{2,1,0:T(8,128)}), f32[8,32,128]{2,1,0:T(8,128)S(1)}, u32[]{:S(2)}, u32[]{:S(2)}) async-start(f32[8,32,128]{2,1,0:T(8,128)} %broadcast_in_dim.3), calls=%async_computation.1 | async-start | bytes 262144 | tf_op jit(solution)/shard_map/all_to_all | solution.py:233
  46.2 4.4 %copy-start.1 = (bf16[1536,384]{1,0:T(8,128)(2,1)S(1)}, bf16[1536,384]{1,0:T(8,128)(2,1)}, u32[]{:S(2)}) copy-start(bf16[1536,384]{1,0:T(8,128)(2,1)} %w_ref.2) | copy-start | bytes 3538948
  48.6 3.9 %collective-permute-start = (bf16[64,768]{1,0:T(8,128)(2,1)}, bf16[64,768]{1,0:T(8,128)(2,1)S(1)}, u32[]{:S(2)}, u32[]{:S(2)}) collective-permute-start(bf16[64,768]{1,0:T(8,128)(2,1)} %get-tuple-element.28), channel_id=1, source_target_pairs={{0,4},{4,8},{8,12},{12,16},{16,20},{20,24},{24,28},{28,32},{32,36}... | collective-permute-start | bytes 294920 | tf_op jit(solution)/shard_map/ppermute | solution.py:277
  56.4 13.0 %all-to-all-start.2 = ((bf16[16,32,128]{2,1,0:T(8,128)(2,1)}), bf16[16,32,128]{2,1,0:T(8,128)(2,1)S(1)}, u32[]{:S(2)}, u32[]{:S(2)}) async-start(bf16[16,32,128]{2,1,0:T(8,128)(2,1)} %shard_map.76), calls=%async_computation.2 | async-start | bytes 262144 | tf_op jit(solution)/shard_map/all_to_all | solution.py:233
  62.7 6.8 %copy-start.2 = (f32[384]{0:T(512)S(1)}, f32[384]{0:T(512)}, u32[]{:S(2)}) copy-start(f32[384]{0:T(512)} %gain_ref.1) | copy-start | bytes 4612

commit v5 on v4

--- a/solution.py
+++ b/solution.py
@@ -67,31 +67,18 @@
     return lax.broadcasted_iota(jnp.int32, shape, len(shape) - 1) < HV
 
 
-def state_kernel(
-    rows, chunks, x_ref, wk_hbm, wv_hbm, state_ref, v_hbm, wk_ref, wv_ref, v_ref, wk_sem, wv_sem, v_sem
-):
-    load = pltpu.make_async_copy(wk_hbm, wk_ref, wk_sem)
-    load.start()
-    parts = wv_sem.shape[0]
-    piece = wv_ref.shape[0] // parts
-    loads = []
-    for n in range(parts):
-        at = pl.ds(n * piece, piece)
-        loads.append(pltpu.make_async_copy(wv_hbm.at[at], wv_ref.at[at], wv_sem.at[n]))
-        loads[n].start()
-    load.wait()
-    blocks = features(project_transposed(wk_ref, x_ref, rows, chunks), 1.0, 1.0)
-    depth = x_ref.shape[1]
-    total = None
-    for c in range(chunks):
-        for n in range(c * parts // chunks, (c + 1) * parts // chunks):
-            loads[n].wait()
-        part = dot(x_ref[c * rows : (c + 1) * rows, :], wv_ref[c * depth : (c + 1) * depth, :])
-        total = part if total is None else total + part
-    v = total.astype(BF16)
+def mean_kernel(out_ref):
+    i = lax.broadcasted_iota(jnp.int32, out_ref.shape, 0) % 128
+    j = lax.broadcasted_iota(jnp.int32, out_ref.shape, 1)
+    out_ref[...] = jnp.where((i < HV) == (j < HV), 1.0 / HV, 0.0).astype(BF16)
+
+
+def state_kernel(rows, chunks, x_ref, wk_ref, wv_ref, state_ref, v_hbm, v_ref, v_sem):
+    v = project(x_ref, wv_ref, rows, chunks).astype(BF16)
     v_ref[...] = v
     store = pltpu.make_async_copy(v_ref, v_hbm, v_sem)
     store.start()
+    blocks = features(project_transposed(wk_ref, x_ref, rows, chunks), 1.0, 1.0)
     pairs = v.shape[1] // 128
     for p in range(pairs):
         left = jnp.concatenate([b[32 * p : 32 * p + 32] for b in blocks], axis=0)
@@ -180,17 +167,14 @@
     plane = plane_ref[0]
     run = jnp.zeros(totals_ref.shape[1:], F32)
     for z in range(totals_ref.shape[0]):
-        run = run + jnp.where(z < plane, totals_ref[z], 0.0)
+        run = run + jnp.where(z < plane, totals_ref[z].astype(F32), 0.0)
     for i in range(slices_ref.shape[0]):
         out_ref[i] = run.astype(BF16)
         run = run + slices_ref[i].astype(F32)
 
 
-def final_kernel(rows, state_ref, phi_ref, intra_ref, window_ref, gain_ref, out_ref):
+def final_kernel(rows, state_ref, phi_ref, intra_ref, window_ref, gain_ref, mean_ref, out_ref):
     low_state = low_half((BLOCKS, FK, 128))
-    i = lax.broadcasted_iota(jnp.int32, (256, 128), 0) % 128
-    j = lax.broadcasted_iota(jnp.int32, (256, 128), 1)
-    ones = jnp.where((i < HV) == (j < HV), 1.0 / HV, 0.0).astype(BF16)
     for p in range(intra_ref.shape[1] // 128):
         at = slice(128 * p, 128 * p + 128)
         state = state_ref[PAIR_ROWS * p : PAIR_ROWS * (p + 1), :].reshape(BLOCKS, FK, 128)
@@ -203,7 +187,7 @@
         square = linear * linear
         hi = square.astype(BF16)
         lo = (square - hi.astype(F32)).astype(BF16)
-        mean = dot(jnp.concatenate([hi, lo], axis=1), ones)
+        mean = dot(jnp.concatenate([hi, lo], axis=1), mean_ref[...])
         normed = linear * lax.rsqrt(mean + 1e-5) * gain_ref[at].reshape(1, 128)
         out_ref[:, at] = (normed + window_ref[:, at]).astype(BF16)
 
@@ -247,25 +231,19 @@
 
     vmem, hbm, smem = pltpu.VMEM, pltpu.HBM, pltpu.SMEM
 
+    (mean,) = call(mean_kernel, [((256, 128), BF16, vmem)], [], 1000)
+    hidden_states, mean, plane, first = lax.optimization_barrier((hidden_states, mean, plane, first))
     whole = lax.all_gather(hidden_states, "head", tiled=True)
-    whole, plane, first = lax.optimization_barrier((whole, plane, first))
     state, v = call(
         functools.partial(state_kernel, rows, chunks),
         [((held, 128), BF16, vmem), ((rows, width), BF16, hbm)],
-        [(whole, vmem), (feature_k.T, hbm), (value_w, hbm)],
-        2200,
-        scratch=[
-            pltpu.VMEM((few, model), BF16),
-            pltpu.VMEM((model, width), BF16),
-            pltpu.VMEM((rows, width), BF16),
-            pltpu.SemaphoreType.DMA(()),
-            pltpu.SemaphoreType.DMA((2 * chunks,)),
-            pltpu.SemaphoreType.DMA(()),
-        ],
+        [(whole, vmem), (feature_k.T, vmem), (value_w, vmem)],
+        1500,
+        scratch=[pltpu.VMEM((rows, width), BF16), pltpu.SemaphoreType.DMA(())],
     )
     slices = exchange(state.reshape(members, held // members, 128), PLANE)
     slices, v = lax.optimization_barrier((slices, v))
-    total = jnp.sum(slices.astype(F32), axis=0)
+    total = jnp.sum(slices.astype(F32), axis=0).astype(BF16)
     totals = exchange(jnp.broadcast_to(total, (planes, *total.shape)), "seq_0")
     wk, halo = call(
         functools.partial(window_key_kernel, rows, chunks),
@@ -304,7 +282,7 @@
     (mixed,) = call(
         functools.partial(final_kernel, rows),
         [((rows, width), BF16, hbm)],
-        [(a, vmem) for a in (prefix, phi, intra, window, norm_gain)],
+        [(a, vmem) for a in (prefix, phi, intra, window, norm_gain, mean)],
         1400,
     )
     return mixed

time: 71.3 us -> 69.2 us (0.971)
  Pallas kernels: 14.2 us -> 11.6 us
  waiting for transfers between devices: 8.62 us -> 6.48 us
  starting transfers between devices: 15.3 us -> 16.6 us
  local copies, waits for them, and re-layouts: 0.68 us -> 1.55 us
    pallas_call x7 -> x8, Pallas kernels: 14.2 us -> 11.6 us  [call(): pl.pallas_call(kernel, out_shape=[space(shape, dtype) for shape, dtype, s...]
    all_to_all x2, waiting for transfers between devices: 8 us -> 5.87 us  [exchange(): return lax.all_to_all(x, axis, split_axis=0, concat_axis=0, tiled=True)]
    all_to_all x2, starting transfers between devices: 13.3 us -> 14.6 us  [exchange(): return lax.all_to_all(x, axis, split_axis=0, concat_axis=0, tiled=True)]
    unnamed x6 -> x12, local copies, waits for them, and re-layouts: 0.02 us -> 0.91 us
  transfers between devices with their start and end apart: 3 -> 3, of which waited for: 3 -> 3; matrix products, arithmetic and copies ran while one was open for 0% -> 0% of each run, Pallas kernels for 11% -> 12%
where the time goes in v5:
time: 69.2 us; the launch traced here: 68.2 us
  blocking collectives  31.8 us (46%)
  starting transfers between devices  16.6 us (24%)
  Pallas kernels  11.6 us (17%)
  waiting for transfers between devices  6.48 us (9%)
  local copies, waits for them, and re-layouts  1.55 us (2%)
    all_to_all x1, blocking collectives, exchange(): return lax.all_to_all(x, axis, split_axis=0, concat_axis=0, tiled=True)  20.2 us
    all_to_all x2, starting transfers between devices, exchange(): return lax.all_to_all(x, axis, split_axis=0, concat_axis=0, tiled=True)  14.6 us
    pallas_call x8, Pallas kernels, call(): pl.pallas_call(kernel, out_shape=[space(shape, dtype) for shape, dtype, s...  11.6 us
    all_gather x1, blocking collectives, body(): whole = lax.all_gather(hidden_states, 'head', tiled=True)  11.6 us
    all_to_all x2, waiting for transfers between devices, exchange(): return lax.all_to_all(x, axis, split_axis=0, concat_axis=0, tiled=True)  5.87 us
    ppermute x1, starting transfers between devices, body(): halo = lax.ppermute(halo, SEQ, [(i, i + 1) for i in range(devices - 1)])  2 us
  transfers between devices with their start and end apart: 3, of which 3 were waited for; matrix products, arithmetic and copies ran while one was open for 0% of the time, Pallas kernels for 12%

profile of v5, /device:TPU:1, one launch (start us, length us, event | category | flops | bytes accessed | tf_op | source)
XLA Modules:
  0.0 68.2 jit_solution(9723309112907144883)
XLA Ops:
  0.0 0.0 copy-start.5
  0.0 0.0 copy-start
  0.0 0.0 copy-start.3
  0.0 0.9 %copy-done.5 = bf16[256,384]{1,0:T(8,128)(2,1)S(1)} copy-done((bf16[256,384]{1,0:T(8,128)(2,1)S(1)}, bf16[256,384]{1,0:T(8,128)(2,1)}, u32[]{:S(2)}) %copy-start.5) | copy-done | bytes 196632
  0.9 11.6 %all_gather.3.x_ref = bf16[1024,384]{1,0:T(8,128)(2,1)S(1)} all-gather(bf16[256,384]{1,0:T(8,128)(2,1)S(1)} %copy-done.5), channel_id=1, replica_groups=mesh['seq_0'=8,'seq_1'=8,'seq_2'=2,'head'=4] {'head'}, dimensions={0}, use_global_device_ids=true | all-gather | bytes 983040 | tf_op jit(solution)/shard_map/all_gather | solution.py:236
  12.5 0.0 copy-done
  12.5 0.0 copy-done.3
  12.5 0.0 copy-start.1
  12.5 1.4 %shard_map.74 = (bf16[512,128]{1,0:T(8,128)(2,1)S(1)}, bf16[256,384]{1,0:T(8,128)(2,1)}) custom-call(bf16[1024,384]{1,0:T(8,128)(2,1)S(1)} %all_gather.3.x_ref, bf16[96,1536]{1,0:T(8,128)(2,1)S(1)} %bitcast.9, bf16[1536,384]{1,0:T(8,128)(2,1)S(1)} %copy-done), custom_call_target="tpu_custom_call" | custom-call | flops 1500000000 | bytes 2260992 | tf_op jit(solution)/shard_map/pallas_call | solution.py:203
  13.9 20.2 %all_to_all.15.slices_ref = bf16[16,32,128]{2,1,0:T(8,128)(2,1)S(1)} all-to-all(bf16[16,32,128]{2,1,0:T(8,128)(2,1)S(1)} %bitcast.7), channel_id=1, replica_groups=mesh['seq_0'=8,'seq_1'=8,'seq_2'=2,'head'=4] {'seq_1','seq_2'}, dimensions={0} | all-to-all | bytes 262144 | tf_op jit(solution)/shard_map/all_to_all | solution.py:217
  34.2 0.6 broadcast_in_dim.3
  34.8 9.5 %all-to-all-start.1 = ((bf16[8,32,128]{2,1,0:T(8,128)(2,1)}), bf16[8,32,128]{2,1,0:T(8,128)(2,1)S(1)}, u32[]{:S(2)}, u32[]{:S(2)}) async-start(bf16[8,32,128]{2,1,0:T(8,128)(2,1)} %broadcast_in_dim.3), calls=%async_computation.1 | async-start | bytes 131072 | tf_op jit(solution)/shard_map/all_to_all | solution.py:217
  44.3 0.0 copy-done.1
  44.3 0.0 copy-start.2
  44.3 2.4 %shard_map.76 = (bf16[256,384]{1,0:T(8,128)(2,1)}, bf16[64,768]{1,0:T(8,128)(2,1)}) custom-call(bf16[1024,384]{1,0:T(8,128)(2,1)S(1)} %all_gather.3.x_ref, bf16[1536,384]{1,0:T(8,128)(2,1)S(1)} %copy-done.1, bf16[256,384]{1,0:T(8,128)(2,1)} %get-tuple-element.31.v_ref), custom_call_target="tpu_custom_call" | custom-call | flops 1500000000 | bytes 2162688 | tf_op jit(solution)/shard_map/pallas_call | solution.py:203
  46.6 2.0 %collective-permute-start = (bf16[64,768]{1,0:T(8,128)(2,1)}, bf16[64,768]{1,0:T(8,128)(2,1)S(1)}, u32[]{:S(2)}, u32[]{:S(2)}) collective-permute-start(bf16[64,768]{1,0:T(8,128)(2,1)} %get-tuple-element.29), channel_id=1, source_target_pairs={{0,4},{4,8},{8,12},{12,16},{16,20},{20,24},{24,28},{28,32},{32,36}... | collective-permute-start | bytes 294920 | tf_op jit(solution)/shard_map/ppermute | solution.py:255
  48.7 0.0 copy-done.2
  48.7 1.3 %shard_map.75.q_ref = bf16[256,384]{1,0:T(8,128)(2,1)} custom-call(bf16[1024,384]{1,0:T(8,128)(2,1)S(1)} %all_gather.3.x_ref, bf16[1536,384]{1,0:T(8,128)(2,1)S(1)} %copy-done.2), custom_call_target="tpu_custom_call" | custom-call | flops 1200000000 | bytes 1966080 | tf_op jit(solution)/shard_map/pallas_call | solution.py:203
  50.0 0.6 collective-permute-done.halo_ref
  50.6 1.1 %all-to-all-done.1.totals_ref = bf16[8,32,128]{2,1,0:T(8,128)(2,1)S(1)} async-done(((bf16[8,32,128]{2,1,0:T(8,128)(2,1)}), bf16[8,32,128]{2,1,0:T(8,128)(2,1)S(1)}, u32[]{:S(2)}, u32[]{:S(2)}) %all-to-all-start.1) | async-done | bytes 65568 | tf_op jit(solution)/shard_map/all_to_all | solution.py:217
  51.7 0.7 shard_map.77
  52.4 5.2 %all-to-all-start.2 = ((bf16[16,32,128]{2,1,0:T(8,128)(2,1)}), bf16[16,32,128]{2,1,0:T(8,128)(2,1)S(1)}, u32[]{:S(2)}, u32[]{:S(2)}) async-start(bf16[16,32,128]{2,1,0:T(8,128)(2,1)} %shard_map.77), calls=%async_computation.2 | async-start | bytes 262144 | tf_op jit(solution)/shard_map/all_to_all | solution.py:217
  57.6 2.4 %shard_map.78 = (f32[256,384]{1,0:T(8,128)S(1)}, bf16[256,1152]{1,0:T(8,128)(2,1)S(1)}) custom-call(bf16[1024,384]{1,0:T(8,128)(2,1)S(1)} %all_gather.3.x_ref, bf16[96,1536]{1,0:T(8,128)(2,1)} %bitcast.10, bf16[96,1536]{1,0:T(8,128)(2,1)} %bitcast.8, bf16[256,384]{1,0:T(8,128)(2,1)} %get-tuple-element.31.v_ref), custom_call_target="tpu_custom_call" | custom-call | flops 2200000000 | bytes 1572864 | tf_op jit(solution)/shard_map/pallas_call | solution.py:203
  60.0 0.0 copy-start.4
  60.0 1.9 %shard_map.79.window_ref = f32[256,384]{1,0:T(8,128)S(1)} custom-call(s32[1]{0:T(128)} %bitcast.1.first_ref, bf16[256,384]{1,0:T(8,128)(2,1)} %shard_map.75.q_ref, bf16[256,384]{1,0:T(8,128)(2,1)} %get-tuple-element.36.k_ref, bf16[256,384]{1,0:T(8,128)(2,1)} %get-tuple-element.31.v_ref, bf16[64,768]{1,0:T(8,128)(2,1)S(1)} %collective-permute-done.halo_ref), custom_call_target="tpu_custom_call" | custom-call | flops 3000000000 | bytes 688132 | tf_op jit(solution)/shard_map/pallas_call | solution.py:203
  62.0 4.8 %all-to-all-done.2 = bf16[16,32,128]{2,1,0:T(8,128)(2,1)S(1)} async-done(((bf16[16,32,128]{2,1,0:T(8,128)(2,1)}), bf16[16,32,128]{2,1,0:T(8,128)(2,1)S(1)}, u32[]{:S(2)}, u32[]{:S(2)}) %all-to-all-start.2) | async-done | bytes 131104 | tf_op jit(solution)/shard_map/all_to_all | solution.py:217
  66.7 0.0 copy-done.4
  66.7 1.5 %shard_map.80 = bf16[256,384]{1,0:T(8,128)(2,1)} custom-call(bf16[512,128]{1,0:T(8,128)(2,1)S(1)} %bitcast.6, bf16[256,1152]{1,0:T(8,128)(2,1)S(1)} %get-tuple-element.32.phi_ref, f32[256,384]{1,0:T(8,128)S(1)} %get-tuple-element.33.intra_ref, f32[256,384]{1,0:T(8,128)S(1)} %shard_map.79.window_ref, f32[384]{0:T(512)S(1)} %copy-done.4, ...), custom_call_target="tpu_custom_call" | custom-call | flops 1400000000 | bytes 1574400 | tf_op jit(solution)/shard_map/pallas_call | solution.py:203
  (2 shorter events, 0.0 us)
Async XLA Ops:
  0.0 0.9 %copy-start.5 = (bf16[256,384]{1,0:T(8,128)(2,1)S(1)}, bf16[256,384]{1,0:T(8,128)(2,1)}, u32[]{:S(2)}) copy-start(bf16[256,384]{1,0:T(8,128)(2,1)} %param.7) | copy-start | bytes 589828
  0.0 12.5 %copy-start = (bf16[1536,384]{1,0:T(8,128)(2,1)S(1)}, bf16[1536,384]{1,0:T(8,128)(2,1)}, u32[]{:S(2)}) copy-start(bf16[1536,384]{1,0:T(8,128)(2,1)} %wv_ref.1) | copy-start | bytes 3538948
  0.0 12.5 %copy-start.3 = (bf16[1536,96]{0,1:T(8,128)(2,1)S(1)}, bf16[1536,96]{0,1:T(8,128)(2,1)}, u32[]{:S(2)}) copy-start(bf16[1536,96]{0,1:T(8,128)(2,1)} %param.9) | copy-start | bytes 884740
  12.5 31.8 %copy-start.1 = (bf16[1536,384]{1,0:T(8,128)(2,1)S(1)}, bf16[1536,384]{1,0:T(8,128)(2,1)}, u32[]{:S(2)}) copy-start(bf16[1536,384]{1,0:T(8,128)(2,1)} %w_ref.3) | copy-start | bytes 3538948
  34.8 16.9 %all-to-all-start.1 = ((bf16[8,32,128]{2,1,0:T(8,128)(2,1)}), bf16[8,32,128]{2,1,0:T(8,128)(2,1)S(1)}, u32[]{:S(2)}, u32[]{:S(2)}) async-start(bf16[8,32,128]{2,1,0:T(8,128)(2,1)} %broadcast_in_dim.3), calls=%async_computation.1 | async-start | bytes 131072 | tf_op jit(solution)/shard_map/all_to_all | solution.py:217
  44.3 4.4 %copy-start.2 = (bf16[1536,384]{1,0:T(8,128)(2,1)S(1)}, bf16[1536,384]{1,0:T(8,128)(2,1)}, u32[]{:S(2)}) copy-start(bf16[1536,384]{1,0:T(8,128)(2,1)} %w_ref.2) | copy-start | bytes 3538948
  46.6 3.9 %collective-permute-start = (bf16[64,768]{1,0:T(8,128)(2,1)}, bf16[64,768]{1,0:T(8,128)(2,1)S(1)}, u32[]{:S(2)}, u32[]{:S(2)}) collective-permute-start(bf16[64,768]{1,0:T(8,128)(2,1)} %get-tuple-element.29), channel_id=1, source_target_pairs={{0,4},{4,8},{8,12},{12,16},{16,20},{20,24},{24,28},{28,32},{32,36}... | collective-permute-start | bytes 294920 | tf_op jit(solution)/shard_map/ppermute | solution.py:255
  52.4 14.3 %all-to-all-start.2 = ((bf16[16,32,128]{2,1,0:T(8,128)(2,1)}), bf16[16,32,128]{2,1,0:T(8,128)(2,1)S(1)}, u32[]{:S(2)}, u32[]{:S(2)}) async-start(bf16[16,32,128]{2,1,0:T(8,128)(2,1)} %shard_map.77), calls=%async_computation.2 | async-start | bytes 262144 | tf_op jit(solution)/shard_map/all_to_all | solution.py:217
  60.0 6.7 %copy-start.4 = (f32[384]{0:T(512)S(1)}, f32[384]{0:T(512)}, u32[]{:S(2)}) copy-start(f32[384]{0:T(512)} %gain_ref.1) | copy-start | bytes 4612

commit v6 on v5

--- a/solution.py
+++ b/solution.py
@@ -90,48 +90,61 @@
     store.wait()
 
 
-def window_key_kernel(rows, chunks, x_ref, w_ref, v_ref, out_ref, halo_ref):
-    keys = project(x_ref, w_ref, rows, chunks).astype(BF16)
-    out_ref[...] = keys
-    width = keys.shape[1]
-    halo_ref[:, :width] = keys[rows - WIN :]
-    halo_ref[:, width:] = v_ref[rows - WIN :, :]
-
-
-def window_query_kernel(rows, chunks, x_ref, w_ref, out_ref):
-    out_ref[...] = project(x_ref, w_ref, rows, chunks).astype(BF16)
-
-
-def window_kernel(rows, first_ref, q_ref, k_ref, v_ref, halo_ref, out_ref):
-    width = k_ref.shape[1]
-    row = lax.broadcasted_iota(jnp.int32, (2 * WIN, 2 * WIN), 0) % WIN
-    col = lax.broadcasted_iota(jnp.int32, (2 * WIN, 2 * WIN), 1)
-    band = (col <= row + WIN) & (col > row)
+def window_tiles(tiles, valid):
     low = low_half((WIN, 128))
-    tiles = [(t, p) for t in range(rows // WIN) for p in range(width // 128)]
-
-    def seen(ref, t, p, shift):
-        at = slice(128 * p, 128 * p + 128)
-        if t > 0:
-            return ref[WIN * (t - 1) : WIN * (t + 1), at]
-        return jnp.concatenate(
-            [halo_ref[:, shift + 128 * p : shift + 128 * p + 128], ref[:WIN, at]], axis=0
-        )
-
     logits = []
-    for t, p in tiles:
-        q = q_ref[WIN * t : WIN * (t + 1), 128 * p : 128 * p + 128]
+    for q, keys, _ in tiles:
         none = jnp.zeros_like(q)
         both = jnp.concatenate([jnp.where(low, q, none), jnp.where(low, none, q)], axis=0)
-        score = lax.dot_general(both, seen(k_ref, t, p, 0), NT, preferred_element_type=F32)
-        valid = band & ((col >= WIN) | (first_ref[0] == 0)) if t == 0 else band
+        score = lax.dot_general(both, keys, NT, preferred_element_type=F32)
         logits.append(jnp.where(valid, score * HV ** (-0.5), -1e30))
     logits = jnp.concatenate(logits, axis=0)
     expw = jnp.exp(logits - jnp.max(logits, axis=-1, keepdims=True))
     weights = (expw / jnp.sum(expw, axis=-1, keepdims=True)).astype(BF16)
-    for n, (t, p) in enumerate(tiles):
-        mixed = dot(weights[2 * WIN * n : 2 * WIN * (n + 1)], seen(v_ref, t, p, width))
-        out_ref[WIN * t : WIN * (t + 1), 128 * p : 128 * p + 128] = jnp.where(low, mixed[:WIN], mixed[WIN:])
+    outs = []
+    for n, (_, _, vals) in enumerate(tiles):
+        mixed = dot(weights[2 * WIN * n : 2 * WIN * (n + 1)], vals)
+        outs.append(jnp.where(low, mixed[:WIN], mixed[WIN:]))
+    return outs
+
+
+def window_band():
+    row = lax.broadcasted_iota(jnp.int32, (2 * WIN, 2 * WIN), 0) % WIN
+    col = lax.broadcasted_iota(jnp.int32, (2 * WIN, 2 * WIN), 1)
+    return (col <= row + WIN) & (col > row), col
+
+
+def window_kernel(rows, chunks, x_ref, wq_ref, wk_ref, v_ref, out_ref, head_ref, halo_ref):
+    keys = project(x_ref, wk_ref, rows, chunks).astype(BF16)
+    queries = project(x_ref, wq_ref, rows, chunks).astype(BF16)
+    width = keys.shape[1]
+    halo_ref[:, :width] = keys[rows - WIN :]
+    halo_ref[:, width:] = v_ref[rows - WIN :, :]
+    head_ref[:, :width] = queries[:WIN]
+    head_ref[:, width : 2 * width] = keys[:WIN]
+    head_ref[:, 2 * width :] = v_ref[:WIN, :]
+    band, _ = window_band()
+    places = [(t, p) for t in range(1, rows // WIN) for p in range(width // 128)]
+    tiles = []
+    for t, p in places:
+        at, seen = slice(128 * p, 128 * p + 128), slice(WIN * (t - 1), WIN * (t + 1))
+        tiles.append((queries[WIN * t : WIN * (t + 1), at], keys[seen, at], v_ref[seen, at]))
+    for (t, p), out in zip(places, window_tiles(tiles, band)):
+        out_ref[WIN * (t - 1) : WIN * t, 128 * p : 128 * p + 128] = out
+
+
+def first_window_kernel(first_ref, head_ref, halo_ref, out_ref):
+    width = out_ref.shape[1]
+    band, col = window_band()
+    valid = band & ((col >= WIN) | (first_ref[0] == 0))
+    tiles = []
+    for p in range(width // 128):
+        at, at2, at3 = (slice(n * width + 128 * p, n * width + 128 * p + 128) for n in range(3))
+        keys = jnp.concatenate([halo_ref[:, at], head_ref[:, at2]], axis=0)
+        vals = jnp.concatenate([halo_ref[:, at2], head_ref[:, at3]], axis=0)
+        tiles.append((head_ref[:, at], keys, vals))
+    for p, out in enumerate(window_tiles(tiles, valid)):
+        out_ref[:, 128 * p : 128 * p + 128] = out
 
 
 def intra_kernel(rows, chunks, x_ref, wq_ref, wk_ref, v_ref, intra_ref, phi_ref):
@@ -173,7 +186,10 @@
         run = run + slices_ref[i].astype(F32)
 
 
-def final_kernel(rows, state_ref, phi_ref, intra_ref, window_ref, gain_ref, mean_ref, out_ref):
+def final_kernel(
+    rows, state_ref, phi_ref, intra_ref, early_ref, window_ref, gain_ref, mean_ref, out_hbm, out_ref, sem
+):
+    stores = []
     low_state = low_half((BLOCKS, FK, 128))
     for p in range(intra_ref.shape[1] // 128):
         at = slice(128 * p, 128 * p + 128)
@@ -189,7 +205,12 @@
         lo = (square - hi.astype(F32)).astype(BF16)
         mean = dot(jnp.concatenate([hi, lo], axis=1), mean_ref[...])
         normed = linear * lax.rsqrt(mean + 1e-5) * gain_ref[at].reshape(1, 128)
-        out_ref[:, at] = (normed + window_ref[:, at]).astype(BF16)
+        out_ref[p, :WIN, :] = (normed[:WIN] + early_ref[:, at]).astype(BF16)
+        out_ref[p, WIN:, :] = (normed[WIN:] + window_ref[:, at]).astype(BF16)
+        stores.append(pltpu.make_async_copy(out_ref.at[p], out_hbm.at[:, at], sem.at[p]))
+        stores[p].start()
+    for store in stores:
+        store.wait()
 
 
 def call(kernel, outs, args, nanoseconds, scratch=(), vmem=12):
@@ -231,7 +252,7 @@
 
     vmem, hbm, smem = pltpu.VMEM, pltpu.HBM, pltpu.SMEM
 
-    (mean,) = call(mean_kernel, [((256, 128), BF16, vmem)], [], 1000)
+    (mean,) = call(mean_kernel, [((256, 128), BF16, vmem)], [], 200)
     hidden_states, mean, plane, first = lax.optimization_barrier((hidden_states, mean, plane, first))
     whole = lax.all_gather(hidden_states, "head", tiled=True)
     state, v = call(
@@ -245,21 +266,21 @@
     slices, v = lax.optimization_barrier((slices, v))
     total = jnp.sum(slices.astype(F32), axis=0).astype(BF16)
     totals = exchange(jnp.broadcast_to(total, (planes, *total.shape)), "seq_0")
-    wk, halo = call(
-        functools.partial(window_key_kernel, rows, chunks),
-        [((rows, width), BF16, hbm), ((WIN, 2 * width), BF16, hbm)],
-        [(whole, vmem), (window_k, vmem), (v, hbm)],
-        1500,
-    )
-    devices = lax.axis_size(SEQ)
-    halo = lax.ppermute(halo, SEQ, [(i, i + 1) for i in range(devices - 1)])
-    (wq,) = call(
-        functools.partial(window_query_kernel, rows, chunks),
-        [((rows, width), BF16, hbm)],
-        [(whole, vmem), (window_q, vmem)],
-        1200,
-    )
-    totals, wq, wk, halo, v = lax.optimization_barrier((totals, wq, wk, halo, v))
+    window, head, halo = call(
+        functools.partial(window_kernel, rows, chunks),
+        [((rows - WIN, width), F32, hbm), ((WIN, 3 * width), BF16, hbm), ((WIN, 2 * width), BF16, hbm)],
+        [(whole, vmem), (window_q, vmem), (window_k, vmem), (v, hbm)],
+        3500,
+    )
+    intra, phi = call(
+        functools.partial(intra_kernel, rows, chunks),
+        [((rows, width), F32, vmem), ((rows, 3 * width), BF16, vmem)],
+        [(whole, vmem), (feature_q.T, hbm), (feature_k.T, hbm), (v, hbm)],
+        2200,
+    )
+    totals, window, head, halo, intra, phi = lax.optimization_barrier(
+        (totals, window, head, halo, intra, phi)
+    )
     (before,) = call(
         prefix_kernel,
         [(slices.shape, BF16, hbm)],
@@ -267,23 +288,20 @@
         1000,
     )
     prefix = exchange(before, PLANE).reshape(held, 128)
-    intra, phi = call(
-        functools.partial(intra_kernel, rows, chunks),
-        [((rows, width), F32, vmem), ((rows, 3 * width), BF16, vmem)],
-        [(whole, vmem), (feature_q.T, hbm), (feature_k.T, hbm), (v, hbm)],
-        2200,
-    )
-    (window,) = call(
-        functools.partial(window_kernel, rows),
-        [((rows, width), F32, vmem)],
-        [(first, smem), (wq, hbm), (wk, hbm), (v, hbm), (halo, vmem)],
-        3000,
+    devices = lax.axis_size(SEQ)
+    halo = lax.ppermute(halo, SEQ, [(i, i + 1) for i in range(devices - 1)])
+    (early,) = call(
+        first_window_kernel,
+        [((WIN, width), F32, vmem)],
+        [(first, smem), (head, vmem), (halo, vmem)],
+        1000,
     )
     (mixed,) = call(
         functools.partial(final_kernel, rows),
         [((rows, width), BF16, hbm)],
-        [(a, vmem) for a in (prefix, phi, intra, window, norm_gain, mean)],
+        [(a, vmem) for a in (prefix, phi, intra, early, window, norm_gain, mean)],
         1400,
+        scratch=[pltpu.VMEM((width // 128, rows, 128), BF16), pltpu.SemaphoreType.DMA((width // 128,))],
     )
     return mixed
 

time: 69.2 us -> 67.4 us (0.974)
  Pallas kernels: 11.6 us -> 9.9 us
  waiting for transfers between devices: 6.48 us -> 5.3 us
  starting transfers between devices: 16.6 us -> 17.6 us
    all_to_all x2, waiting for transfers between devices: 5.87 us -> 3.25 us  [exchange(): return lax.all_to_all(x, axis, split_axis=0, concat_axis=0, tiled=True)]
    pallas_call x8 -> x7, Pallas kernels: 11.6 us -> 9.9 us  [call(): pl.pallas_call(kernel, out_shape=[space(shape, dtype) for shape, dtype, s...]
    ppermute x1, starting transfers between devices: 2 us -> 3.68 us  [body(): halo = lax.ppermute(halo, SEQ, [(i, i + 1) for i in range(devices - 1)])]
    ppermute x1, waiting for transfers between devices: 0.61 us -> 2.05 us  [body(): halo = lax.ppermute(halo, SEQ, [(i, i + 1) for i in range(devices - 1)])]
  transfers between devices with their start and end apart: 3 -> 3, of which waited for: 3 -> 3; matrix products, arithmetic and copies ran while one was open for 0% -> 0% of each run, Pallas kernels for 12% -> 9%
where the time goes in v6:
time: 67.4 us; the launch traced here: 67 us
  blocking collectives  32.2 us (48%)
  starting transfers between devices  17.6 us (26%)
  Pallas kernels  9.9 us (15%)
  waiting for transfers between devices  5.3 us (8%)
  local copies, waits for them, and re-layouts  1.92 us (3%)
    all_to_all x1, blocking collectives, exchange(): return lax.all_to_all(x, axis, split_axis=0, concat_axis=0, tiled=True)  20.2 us
    all_to_all x2, starting transfers between devices, exchange(): return lax.all_to_all(x, axis, split_axis=0, concat_axis=0, tiled=True)  14 us
    all_gather x1, blocking collectives, body(): whole = lax.all_gather(hidden_states, 'head', tiled=True)  11.9 us
    pallas_call x7, Pallas kernels, call(): pl.pallas_call(kernel, out_shape=[space(shape, dtype) for shape, dtype, s...  9.9 us
    ppermute x1, starting transfers between devices, body(): halo = lax.ppermute(halo, SEQ, [(i, i + 1) for i in range(devices - 1)])  3.68 us
    all_to_all x2, waiting for transfers between devices, exchange(): return lax.all_to_all(x, axis, split_axis=0, concat_axis=0, tiled=True)  3.25 us
    ppermute x1, waiting for transfers between devices, body(): halo = lax.ppermute(halo, SEQ, [(i, i + 1) for i in range(devices - 1)])  2.05 us
  transfers between devices with their start and end apart: 3, of which 3 were waited for; matrix products, arithmetic and copies ran while one was open for 0% of the time, Pallas kernels for 9%

profile of v6, /device:TPU:1, one launch (start us, length us, event | category | flops | bytes accessed | tf_op | source)
XLA Modules:
  0.0 67.0 jit_solution(18057650959868419199)
XLA Ops:
  0.0 0.0 copy-start.3
  0.0 0.0 copy-start
  0.0 11.9 %all_gather.3.x_ref = bf16[1024,384]{1,0:T(8,128)(2,1)S(1)} all-gather(bf16[256,384]{1,0:T(8,128)(2,1)} %param.7), channel_id=1, replica_groups=mesh['seq_0'=8,'seq_1'=8,'seq_2'=2,'head'=4] {'head'}, dimensions={0}, use_global_device_ids=true | all-gather | bytes 983040 | tf_op jit(solution)/shard_map/all_gather | solution.py:257
  12.0 0.0 copy-done.3
  12.0 0.0 copy-done
  12.0 0.0 copy-start.1
  12.0 1.4 %shard_map.74 = (bf16[512,128]{1,0:T(8,128)(2,1)S(1)}, bf16[256,384]{1,0:T(8,128)(2,1)}) custom-call(bf16[1024,384]{1,0:T(8,128)(2,1)S(1)} %all_gather.3.x_ref, bf16[96,1536]{1,0:T(8,128)(2,1)S(1)} %bitcast.9, bf16[1536,384]{1,0:T(8,128)(2,1)S(1)} %copy-done), custom_call_target="tpu_custom_call" | custom-call | flops 1500000000 | bytes 2260992 | tf_op jit(solution)/shard_map/pallas_call | solution.py:224
  13.4 20.2 %all_to_all.15.slices_ref = bf16[16,32,128]{2,1,0:T(8,128)(2,1)S(1)} all-to-all(bf16[16,32,128]{2,1,0:T(8,128)(2,1)S(1)} %bitcast.7), channel_id=1, replica_groups=mesh['seq_0'=8,'seq_1'=8,'seq_2'=2,'head'=4] {'seq_1','seq_2'}, dimensions={0} | all-to-all | bytes 262144 | tf_op jit(solution)/shard_map/all_to_all | solution.py:238
  33.6 0.6 broadcast_in_dim.3
  34.3 9.5 %all-to-all-start.1 = ((bf16[8,32,128]{2,1,0:T(8,128)(2,1)}), bf16[8,32,128]{2,1,0:T(8,128)(2,1)S(1)}, u32[]{:S(2)}, u32[]{:S(2)}) async-start(bf16[8,32,128]{2,1,0:T(8,128)(2,1)} %broadcast_in_dim.3), calls=%async_computation.1 | async-start | bytes 131072 | tf_op jit(solution)/shard_map/all_to_all | solution.py:238
  43.7 0.0 copy-done.1
  43.7 0.0 copy-start.2
  43.7 1.3 %copy-done.2 = bf16[1536,384]{1,0:T(8,128)(2,1)S(1)} copy-done((bf16[1536,384]{1,0:T(8,128)(2,1)S(1)}, bf16[1536,384]{1,0:T(8,128)(2,1)}, u32[]{:S(2)}) %copy-start.2) | copy-done | bytes 1179672
  45.0 3.4 %shard_map.75 = (f32[192,384]{1,0:T(8,128)}, bf16[64,1152]{1,0:T(8,128)(2,1)}, bf16[64,768]{1,0:T(8,128)(2,1)}) custom-call(bf16[1024,384]{1,0:T(8,128)(2,1)S(1)} %all_gather.3.x_ref, bf16[1536,384]{1,0:T(8,128)(2,1)S(1)} %copy-done.1, bf16[1536,384]{1,0:T(8,128)(2,1)S(1)} %copy-done.2, bf16[256,384]{1,0:T(8,128)(2,1)} %get-tuple-element.29.v_ref), custom_call_target="tpu_custom_call" | custom-call | flops 3500000000 | bytes 3342336 | tf_op jit(solution)/shard_map/pallas_call | solution.py:224
  48.4 2.4 %shard_map.76 = (f32[256,384]{1,0:T(8,128)S(1)}, bf16[256,1152]{1,0:T(8,128)(2,1)S(1)}) custom-call(bf16[1024,384]{1,0:T(8,128)(2,1)S(1)} %all_gather.3.x_ref, bf16[96,1536]{1,0:T(8,128)(2,1)} %bitcast.10, bf16[96,1536]{1,0:T(8,128)(2,1)} %bitcast.8, bf16[256,384]{1,0:T(8,128)(2,1)} %get-tuple-element.29.v_ref), custom_call_target="tpu_custom_call" | custom-call | flops 2200000000 | bytes 1572864 | tf_op jit(solution)/shard_map/pallas_call | solution.py:224
  50.9 0.3 all-to-all-done.1.totals_ref
  51.2 0.0 copy-start.7
  51.2 0.0 copy-start.6
  51.2 0.7 %shard_map.77 = bf16[16,32,128]{2,1,0:T(8,128)(2,1)} custom-call(s32[1]{0:T(128)} %bitcast.plane_ref, bf16[16,32,128]{2,1,0:T(8,128)(2,1)S(1)} %all_to_all.15.slices_ref, bf16[8,32,128]{2,1,0:T(8,128)(2,1)S(1)} %all-to-all-done.1.totals_ref), custom_call_target="tpu_custom_call" | custom-call | flops 1000000000 | bytes 196612 | tf_op jit(solution)/shard_map/pallas_call | solution.py:224
  51.9 4.5 %all-to-all-start.2 = ((bf16[16,32,128]{2,1,0:T(8,128)(2,1)}), bf16[16,32,128]{2,1,0:T(8,128)(2,1)S(1)}, u32[]{:S(2)}, u32[]{:S(2)}) async-start(bf16[16,32,128]{2,1,0:T(8,128)(2,1)} %shard_map.77), calls=%async_computation.2 | async-start | bytes 262144 | tf_op jit(solution)/shard_map/all_to_all | solution.py:238
  56.3 0.0 copy-done.7
  56.3 0.0 copy-start.4
  56.4 0.0 copy-start.5
  56.4 3.7 %collective-permute-start = (bf16[64,768]{1,0:T(8,128)(2,1)S(1)}, bf16[64,768]{1,0:T(8,128)(2,1)S(1)}, u32[]{:S(2)}, u32[]{:S(2)}) collective-permute-start(bf16[64,768]{1,0:T(8,128)(2,1)S(1)} %copy-done.7), channel_id=1, source_target_pairs={{0,4},{4,8},{8,12},{12,16},{16,20},{20,24},{24,28},{28,32},{32,36}... | collective-permute-start | bytes 294920 | tf_op jit(solution)/shard_map/ppermute | solution.py:292
  60.1 2.1 %collective-permute-done.halo_ref = bf16[64,768]{1,0:T(8,128)(2,1)S(1)} collective-permute-done((bf16[64,768]{1,0:T(8,128)(2,1)S(1)}, bf16[64,768]{1,0:T(8,128)(2,1)S(1)}, u32[]{:S(2)}, u32[]{:S(2)}) %collective-permute-start) | collective-permute-done | bytes 98336 | tf_op jit(solution)/shard_map/ppermute | solution.py:292
  62.1 0.0 copy-done.6
  62.1 0.5 shard_map.78.early_ref
  62.6 3.0 %all-to-all-done.2 = bf16[16,32,128]{2,1,0:T(8,128)(2,1)S(1)} async-done(((bf16[16,32,128]{2,1,0:T(8,128)(2,1)}), bf16[16,32,128]{2,1,0:T(8,128)(2,1)S(1)}, u32[]{:S(2)}, u32[]{:S(2)}) %all-to-all-start.2) | async-done | bytes 131104 | tf_op jit(solution)/shard_map/all_to_all | solution.py:238
  65.6 0.0 copy-done.4
  65.6 0.0 copy-done.5
  65.6 1.4 %shard_map.79 = bf16[256,384]{1,0:T(8,128)(2,1)} custom-call(bf16[512,128]{1,0:T(8,128)(2,1)S(1)} %bitcast.6, bf16[256,1152]{1,0:T(8,128)(2,1)S(1)} %get-tuple-element.36.phi_ref, f32[256,384]{1,0:T(8,128)S(1)} %get-tuple-element.37.intra_ref, f32[64,384]{1,0:T(8,128)S(1)} %shard_map.78.early_ref, f32[192,384]{1,0:T(8,128)S(1)} %copy-done.5, ...), custom_call_target="tpu_custom_call" | custom-call | flops 1400000000 | bytes 1574400 | tf_op jit(solution)/shard_map/pallas_call | solution.py:224
  (2 shorter events, 0.0 us)
Async XLA Ops:
  0.0 12.0 %copy-start.3 = (bf16[1536,96]{0,1:T(8,128)(2,1)S(1)}, bf16[1536,96]{0,1:T(8,128)(2,1)}, u32[]{:S(2)}) copy-start(bf16[1536,96]{0,1:T(8,128)(2,1)} %param.9) | copy-start | bytes 884740
  0.0 12.0 %copy-start = (bf16[1536,384]{1,0:T(8,128)(2,1)S(1)}, bf16[1536,384]{1,0:T(8,128)(2,1)}, u32[]{:S(2)}) copy-start(bf16[1536,384]{1,0:T(8,128)(2,1)} %wv_ref.1) | copy-start | bytes 3538948
  12.0 31.7 %copy-start.1 = (bf16[1536,384]{1,0:T(8,128)(2,1)S(1)}, bf16[1536,384]{1,0:T(8,128)(2,1)}, u32[]{:S(2)}) copy-start(bf16[1536,384]{1,0:T(8,128)(2,1)} %wq_ref.1) | copy-start | bytes 3538948
  34.3 16.9 %all-to-all-start.1 = ((bf16[8,32,128]{2,1,0:T(8,128)(2,1)}), bf16[8,32,128]{2,1,0:T(8,128)(2,1)S(1)}, u32[]{:S(2)}, u32[]{:S(2)}) async-start(bf16[8,32,128]{2,1,0:T(8,128)(2,1)} %broadcast_in_dim.3), calls=%async_computation.1 | async-start | bytes 131072 | tf_op jit(solution)/shard_map/all_to_all | solution.py:238
  43.7 1.3 %copy-start.2 = (bf16[1536,384]{1,0:T(8,128)(2,1)S(1)}, bf16[1536,384]{1,0:T(8,128)(2,1)}, u32[]{:S(2)}) copy-start(bf16[1536,384]{1,0:T(8,128)(2,1)} %wk_ref.1) | copy-start | bytes 3538948
  51.2 5.2 %copy-start.7 = (bf16[64,768]{1,0:T(8,128)(2,1)S(1)}, bf16[64,768]{1,0:T(8,128)(2,1)}, u32[]{:S(2)}) copy-start(bf16[64,768]{1,0:T(8,128)(2,1)} %get-tuple-element.40) | copy-start | bytes 294916
  51.2 11.0 %copy-start.6 = (bf16[64,1152]{1,0:T(8,128)(2,1)S(1)}, bf16[64,1152]{1,0:T(8,128)(2,1)}, u32[]{:S(2)}) copy-start(bf16[64,1152]{1,0:T(8,128)(2,1)} %get-tuple-element.39.head_ref) | copy-start | bytes 442372
  51.9 13.7 %all-to-all-start.2 = ((bf16[16,32,128]{2,1,0:T(8,128)(2,1)}), bf16[16,32,128]{2,1,0:T(8,128)(2,1)S(1)}, u32[]{:S(2)}, u32[]{:S(2)}) async-start(bf16[16,32,128]{2,1,0:T(8,128)(2,1)} %shard_map.77), calls=%async_computation.2 | async-start | bytes 262144 | tf_op jit(solution)/shard_map/all_to_all | solution.py:238
  56.3 9.2 %copy-start.4 = (f32[384]{0:T(512)S(1)}, f32[384]{0:T(512)}, u32[]{:S(2)}) copy-start(f32[384]{0:T(512)} %gain_ref.1) | copy-start | bytes 4612
  56.4 9.2 %copy-start.5 = (f32[192,384]{1,0:T(8,128)S(1)}, f32[192,384]{1,0:T(8,128)}, u32[]{:S(2)}) copy-start(f32[192,384]{1,0:T(8,128)} %get-tuple-element.41.window_ref) | copy-start | bytes 884740
  56.4 5.7 %collective-permute-start = (bf16[64,768]{1,0:T(8,128)(2,1)S(1)}, bf16[64,768]{1,0:T(8,128)(2,1)S(1)}, u32[]{:S(2)}, u32[]{:S(2)}) collective-permute-start(bf16[64,768]{1,0:T(8,128)(2,1)S(1)} %copy-done.7), channel_id=1, source_target_pairs={{0,4},{4,8},{8,12},{12,16},{16,20},{20,24},{24,28},{28,32},{32,36}... | collective-permute-start | bytes 294920 | tf_op jit(solution)/shard_map/ppermute | solution.py:292

commit v7 on v6

--- a/solution.py
+++ b/solution.py
@@ -176,35 +176,58 @@
         intra_ref[:, 128 * p : 128 * p + 128] = jnp.where(low_half((rows, 128)), outs[0], outs[1])
 
 
-def prefix_kernel(plane_ref, slices_ref, totals_ref, out_ref):
+def total_kernel(slices_ref, out_hbm, total_ref, sem):
+    total = slices_ref[0].astype(F32)
+    for i in range(1, slices_ref.shape[0]):
+        total = total + slices_ref[i].astype(F32)
+    total_ref[...] = total.astype(BF16)
+    stores = [pltpu.make_async_copy(total_ref, out_hbm.at[z], sem.at[z]) for z in range(out_hbm.shape[0])]
+    for store in stores:
+        store.start()
+    for store in stores:
+        store.wait()
+
+
+def prefix_kernel(plane_ref, slices_ref, totals_ref, out_hbm, out_ref, sem):
     plane = plane_ref[0]
     run = jnp.zeros(totals_ref.shape[1:], F32)
     for z in range(totals_ref.shape[0]):
         run = run + jnp.where(z < plane, totals_ref[z].astype(F32), 0.0)
-    for i in range(slices_ref.shape[0]):
-        out_ref[i] = run.astype(BF16)
-        run = run + slices_ref[i].astype(F32)
+    stores = []
+    each = slices_ref.shape[0] // sem.shape[0]
+    for n in range(sem.shape[0]):
+        for i in range(each * n, each * (n + 1)):
+            out_ref[i] = run.astype(BF16)
+            run = run + slices_ref[i].astype(F32)
+        at = pl.ds(each * n, each)
+        stores.append(pltpu.make_async_copy(out_ref.at[at], out_hbm.at[at], sem.at[n]))
+        stores[n].start()
+    for store in stores:
+        store.wait()
 
 
 def final_kernel(
     rows, state_ref, phi_ref, intra_ref, early_ref, window_ref, gain_ref, mean_ref, out_hbm, out_ref, sem
 ):
-    stores = []
     low_state = low_half((BLOCKS, FK, 128))
-    for p in range(intra_ref.shape[1] // 128):
-        at = slice(128 * p, 128 * p + 128)
+    pairs = [slice(128 * p, 128 * p + 128) for p in range(intra_ref.shape[1] // 128)]
+    linears, squares = [], []
+    for p, at in enumerate(pairs):
         state = state_ref[PAIR_ROWS * p : PAIR_ROWS * (p + 1), :].reshape(BLOCKS, FK, 128)
         none = jnp.zeros_like(state)
         even = jnp.where(low_state, state, none)[:, None]
         odd = jnp.where(low_state, none, state)[:, None]
         right = jnp.concatenate([even, odd], axis=1).reshape(2 * PAIR_ROWS, 128)
         right = jnp.concatenate([right, jnp.zeros((384 - 2 * PAIR_ROWS, 128), BF16)], axis=0)
-        linear = intra_ref[:, at] + dot(phi_ref[:, 384 * p : 384 * (p + 1)], right)
+        linears.append(intra_ref[:, at] + dot(phi_ref[:, 384 * p : 384 * (p + 1)], right))
+    for linear in linears:
         square = linear * linear
         hi = square.astype(BF16)
         lo = (square - hi.astype(F32)).astype(BF16)
-        mean = dot(jnp.concatenate([hi, lo], axis=1), mean_ref[...])
-        normed = linear * lax.rsqrt(mean + 1e-5) * gain_ref[at].reshape(1, 128)
+        squares.append(dot(jnp.concatenate([hi, lo], axis=1), mean_ref[...]))
+    stores = []
+    for p, at in enumerate(pairs):
+        normed = linears[p] * lax.rsqrt(squares[p] + 1e-5) * gain_ref[at].reshape(1, 128)
         out_ref[p, :WIN, :] = (normed[:WIN] + early_ref[:, at]).astype(BF16)
         out_ref[p, WIN:, :] = (normed[WIN:] + window_ref[:, at]).astype(BF16)
         stores.append(pltpu.make_async_copy(out_ref.at[p], out_hbm.at[:, at], sem.at[p]))
@@ -264,8 +287,15 @@
     )
     slices = exchange(state.reshape(members, held // members, 128), PLANE)
     slices, v = lax.optimization_barrier((slices, v))
-    total = jnp.sum(slices.astype(F32), axis=0).astype(BF16)
-    totals = exchange(jnp.broadcast_to(total, (planes, *total.shape)), "seq_0")
+    piece_shape = slices.shape[1:]
+    (totals,) = call(
+        total_kernel,
+        [((planes, *piece_shape), BF16, hbm)],
+        [(slices, vmem)],
+        600,
+        scratch=[pltpu.VMEM(piece_shape, BF16), pltpu.SemaphoreType.DMA((planes,))],
+    )
+    totals = exchange(totals, "seq_0")
     window, head, halo = call(
         functools.partial(window_kernel, rows, chunks),
         [((rows - WIN, width), F32, hbm), ((WIN, 3 * width), BF16, hbm), ((WIN, 2 * width), BF16, hbm)],
@@ -286,6 +316,7 @@
         [(slices.shape, BF16, hbm)],
         [(plane, smem), (slices, vmem), (totals, vmem)],
         1000,
+        scratch=[pltpu.VMEM(slices.shape, BF16), pltpu.SemaphoreType.DMA((4,))],
     )
     prefix = exchange(before, PLANE).reshape(held, 128)
     devices = lax.axis_size(SEQ)

time: 67.4 us -> 67.3 us (level)
  local copies, waits for them, and re-layouts: 1.92 us -> 0.04 us
  waiting for transfers between devices: 5.3 us -> 6.58 us
    all_to_all x2, waiting for transfers between devices: 3.25 us -> 4.53 us  [exchange(): return lax.all_to_all(x, axis, split_axis=0, concat_axis=0, tiled=True)]
    unnamed x16, local copies, waits for them, and re-layouts: 1.29 us -> 0.04 us
    pallas_call x7 -> x8, Pallas kernels: 9.9 us -> 10.3 us  [call(): pl.pallas_call(kernel, out_shape=[space(shape, dtype) for shape, dtype, s...]
where the time goes in v7:
time: 67.3 us; the launch traced here: 67 us
  blocking collectives  32.3 us (48%)
  starting transfers between devices  17.7 us (26%)
  Pallas kernels  10.3 us (15%)
  waiting for transfers between devices  6.58 us (10%)
    all_to_all x1, blocking collectives, exchange(): return lax.all_to_all(x, axis, split_axis=0, concat_axis=0, tiled=True)  20.3 us
    all_to_all x2, starting transfers between devices, exchange(): return lax.all_to_all(x, axis, split_axis=0, concat_axis=0, tiled=True)  14 us
    all_gather x1, blocking collectives, body(): whole = lax.all_gather(hidden_states, 'head', tiled=True)  11.9 us
    pallas_call x8, Pallas kernels, call(): pl.pallas_call(kernel, out_shape=[space(shape, dtype) for shape, dtype, s...  10.3 us
    all_to_all x2, waiting for transfers between devices, exchange(): return lax.all_to_all(x, axis, split_axis=0, concat_axis=0, tiled=True)  4.53 us
    ppermute x1, starting transfers between devices, body(): halo = lax.ppermute(halo, SEQ, [(i, i + 1) for i in range(devices - 1)])  3.68 us
    ppermute x1, waiting for transfers between devices, body(): halo = lax.ppermute(halo, SEQ, [(i, i + 1) for i in range(devices - 1)])  2.05 us
  transfers between devices with their start and end apart: 3, of which 3 were waited for; matrix products, arithmetic and copies ran while one was open for 0% of the time, Pallas kernels for 9%

profile of v7, /device:TPU:1, one launch (start us, length us, event | category | flops | bytes accessed | tf_op | source)
XLA Modules:
  0.0 67.0 jit_solution(11084759300397802203)
XLA Ops:
  0.0 0.0 copy-start.3
  0.0 0.0 copy-start
  0.0 11.9 %all_gather.3.x_ref = bf16[1024,384]{1,0:T(8,128)(2,1)S(1)} all-gather(bf16[256,384]{1,0:T(8,128)(2,1)} %param.7), channel_id=1, replica_groups=mesh['seq_0'=8,'seq_1'=8,'seq_2'=2,'head'=4] {'head'}, dimensions={0}, use_global_device_ids=true | all-gather | bytes 983040 | tf_op jit(solution)/shard_map/all_gather | solution.py:280
  12.0 0.0 copy-done.3
  12.0 0.0 copy-done
  12.0 1.4 %shard_map.74 = (bf16[512,128]{1,0:T(8,128)(2,1)S(1)}, bf16[256,384]{1,0:T(8,128)(2,1)}) custom-call(bf16[1024,384]{1,0:T(8,128)(2,1)S(1)} %all_gather.3.x_ref, bf16[96,1536]{1,0:T(8,128)(2,1)S(1)} %bitcast.9, bf16[1536,384]{1,0:T(8,128)(2,1)S(1)} %copy-done), custom_call_target="tpu_custom_call" | custom-call | flops 1500000000 | bytes 2260992 | tf_op jit(solution)/shard_map/pallas_call | solution.py:247
  13.4 0.0 copy-start.2
  13.4 20.3 %all_to_all.15.slices_ref = bf16[16,32,128]{2,1,0:T(8,128)(2,1)S(1)} all-to-all(bf16[16,32,128]{2,1,0:T(8,128)(2,1)S(1)} %bitcast.7), channel_id=1, replica_groups=mesh['seq_0'=8,'seq_1'=8,'seq_2'=2,'head'=4] {'seq_1','seq_2'}, dimensions={0} | all-to-all | bytes 262144 | tf_op jit(solution)/shard_map/all_to_all | solution.py:261
  33.7 0.0 copy-start.1
  33.7 0.7 %shard_map.75 = bf16[8,32,128]{2,1,0:T(8,128)(2,1)} custom-call(bf16[16,32,128]{2,1,0:T(8,128)(2,1)S(1)} %all_to_all.15.slices_ref), custom_call_target="tpu_custom_call" | custom-call | flops 600000000 | bytes 131072 | tf_op jit(solution)/shard_map/pallas_call | solution.py:247
  34.5 9.5 %all-to-all-start.1 = ((bf16[8,32,128]{2,1,0:T(8,128)(2,1)}), bf16[8,32,128]{2,1,0:T(8,128)(2,1)S(1)}, u32[]{:S(2)}, u32[]{:S(2)}) async-start(bf16[8,32,128]{2,1,0:T(8,128)(2,1)} %shard_map.75), calls=%async_computation.1 | async-start | bytes 131072 | tf_op jit(solution)/shard_map/all_to_all | solution.py:261
  43.9 0.0 copy-done.2
  44.0 0.0 copy-done.1
  44.0 3.4 %shard_map.76 = (f32[192,384]{1,0:T(8,128)}, bf16[64,1152]{1,0:T(8,128)(2,1)}, bf16[64,768]{1,0:T(8,128)(2,1)}) custom-call(bf16[1024,384]{1,0:T(8,128)(2,1)S(1)} %all_gather.3.x_ref, bf16[1536,384]{1,0:T(8,128)(2,1)S(1)} %copy-done.1, bf16[1536,384]{1,0:T(8,128)(2,1)S(1)} %copy-done.2, bf16[256,384]{1,0:T(8,128)(2,1)} %get-tuple-element.29.v_ref), custom_call_target="tpu_custom_call" | custom-call | flops 3500000000 | bytes 3342336 | tf_op jit(solution)/shard_map/pallas_call | solution.py:247
  47.4 2.4 %shard_map.77 = (f32[256,384]{1,0:T(8,128)S(1)}, bf16[256,1152]{1,0:T(8,128)(2,1)S(1)}) custom-call(bf16[1024,384]{1,0:T(8,128)(2,1)S(1)} %all_gather.3.x_ref, bf16[96,1536]{1,0:T(8,128)(2,1)} %bitcast.10, bf16[96,1536]{1,0:T(8,128)(2,1)} %bitcast.8, bf16[256,384]{1,0:T(8,128)(2,1)} %get-tuple-element.29.v_ref), custom_call_target="tpu_custom_call" | custom-call | flops 2200000000 | bytes 1572864 | tf_op jit(solution)/shard_map/pallas_call | solution.py:247
  49.8 1.6 %all-to-all-done.1.totals_ref = bf16[8,32,128]{2,1,0:T(8,128)(2,1)S(1)} async-done(((bf16[8,32,128]{2,1,0:T(8,128)(2,1)}), bf16[8,32,128]{2,1,0:T(8,128)(2,1)S(1)}, u32[]{:S(2)}, u32[]{:S(2)}) %all-to-all-start.1) | async-done | bytes 65568 | tf_op jit(solution)/shard_map/all_to_all | solution.py:261
  51.4 0.0 copy-start.7
  51.4 0.0 copy-start.6
  51.4 0.7 %shard_map.78 = bf16[16,32,128]{2,1,0:T(8,128)(2,1)} custom-call(s32[1]{0:T(128)} %bitcast.plane_ref, bf16[16,32,128]{2,1,0:T(8,128)(2,1)S(1)} %all_to_all.15.slices_ref, bf16[8,32,128]{2,1,0:T(8,128)(2,1)S(1)} %all-to-all-done.1.totals_ref), custom_call_target="tpu_custom_call" | custom-call | flops 1000000000 | bytes 196612 | tf_op jit(solution)/shard_map/pallas_call | solution.py:247
  52.1 4.5 %all-to-all-start.2 = ((bf16[16,32,128]{2,1,0:T(8,128)(2,1)}), bf16[16,32,128]{2,1,0:T(8,128)(2,1)S(1)}, u32[]{:S(2)}, u32[]{:S(2)}) async-start(bf16[16,32,128]{2,1,0:T(8,128)(2,1)} %shard_map.78), calls=%async_computation.2 | async-start | bytes 262144 | tf_op jit(solution)/shard_map/all_to_all | solution.py:261
  56.6 0.0 copy-done.7
  56.6 0.0 copy-start.4
  56.6 0.0 copy-start.5
  56.6 3.7 %collective-permute-start = (bf16[64,768]{1,0:T(8,128)(2,1)S(1)}, bf16[64,768]{1,0:T(8,128)(2,1)S(1)}, u32[]{:S(2)}, u32[]{:S(2)}) collective-permute-start(bf16[64,768]{1,0:T(8,128)(2,1)S(1)} %copy-done.7), channel_id=1, source_target_pairs={{0,4},{4,8},{8,12},{12,16},{16,20},{20,24},{24,28},{28,32},{32,36}... | collective-permute-start | bytes 294920 | tf_op jit(solution)/shard_map/ppermute | solution.py:323
  60.3 2.1 %collective-permute-done.halo_ref = bf16[64,768]{1,0:T(8,128)(2,1)S(1)} collective-permute-done((bf16[64,768]{1,0:T(8,128)(2,1)S(1)}, bf16[64,768]{1,0:T(8,128)(2,1)S(1)}, u32[]{:S(2)}, u32[]{:S(2)}) %collective-permute-start) | collective-permute-done | bytes 98336 | tf_op jit(solution)/shard_map/ppermute | solution.py:323
  62.4 0.0 copy-done.6
  62.4 0.5 shard_map.79.early_ref
  62.9 3.0 %all-to-all-done.2 = bf16[16,32,128]{2,1,0:T(8,128)(2,1)S(1)} async-done(((bf16[16,32,128]{2,1,0:T(8,128)(2,1)}), bf16[16,32,128]{2,1,0:T(8,128)(2,1)S(1)}, u32[]{:S(2)}, u32[]{:S(2)}) %all-to-all-start.2) | async-done | bytes 131104 | tf_op jit(solution)/shard_map/all_to_all | solution.py:261
  65.8 0.0 copy-done.4
  65.8 0.0 copy-done.5
  65.8 1.1 %shard_map.80 = bf16[256,384]{1,0:T(8,128)(2,1)} custom-call(bf16[512,128]{1,0:T(8,128)(2,1)S(1)} %bitcast.6, bf16[256,1152]{1,0:T(8,128)(2,1)S(1)} %get-tuple-element.36.phi_ref, f32[256,384]{1,0:T(8,128)S(1)} %get-tuple-element.37.intra_ref, f32[64,384]{1,0:T(8,128)S(1)} %shard_map.79.early_ref, f32[192,384]{1,0:T(8,128)S(1)} %copy-done.5, ...), custom_call_target="tpu_custom_call" | custom-call | flops 1400000000 | bytes 1574400 | tf_op jit(solution)/shard_map/pallas_call | solution.py:247
  (1 shorter events, 0.0 us)
Async XLA Ops:
  0.0 12.0 %copy-start.3 = (bf16[1536,96]{0,1:T(8,128)(2,1)S(1)}, bf16[1536,96]{0,1:T(8,128)(2,1)}, u32[]{:S(2)}) copy-start(bf16[1536,96]{0,1:T(8,128)(2,1)} %param.9) | copy-start | bytes 884740
  0.0 12.0 %copy-start = (bf16[1536,384]{1,0:T(8,128)(2,1)S(1)}, bf16[1536,384]{1,0:T(8,128)(2,1)}, u32[]{:S(2)}) copy-start(bf16[1536,384]{1,0:T(8,128)(2,1)} %wv_ref.1) | copy-start | bytes 3538948
  13.4 30.6 %copy-start.2 = (bf16[1536,384]{1,0:T(8,128)(2,1)S(1)}, bf16[1536,384]{1,0:T(8,128)(2,1)}, u32[]{:S(2)}) copy-start(bf16[1536,384]{1,0:T(8,128)(2,1)} %wk_ref.1) | copy-start | bytes 3538948
  33.7 10.2 %copy-start.1 = (bf16[1536,384]{1,0:T(8,128)(2,1)S(1)}, bf16[1536,384]{1,0:T(8,128)(2,1)}, u32[]{:S(2)}) copy-start(bf16[1536,384]{1,0:T(8,128)(2,1)} %wq_ref.1) | copy-start | bytes 3538948
  34.5 16.9 %all-to-all-start.1 = ((bf16[8,32,128]{2,1,0:T(8,128)(2,1)}), bf16[8,32,128]{2,1,0:T(8,128)(2,1)S(1)}, u32[]{:S(2)}, u32[]{:S(2)}) async-start(bf16[8,32,128]{2,1,0:T(8,128)(2,1)} %shard_map.75), calls=%async_computation.1 | async-start | bytes 131072 | tf_op jit(solution)/shard_map/all_to_all | solution.py:261
  51.4 5.2 %copy-start.7 = (bf16[64,768]{1,0:T(8,128)(2,1)S(1)}, bf16[64,768]{1,0:T(8,128)(2,1)}, u32[]{:S(2)}) copy-start(bf16[64,768]{1,0:T(8,128)(2,1)} %get-tuple-element.40) | copy-start | bytes 294916
  51.4 11.0 %copy-start.6 = (bf16[64,1152]{1,0:T(8,128)(2,1)S(1)}, bf16[64,1152]{1,0:T(8,128)(2,1)}, u32[]{:S(2)}) copy-start(bf16[64,1152]{1,0:T(8,128)(2,1)} %get-tuple-element.39.head_ref) | copy-start | bytes 442372
  52.1 13.7 %all-to-all-start.2 = ((bf16[16,32,128]{2,1,0:T(8,128)(2,1)}), bf16[16,32,128]{2,1,0:T(8,128)(2,1)S(1)}, u32[]{:S(2)}, u32[]{:S(2)}) async-start(bf16[16,32,128]{2,1,0:T(8,128)(2,1)} %shard_map.78), calls=%async_computation.2 | async-start | bytes 262144 | tf_op jit(solution)/shard_map/all_to_all | solution.py:261
  56.6 9.2 %copy-start.4 = (f32[384]{0:T(512)S(1)}, f32[384]{0:T(512)}, u32[]{:S(2)}) copy-start(f32[384]{0:T(512)} %gain_ref.1) | copy-start | bytes 4612
  56.6 9.2 %copy-start.5 = (f32[192,384]{1,0:T(8,128)S(1)}, f32[192,384]{1,0:T(8,128)}, u32[]{:S(2)}) copy-start(f32[192,384]{1,0:T(8,128)} %get-tuple-element.41.window_ref) | copy-start | bytes 884740
  56.6 5.7 %collective-permute-start = (bf16[64,768]{1,0:T(8,128)(2,1)S(1)}, bf16[64,768]{1,0:T(8,128)(2,1)S(1)}, u32[]{:S(2)}, u32[]{:S(2)}) collective-permute-start(bf16[64,768]{1,0:T(8,128)(2,1)S(1)} %copy-done.7), channel_id=1, source_target_pairs={{0,4},{4,8},{8,12},{12,16},{16,20},{20,24},{24,28},{28,32},{32,36}... | collective-permute-start | bytes 294920 | tf_op jit(solution)/shard_map/ppermute | solution.py:323

commit v8 on v7

--- a/solution.py
+++ b/solution.py
@@ -18,6 +18,7 @@
 PLANE = ("seq_1", "seq_2")
 F32 = jnp.float32
 BF16 = jnp.bfloat16
+SHRINK = 2.0**-30
 FLOPS_PER_NS = 1_000_000
 NT = (((1,), (1,)), ((), ()))
 
@@ -74,15 +75,16 @@
 
 
 def state_kernel(rows, chunks, x_ref, wk_ref, wv_ref, state_ref, v_hbm, v_ref, v_sem):
+    kt = project_transposed(wk_ref, x_ref, rows, chunks)
     v = project(x_ref, wv_ref, rows, chunks).astype(BF16)
+    blocks = features(kt, 1.0, 1.0)
+    pairs = v.shape[1] // 128
+    lefts = [jnp.concatenate([b[32 * p : 32 * p + 32] for b in blocks], axis=0) for p in range(pairs)]
     v_ref[...] = v
     store = pltpu.make_async_copy(v_ref, v_hbm, v_sem)
     store.start()
-    blocks = features(project_transposed(wk_ref, x_ref, rows, chunks), 1.0, 1.0)
-    pairs = v.shape[1] // 128
     for p in range(pairs):
-        left = jnp.concatenate([b[32 * p : 32 * p + 32] for b in blocks], axis=0)
-        both = dot(left, v[:, 128 * p : 128 * p + 128]).reshape(BLOCKS, 2, FK, 128)
+        both = dot(lefts[p], v[:, 128 * p : 128 * p + 128]).reshape(BLOCKS, 2, FK, 128)
         one = jnp.where(low_half((BLOCKS, FK, 128)), both[:, 0], both[:, 1])
         state_ref[PAIR_ROWS * p : PAIR_ROWS * (p + 1), :] = one.reshape(PAIR_ROWS, 128).astype(BF16)
     used = PAIR_ROWS * pairs
@@ -221,13 +223,14 @@
         right = jnp.concatenate([right, jnp.zeros((384 - 2 * PAIR_ROWS, 128), BF16)], axis=0)
         linears.append(intra_ref[:, at] + dot(phi_ref[:, 384 * p : 384 * (p + 1)], right))
     for linear in linears:
-        square = linear * linear
+        square = (linear * SHRINK) * (linear * SHRINK)
         hi = square.astype(BF16)
         lo = (square - hi.astype(F32)).astype(BF16)
         squares.append(dot(jnp.concatenate([hi, lo], axis=1), mean_ref[...]))
     stores = []
     for p, at in enumerate(pairs):
-        normed = linears[p] * lax.rsqrt(squares[p] + 1e-5) * gain_ref[at].reshape(1, 128)
+        scale = lax.rsqrt(squares[p] + 1e-5 * SHRINK * SHRINK) * SHRINK
+        normed = linears[p] * scale * gain_ref[at].reshape(1, 128)
         out_ref[p, :WIN, :] = (normed[:WIN] + early_ref[:, at]).astype(BF16)
         out_ref[p, WIN:, :] = (normed[WIN:] + window_ref[:, at]).astype(BF16)
         stores.append(pltpu.make_async_copy(out_ref.at[p], out_hbm.at[:, at], sem.at[p]))

time: 67.3 us -> 67.6 us (level)
  no operation moved by 1% of the time
where the time goes in v8:
time: 67.6 us; the launch traced here: 67.3 us
  blocking collectives  32.3 us (48%)
  starting transfers between devices  17.7 us (26%)
  Pallas kernels  10.6 us (16%)
  waiting for transfers between devices  6.58 us (10%)
    all_to_all x1, blocking collectives, exchange(): return lax.all_to_all(x, axis, split_axis=0, concat_axis=0, tiled=True)  20.3 us
    all_to_all x2, starting transfers between devices, exchange(): return lax.all_to_all(x, axis, split_axis=0, concat_axis=0, tiled=True)  14 us
    all_gather x1, blocking collectives, body(): whole = lax.all_gather(hidden_states, 'head', tiled=True)  11.9 us
    pallas_call x8, Pallas kernels, call(): pl.pallas_call(kernel, out_shape=[space(shape, dtype) for shape, dtype, s...  10.6 us
    all_to_all x2, waiting for transfers between devices, exchange(): return lax.all_to_all(x, axis, split_axis=0, concat_axis=0, tiled=True)  4.52 us
    ppermute x1, starting transfers between devices, body(): halo = lax.ppermute(halo, SEQ, [(i, i + 1) for i in range(devices - 1)])  3.68 us
    ppermute x1, waiting for transfers between devices, body(): halo = lax.ppermute(halo, SEQ, [(i, i + 1) for i in range(devices - 1)])  2.05 us
  transfers between devices with their start and end apart: 3, of which 3 were waited for; matrix products, arithmetic and copies ran while one was open for 0% of the time, Pallas kernels for 9%

profile of v8, /device:TPU:1, one launch (start us, length us, event | category | flops | bytes accessed | tf_op | source)
XLA Modules:
  0.0 67.3 jit_solution(9867050819703573753)
XLA Ops:
  0.0 0.0 copy-start.3
  0.0 0.0 copy-start
  0.0 11.9 %all_gather.3.x_ref = bf16[1024,384]{1,0:T(8,128)(2,1)S(1)} all-gather(bf16[256,384]{1,0:T(8,128)(2,1)} %param.7), channel_id=1, replica_groups=mesh['seq_0'=8,'seq_1'=8,'seq_2'=2,'head'=4] {'head'}, dimensions={0}, use_global_device_ids=true | all-gather | bytes 983040 | tf_op jit(solution)/shard_map/all_gather | solution.py:283
  12.0 0.0 copy-done.3
  12.0 0.0 copy-done
  12.0 1.7 %shard_map.74 = (bf16[512,128]{1,0:T(8,128)(2,1)S(1)}, bf16[256,384]{1,0:T(8,128)(2,1)}) custom-call(bf16[1024,384]{1,0:T(8,128)(2,1)S(1)} %all_gather.3.x_ref, bf16[96,1536]{1,0:T(8,128)(2,1)S(1)} %bitcast.9, bf16[1536,384]{1,0:T(8,128)(2,1)S(1)} %copy-done), custom_call_target="tpu_custom_call" | custom-call | flops 1500000000 | bytes 2260992 | tf_op jit(solution)/shard_map/pallas_call | solution.py:250
  13.7 0.0 copy-start.2
  13.7 20.3 %all_to_all.15.slices_ref = bf16[16,32,128]{2,1,0:T(8,128)(2,1)S(1)} all-to-all(bf16[16,32,128]{2,1,0:T(8,128)(2,1)S(1)} %bitcast.7), channel_id=1, replica_groups=mesh['seq_0'=8,'seq_1'=8,'seq_2'=2,'head'=4] {'seq_1','seq_2'}, dimensions={0} | all-to-all | bytes 262144 | tf_op jit(solution)/shard_map/all_to_all | solution.py:264
  34.0 0.0 copy-start.1
  34.0 0.7 %shard_map.75 = bf16[8,32,128]{2,1,0:T(8,128)(2,1)} custom-call(bf16[16,32,128]{2,1,0:T(8,128)(2,1)S(1)} %all_to_all.15.slices_ref), custom_call_target="tpu_custom_call" | custom-call | flops 600000000 | bytes 131072 | tf_op jit(solution)/shard_map/pallas_call | solution.py:250
  34.7 9.5 %all-to-all-start.1 = ((bf16[8,32,128]{2,1,0:T(8,128)(2,1)}), bf16[8,32,128]{2,1,0:T(8,128)(2,1)S(1)}, u32[]{:S(2)}, u32[]{:S(2)}) async-start(bf16[8,32,128]{2,1,0:T(8,128)(2,1)} %shard_map.75), calls=%async_computation.1 | async-start | bytes 131072 | tf_op jit(solution)/shard_map/all_to_all | solution.py:264
  44.2 0.0 copy-done.2
  44.2 0.0 copy-done.1
  44.2 3.4 %shard_map.76 = (f32[192,384]{1,0:T(8,128)}, bf16[64,1152]{1,0:T(8,128)(2,1)}, bf16[64,768]{1,0:T(8,128)(2,1)}) custom-call(bf16[1024,384]{1,0:T(8,128)(2,1)S(1)} %all_gather.3.x_ref, bf16[1536,384]{1,0:T(8,128)(2,1)S(1)} %copy-done.1, bf16[1536,384]{1,0:T(8,128)(2,1)S(1)} %copy-done.2, bf16[256,384]{1,0:T(8,128)(2,1)} %get-tuple-element.29.v_ref), custom_call_target="tpu_custom_call" | custom-call | flops 3500000000 | bytes 3342336 | tf_op jit(solution)/shard_map/pallas_call | solution.py:250
  47.7 2.4 %shard_map.77 = (f32[256,384]{1,0:T(8,128)S(1)}, bf16[256,1152]{1,0:T(8,128)(2,1)S(1)}) custom-call(bf16[1024,384]{1,0:T(8,128)(2,1)S(1)} %all_gather.3.x_ref, bf16[96,1536]{1,0:T(8,128)(2,1)} %bitcast.10, bf16[96,1536]{1,0:T(8,128)(2,1)} %bitcast.8, bf16[256,384]{1,0:T(8,128)(2,1)} %get-tuple-element.29.v_ref), custom_call_target="tpu_custom_call" | custom-call | flops 2200000000 | bytes 1572864 | tf_op jit(solution)/shard_map/pallas_call | solution.py:250
  50.1 1.6 %all-to-all-done.1.totals_ref = bf16[8,32,128]{2,1,0:T(8,128)(2,1)S(1)} async-done(((bf16[8,32,128]{2,1,0:T(8,128)(2,1)}), bf16[8,32,128]{2,1,0:T(8,128)(2,1)S(1)}, u32[]{:S(2)}, u32[]{:S(2)}) %all-to-all-start.1) | async-done | bytes 65568 | tf_op jit(solution)/shard_map/all_to_all | solution.py:264
  51.7 0.0 copy-start.7
  51.7 0.0 copy-start.6
  51.7 0.7 %shard_map.78 = bf16[16,32,128]{2,1,0:T(8,128)(2,1)} custom-call(s32[1]{0:T(128)} %bitcast.plane_ref, bf16[16,32,128]{2,1,0:T(8,128)(2,1)S(1)} %all_to_all.15.slices_ref, bf16[8,32,128]{2,1,0:T(8,128)(2,1)S(1)} %all-to-all-done.1.totals_ref), custom_call_target="tpu_custom_call" | custom-call | flops 1000000000 | bytes 196612 | tf_op jit(solution)/shard_map/pallas_call | solution.py:250
  52.4 4.5 %all-to-all-start.2 = ((bf16[16,32,128]{2,1,0:T(8,128)(2,1)}), bf16[16,32,128]{2,1,0:T(8,128)(2,1)S(1)}, u32[]{:S(2)}, u32[]{:S(2)}) async-start(bf16[16,32,128]{2,1,0:T(8,128)(2,1)} %shard_map.78), calls=%async_computation.2 | async-start | bytes 262144 | tf_op jit(solution)/shard_map/all_to_all | solution.py:264
  56.9 0.0 copy-done.7
  56.9 0.0 copy-start.4
  56.9 0.0 copy-start.5
  56.9 3.7 %collective-permute-start = (bf16[64,768]{1,0:T(8,128)(2,1)S(1)}, bf16[64,768]{1,0:T(8,128)(2,1)S(1)}, u32[]{:S(2)}, u32[]{:S(2)}) collective-permute-start(bf16[64,768]{1,0:T(8,128)(2,1)S(1)} %copy-done.7), channel_id=1, source_target_pairs={{0,4},{4,8},{8,12},{12,16},{16,20},{20,24},{24,28},{28,32},{32,36}... | collective-permute-start | bytes 294920 | tf_op jit(solution)/shard_map/ppermute | solution.py:326
  60.6 2.1 %collective-permute-done.halo_ref = bf16[64,768]{1,0:T(8,128)(2,1)S(1)} collective-permute-done((bf16[64,768]{1,0:T(8,128)(2,1)S(1)}, bf16[64,768]{1,0:T(8,128)(2,1)S(1)}, u32[]{:S(2)}, u32[]{:S(2)}) %collective-permute-start) | collective-permute-done | bytes 98336 | tf_op jit(solution)/shard_map/ppermute | solution.py:326
  62.6 0.0 copy-done.6
  62.6 0.5 shard_map.79.early_ref
  63.1 3.0 %all-to-all-done.2 = bf16[16,32,128]{2,1,0:T(8,128)(2,1)S(1)} async-done(((bf16[16,32,128]{2,1,0:T(8,128)(2,1)}), bf16[16,32,128]{2,1,0:T(8,128)(2,1)S(1)}, u32[]{:S(2)}, u32[]{:S(2)}) %all-to-all-start.2) | async-done | bytes 131104 | tf_op jit(solution)/shard_map/all_to_all | solution.py:264
  66.1 0.0 copy-done.4
  66.1 0.0 copy-done.5
  66.1 1.1 %shard_map.80 = bf16[256,384]{1,0:T(8,128)(2,1)} custom-call(bf16[512,128]{1,0:T(8,128)(2,1)S(1)} %bitcast.6, bf16[256,1152]{1,0:T(8,128)(2,1)S(1)} %get-tuple-element.36.phi_ref, f32[256,384]{1,0:T(8,128)S(1)} %get-tuple-element.37.intra_ref, f32[64,384]{1,0:T(8,128)S(1)} %shard_map.79.early_ref, f32[192,384]{1,0:T(8,128)S(1)} %copy-done.5, ...), custom_call_target="tpu_custom_call" | custom-call | flops 1400000000 | bytes 1574400 | tf_op jit(solution)/shard_map/pallas_call | solution.py:250
  (1 shorter events, 0.0 us)
Async XLA Ops:
  0.0 12.0 %copy-start.3 = (bf16[1536,96]{0,1:T(8,128)(2,1)S(1)}, bf16[1536,96]{0,1:T(8,128)(2,1)}, u32[]{:S(2)}) copy-start(bf16[1536,96]{0,1:T(8,128)(2,1)} %param.9) | copy-start | bytes 884740
  0.0 12.0 %copy-start = (bf16[1536,384]{1,0:T(8,128)(2,1)S(1)}, bf16[1536,384]{1,0:T(8,128)(2,1)}, u32[]{:S(2)}) copy-start(bf16[1536,384]{1,0:T(8,128)(2,1)} %wv_ref.1) | copy-start | bytes 3538948
  13.7 30.6 %copy-start.2 = (bf16[1536,384]{1,0:T(8,128)(2,1)S(1)}, bf16[1536,384]{1,0:T(8,128)(2,1)}, u32[]{:S(2)}) copy-start(bf16[1536,384]{1,0:T(8,128)(2,1)} %wk_ref.1) | copy-start | bytes 3538948
  34.0 10.2 %copy-start.1 = (bf16[1536,384]{1,0:T(8,128)(2,1)S(1)}, bf16[1536,384]{1,0:T(8,128)(2,1)}, u32[]{:S(2)}) copy-start(bf16[1536,384]{1,0:T(8,128)(2,1)} %wq_ref.1) | copy-start | bytes 3538948
  34.7 16.9 %all-to-all-start.1 = ((bf16[8,32,128]{2,1,0:T(8,128)(2,1)}), bf16[8,32,128]{2,1,0:T(8,128)(2,1)S(1)}, u32[]{:S(2)}, u32[]{:S(2)}) async-start(bf16[8,32,128]{2,1,0:T(8,128)(2,1)} %shard_map.75), calls=%async_computation.1 | async-start | bytes 131072 | tf_op jit(solution)/shard_map/all_to_all | solution.py:264
  51.7 5.2 %copy-start.7 = (bf16[64,768]{1,0:T(8,128)(2,1)S(1)}, bf16[64,768]{1,0:T(8,128)(2,1)}, u32[]{:S(2)}) copy-start(bf16[64,768]{1,0:T(8,128)(2,1)} %get-tuple-element.40) | copy-start | bytes 294916
  51.7 11.0 %copy-start.6 = (bf16[64,1152]{1,0:T(8,128)(2,1)S(1)}, bf16[64,1152]{1,0:T(8,128)(2,1)}, u32[]{:S(2)}) copy-start(bf16[64,1152]{1,0:T(8,128)(2,1)} %get-tuple-element.39.head_ref) | copy-start | bytes 442372
  52.4 13.7 %all-to-all-start.2 = ((bf16[16,32,128]{2,1,0:T(8,128)(2,1)}), bf16[16,32,128]{2,1,0:T(8,128)(2,1)S(1)}, u32[]{:S(2)}, u32[]{:S(2)}) async-start(bf16[16,32,128]{2,1,0:T(8,128)(2,1)} %shard_map.78), calls=%async_computation.2 | async-start | bytes 262144 | tf_op jit(solution)/shard_map/all_to_all | solution.py:264
  56.9 9.2 %copy-start.4 = (f32[384]{0:T(512)S(1)}, f32[384]{0:T(512)}, u32[]{:S(2)}) copy-start(f32[384]{0:T(512)} %gain_ref.1) | copy-start | bytes 4612
  56.9 9.2 %copy-start.5 = (f32[192,384]{1,0:T(8,128)S(1)}, f32[192,384]{1,0:T(8,128)}, u32[]{:S(2)}) copy-start(f32[192,384]{1,0:T(8,128)} %get-tuple-element.41.window_ref) | copy-start | bytes 884740
  56.9 5.7 %collective-permute-start = (bf16[64,768]{1,0:T(8,128)(2,1)S(1)}, bf16[64,768]{1,0:T(8,128)(2,1)S(1)}, u32[]{:S(2)}, u32[]{:S(2)}) collective-permute-start(bf16[64,768]{1,0:T(8,128)(2,1)S(1)} %copy-done.7), channel_id=1, source_target_pairs={{0,4},{4,8},{8,12},{12,16},{16,20},{20,24},{24,28},{28,32},{32,36}... | collective-permute-start | bytes 294920 | tf_op jit(solution)/shard_map/ppermute | solution.py:326

commit v9 on v8

--- a/solution.py
+++ b/solution.py
@@ -74,17 +74,23 @@
     out_ref[...] = jnp.where((i < HV) == (j < HV), 1.0 / HV, 0.0).astype(BF16)
 
 
-def state_kernel(rows, chunks, x_ref, wk_ref, wv_ref, state_ref, v_hbm, v_ref, v_sem):
-    kt = project_transposed(wk_ref, x_ref, rows, chunks)
-    v = project(x_ref, wv_ref, rows, chunks).astype(BF16)
-    blocks = features(kt, 1.0, 1.0)
-    pairs = v.shape[1] // 128
-    lefts = [jnp.concatenate([b[32 * p : 32 * p + 32] for b in blocks], axis=0) for p in range(pairs)]
-    v_ref[...] = v
+def whole_rows(x_ref, rows, chunks):
+    return jnp.concatenate([x_ref[c * rows : (c + 1) * rows, :] for c in range(chunks)], axis=1)
+
+
+def state_kernel(rows, chunks, x_ref, wk_ref, wv_ref, state_ref, v_hbm, v_ref, left_ref, v_sem):
+    x = whole_rows(x_ref, rows, chunks)
+    kt = lax.dot_general(wk_ref[...], x, NT, preferred_element_type=F32) * FK ** (-0.25)
+    v_ref[...] = dot(x, wv_ref[...]).astype(BF16)
     store = pltpu.make_async_copy(v_ref, v_hbm, v_sem)
     store.start()
+    blocks = features(kt, 1.0, 1.0)
+    pairs = left_ref.shape[0]
     for p in range(pairs):
-        both = dot(lefts[p], v[:, 128 * p : 128 * p + 128]).reshape(BLOCKS, 2, FK, 128)
+        for n, block in enumerate(blocks):
+            left_ref[p, 32 * n : 32 * (n + 1), :] = block[32 * p : 32 * p + 32]
+    for p in range(pairs):
+        both = dot(left_ref[p], v_ref[:, 128 * p : 128 * p + 128]).reshape(BLOCKS, 2, FK, 128)
         one = jnp.where(low_half((BLOCKS, FK, 128)), both[:, 0], both[:, 1])
         state_ref[PAIR_ROWS * p : PAIR_ROWS * (p + 1), :] = one.reshape(PAIR_ROWS, 128).astype(BF16)
     used = PAIR_ROWS * pairs
@@ -178,16 +184,13 @@
         intra_ref[:, 128 * p : 128 * p + 128] = jnp.where(low_half((rows, 128)), outs[0], outs[1])
 
 
-def total_kernel(slices_ref, out_hbm, total_ref, sem):
+def total_kernel(slices_ref, out_ref):
     total = slices_ref[0].astype(F32)
     for i in range(1, slices_ref.shape[0]):
         total = total + slices_ref[i].astype(F32)
-    total_ref[...] = total.astype(BF16)
-    stores = [pltpu.make_async_copy(total_ref, out_hbm.at[z], sem.at[z]) for z in range(out_hbm.shape[0])]
-    for store in stores:
-        store.start()
-    for store in stores:
-        store.wait()
+    total = total.astype(BF16)
+    for z in range(out_ref.shape[0]):
+        out_ref[z] = total
 
 
 def prefix_kernel(plane_ref, slices_ref, totals_ref, out_hbm, out_ref, sem):
@@ -286,34 +289,18 @@
         [((held, 128), BF16, vmem), ((rows, width), BF16, hbm)],
         [(whole, vmem), (feature_k.T, vmem), (value_w, vmem)],
         1500,
-        scratch=[pltpu.VMEM((rows, width), BF16), pltpu.SemaphoreType.DMA(())],
+        scratch=[
+            pltpu.VMEM((rows, width), BF16),
+            pltpu.VMEM((width // 128, 2 * PAIR_ROWS, rows), BF16),
+            pltpu.SemaphoreType.DMA(()),
+        ],
     )
     slices = exchange(state.reshape(members, held // members, 128), PLANE)
     slices, v = lax.optimization_barrier((slices, v))
-    piece_shape = slices.shape[1:]
     (totals,) = call(
-        total_kernel,
-        [((planes, *piece_shape), BF16, hbm)],
-        [(slices, vmem)],
-        600,
-        scratch=[pltpu.VMEM(piece_shape, BF16), pltpu.SemaphoreType.DMA((planes,))],
+        total_kernel, [((planes, *slices.shape[1:]), BF16, vmem)], [(slices, vmem)], 300
     )
     totals = exchange(totals, "seq_0")
-    window, head, halo = call(
-        functools.partial(window_kernel, rows, chunks),
-        [((rows - WIN, width), F32, hbm), ((WIN, 3 * width), BF16, hbm), ((WIN, 2 * width), BF16, hbm)],
-        [(whole, vmem), (window_q, vmem), (window_k, vmem), (v, hbm)],
-        3500,
-    )
-    intra, phi = call(
-        functools.partial(intra_kernel, rows, chunks),
-        [((rows, width), F32, vmem), ((rows, 3 * width), BF16, vmem)],
-        [(whole, vmem), (feature_q.T, hbm), (feature_k.T, hbm), (v, hbm)],
-        2200,
-    )
-    totals, window, head, halo, intra, phi = lax.optimization_barrier(
-        (totals, window, head, halo, intra, phi)
-    )
     (before,) = call(
         prefix_kernel,
         [(slices.shape, BF16, hbm)],
@@ -321,9 +308,22 @@
         1000,
         scratch=[pltpu.VMEM(slices.shape, BF16), pltpu.SemaphoreType.DMA((4,))],
     )
+    before, v = lax.optimization_barrier((before, v))
     prefix = exchange(before, PLANE).reshape(held, 128)
+    window, head, halo = call(
+        functools.partial(window_kernel, rows, chunks),
+        [((rows - WIN, width), F32, hbm), ((WIN, 3 * width), BF16, hbm), ((WIN, 2 * width), BF16, hbm)],
+        [(whole, vmem), (window_q, vmem), (window_k, vmem), (v, hbm)],
+        1000,
+    )
     devices = lax.axis_size(SEQ)
     halo = lax.ppermute(halo, SEQ, [(i, i + 1) for i in range(devices - 1)])
+    intra, phi = call(
+        functools.partial(intra_kernel, rows, chunks),
+        [((rows, width), F32, vmem), ((rows, 3 * width), BF16, vmem)],
+        [(whole, vmem), (feature_q.T, hbm), (feature_k.T, hbm), (v, hbm)],
+        700,
+    )
     (early,) = call(
         first_window_kernel,
         [((WIN, width), F32, vmem)],

time: 67.6 us -> 68.3 us (1.010)
  blocking collectives: 32.3 us -> 48.8 us
  starting transfers between devices: 17.7 us -> 8.16 us
  waiting for transfers between devices: 6.58 us -> 0.01 us
  Pallas kernels: 10.6 us -> 9.81 us
    all_to_all x1 -> x2, blocking collectives: 20.3 us -> 36.9 us  [exchange(): return lax.all_to_all(x, axis, split_axis=0, concat_axis=0, tiled=True)]
    all_to_all x2 -> x1, starting transfers between devices: 14 us -> 4.63 us  [exchange(): return lax.all_to_all(x, axis, split_axis=0, concat_axis=0, tiled=True)]
    all_to_all x2 -> x1, waiting for transfers between devices: 4.52 us -> 0.01 us  [exchange(): return lax.all_to_all(x, axis, split_axis=0, concat_axis=0, tiled=True)]
    ppermute x1, waiting for transfers between devices: 2.05 us -> 0.01 us  [body(): halo = lax.ppermute(halo, SEQ, [(i, i + 1) for i in range(devices - 1)])]
    pallas_call x8, Pallas kernels: 10.6 us -> 9.81 us  [call(): pl.pallas_call(kernel, out_shape=[space(shape, dtype) for shape, dtype, s...]
  transfers between devices with their start and end apart: 3 -> 2, of which waited for: 3 -> 0; matrix products, arithmetic and copies ran while one was open for 0% -> 0% of each run, Pallas kernels for 9% -> 10%
where the time goes in v9:
time: 68.3 us; the launch traced here: 67.4 us
  blocking collectives  48.8 us (71%)
  Pallas kernels  9.81 us (14%)
  starting transfers between devices  8.16 us (12%)
    all_to_all x2, blocking collectives, exchange(): return lax.all_to_all(x, axis, split_axis=0, concat_axis=0, tiled=True)  36.9 us
    all_gather x1, blocking collectives, body(): whole = lax.all_gather(hidden_states, 'head', tiled=True)  11.9 us
    pallas_call x8, Pallas kernels, call(): pl.pallas_call(kernel, out_shape=[space(shape, dtype) for shape, dtype, s...  9.81 us
    all_to_all x1, starting transfers between devices, exchange(): return lax.all_to_all(x, axis, split_axis=0, concat_axis=0, tiled=True)  4.63 us
    ppermute x1, starting transfers between devices, body(): halo = lax.ppermute(halo, SEQ, [(i, i + 1) for i in range(devices - 1)])  3.53 us
  transfers between devices with their start and end apart: 2, of which 0 were waited for; matrix products, arithmetic and copies ran while one was open for 0% of the time, Pallas kernels for 10%

profile of v9, /device:TPU:1, one launch (start us, length us, event | category | flops | bytes accessed | tf_op | source)
XLA Modules:
  0.0 67.4 jit_solution(14232773963613195935)
XLA Ops:
  0.0 0.0 copy-start.3
  0.0 0.0 copy-start
  0.0 11.9 %all_gather.3.x_ref = bf16[1024,384]{1,0:T(8,128)(2,1)S(1)} all-gather(bf16[256,384]{1,0:T(8,128)(2,1)} %param.7), channel_id=1, replica_groups=mesh['seq_0'=8,'seq_1'=8,'seq_2'=2,'head'=4] {'head'}, dimensions={0}, use_global_device_ids=true | all-gather | bytes 983040 | tf_op jit(solution)/shard_map/all_gather | solution.py:286
  12.0 0.0 copy-done.3
  12.0 0.0 copy-done
  12.0 1.5 %shard_map.74 = (bf16[512,128]{1,0:T(8,128)(2,1)S(1)}, bf16[256,384]{1,0:T(8,128)(2,1)}) custom-call(bf16[1024,384]{1,0:T(8,128)(2,1)S(1)} %all_gather.3.x_ref, bf16[96,1536]{1,0:T(8,128)(2,1)S(1)} %bitcast.9, bf16[1536,384]{1,0:T(8,128)(2,1)S(1)} %copy-done), custom_call_target="tpu_custom_call" | custom-call | flops 1500000000 | bytes 2260992 | tf_op jit(solution)/shard_map/pallas_call | solution.py:253
  13.5 20.2 %all_to_all.15.slices_ref = bf16[16,32,128]{2,1,0:T(8,128)(2,1)S(1)} all-to-all(bf16[16,32,128]{2,1,0:T(8,128)(2,1)S(1)} %bitcast.7), channel_id=1, replica_groups=mesh['seq_0'=8,'seq_1'=8,'seq_2'=2,'head'=4] {'seq_1','seq_2'}, dimensions={0} | all-to-all | bytes 262144 | tf_op jit(solution)/shard_map/all_to_all | solution.py:267
  33.8 16.7 %all_to_all.16.totals_ref = bf16[8,32,128]{2,1,0:T(8,128)(2,1)S(1)} all-to-all(bf16[8,32,128]{2,1,0:T(8,128)(2,1)S(1)} %shard_map.75), channel_id=1, replica_groups=mesh['seq_0'=8,'seq_1'=8,'seq_2'=2,'head'=4] {'seq_0'}, dimensions={0} | all-to-all | bytes 131072 | tf_op jit(solution)/shard_map/all_to_all | solution.py:267
  50.5 0.0 copy-start.1
  50.5 0.0 copy-start.2
  50.5 0.7 %shard_map.76 = bf16[16,32,128]{2,1,0:T(8,128)(2,1)} custom-call(s32[1]{0:T(128)} %bitcast.plane_ref, bf16[16,32,128]{2,1,0:T(8,128)(2,1)S(1)} %all_to_all.15.slices_ref, bf16[8,32,128]{2,1,0:T(8,128)(2,1)S(1)} %all_to_all.16.totals_ref), custom_call_target="tpu_custom_call" | custom-call | flops 1000000000 | bytes 196612 | tf_op jit(solution)/shard_map/pallas_call | solution.py:253
  51.2 4.6 %all-to-all-start.2 = ((bf16[16,32,128]{2,1,0:T(8,128)(2,1)}), bf16[16,32,128]{2,1,0:T(8,128)(2,1)S(1)}, u32[]{:S(2)}, u32[]{:S(2)}) async-start(bf16[16,32,128]{2,1,0:T(8,128)(2,1)} %shard_map.76), calls=%async_computation.2 | async-start | bytes 262144 | tf_op jit(solution)/shard_map/all_to_all | solution.py:267
  55.8 0.0 copy-done.1
  55.8 0.0 copy-done.2
  55.8 3.4 %shard_map.78 = (f32[192,384]{1,0:T(8,128)}, bf16[64,1152]{1,0:T(8,128)(2,1)}, bf16[64,768]{1,0:T(8,128)(2,1)}) custom-call(bf16[1024,384]{1,0:T(8,128)(2,1)S(1)} %all_gather.3.x_ref, bf16[1536,384]{1,0:T(8,128)(2,1)S(1)} %copy-done.1, bf16[1536,384]{1,0:T(8,128)(2,1)S(1)} %copy-done.2, bf16[256,384]{1,0:T(8,128)(2,1)} %get-tuple-element.27.v_ref), custom_call_target="tpu_custom_call" | custom-call | flops 1000000000 | bytes 3342336 | tf_op jit(solution)/shard_map/pallas_call | solution.py:253
  59.3 3.5 %collective-permute-start = (bf16[64,768]{1,0:T(8,128)(2,1)}, bf16[64,768]{1,0:T(8,128)(2,1)S(1)}, u32[]{:S(2)}, u32[]{:S(2)}) collective-permute-start(bf16[64,768]{1,0:T(8,128)(2,1)} %get-tuple-element.32), channel_id=1, source_target_pairs={{0,4},{4,8},{8,12},{12,16},{16,20},{20,24},{24,28},{28,32},{32,36}... | collective-permute-start | bytes 294920 | tf_op jit(solution)/shard_map/ppermute | solution.py:320
  62.8 0.0 copy-start.6
  62.8 2.5 %shard_map.77 = (f32[256,384]{1,0:T(8,128)S(1)}, bf16[256,1152]{1,0:T(8,128)(2,1)S(1)}) custom-call(bf16[1024,384]{1,0:T(8,128)(2,1)S(1)} %all_gather.3.x_ref, bf16[96,1536]{1,0:T(8,128)(2,1)} %bitcast.10, bf16[96,1536]{1,0:T(8,128)(2,1)} %bitcast.8, bf16[256,384]{1,0:T(8,128)(2,1)} %get-tuple-element.27.v_ref), custom_call_target="tpu_custom_call" | custom-call | flops 700000000 | bytes 1572864 | tf_op jit(solution)/shard_map/pallas_call | solution.py:253
  65.3 0.0 collective-permute-done.halo_ref
  65.3 0.0 copy-done.6
  65.3 0.0 copy-start.4
  65.3 0.0 copy-start.5
  65.3 0.5 shard_map.79.early_ref
  65.8 0.0 all-to-all-done.2
  65.8 0.1 copy-done.4
  66.0 0.3 copy-done.5
  66.3 1.1 %shard_map.80 = bf16[256,384]{1,0:T(8,128)(2,1)} custom-call(bf16[512,128]{1,0:T(8,128)(2,1)S(1)} %bitcast.6, bf16[256,1152]{1,0:T(8,128)(2,1)S(1)} %get-tuple-element.28.phi_ref, f32[256,384]{1,0:T(8,128)S(1)} %get-tuple-element.29.intra_ref, f32[64,384]{1,0:T(8,128)S(1)} %shard_map.79.early_ref, f32[192,384]{1,0:T(8,128)S(1)} %copy-done.5, ...), custom_call_target="tpu_custom_call" | custom-call | flops 1400000000 | bytes 1574400 | tf_op jit(solution)/shard_map/pallas_call | solution.py:253
  (2 shorter events, 0.0 us)
Async XLA Ops:
  0.0 12.0 %copy-start.3 = (bf16[1536,96]{0,1:T(8,128)(2,1)S(1)}, bf16[1536,96]{0,1:T(8,128)(2,1)}, u32[]{:S(2)}) copy-start(bf16[1536,96]{0,1:T(8,128)(2,1)} %param.9) | copy-start | bytes 884740
  0.0 12.0 %copy-start = (bf16[1536,384]{1,0:T(8,128)(2,1)S(1)}, bf16[1536,384]{1,0:T(8,128)(2,1)}, u32[]{:S(2)}) copy-start(bf16[1536,384]{1,0:T(8,128)(2,1)} %wv_ref.1) | copy-start | bytes 3538948
  50.5 5.3 %copy-start.1 = (bf16[1536,384]{1,0:T(8,128)(2,1)S(1)}, bf16[1536,384]{1,0:T(8,128)(2,1)}, u32[]{:S(2)}) copy-start(bf16[1536,384]{1,0:T(8,128)(2,1)} %wq_ref.1) | copy-start | bytes 3538948
  50.5 5.3 %copy-start.2 = (bf16[1536,384]{1,0:T(8,128)(2,1)S(1)}, bf16[1536,384]{1,0:T(8,128)(2,1)}, u32[]{:S(2)}) copy-start(bf16[1536,384]{1,0:T(8,128)(2,1)} %wk_ref.1) | copy-start | bytes 3538948
  51.2 14.7 %all-to-all-start.2 = ((bf16[16,32,128]{2,1,0:T(8,128)(2,1)}), bf16[16,32,128]{2,1,0:T(8,128)(2,1)S(1)}, u32[]{:S(2)}, u32[]{:S(2)}) async-start(bf16[16,32,128]{2,1,0:T(8,128)(2,1)} %shard_map.76), calls=%async_computation.2 | async-start | bytes 262144 | tf_op jit(solution)/shard_map/all_to_all | solution.py:267
  59.3 6.0 %collective-permute-start = (bf16[64,768]{1,0:T(8,128)(2,1)}, bf16[64,768]{1,0:T(8,128)(2,1)S(1)}, u32[]{:S(2)}, u32[]{:S(2)}) collective-permute-start(bf16[64,768]{1,0:T(8,128)(2,1)} %get-tuple-element.32), channel_id=1, source_target_pairs={{0,4},{4,8},{8,12},{12,16},{16,20},{20,24},{24,28},{28,32},{32,36}... | collective-permute-start | bytes 294920 | tf_op jit(solution)/shard_map/ppermute | solution.py:320
  62.8 2.5 %copy-start.6 = (bf16[64,1152]{1,0:T(8,128)(2,1)S(1)}, bf16[64,1152]{1,0:T(8,128)(2,1)}, u32[]{:S(2)}) copy-start(bf16[64,1152]{1,0:T(8,128)(2,1)} %get-tuple-element.31.head_ref) | copy-start | bytes 442372
  65.3 0.7 %copy-start.4 = (f32[384]{0:T(512)S(1)}, f32[384]{0:T(512)}, u32[]{:S(2)}) copy-start(f32[384]{0:T(512)} %gain_ref.1) | copy-start | bytes 4612
  65.3 1.0 %copy-start.5 = (f32[192,384]{1,0:T(8,128)S(1)}, f32[192,384]{1,0:T(8,128)}, u32[]{:S(2)}) copy-start(f32[192,384]{1,0:T(8,128)} %get-tuple-element.33.window_ref) | copy-start | bytes 884740

commit v10 on v8

--- a/solution.py
+++ b/solution.py
@@ -74,22 +74,25 @@
     out_ref[...] = jnp.where((i < HV) == (j < HV), 1.0 / HV, 0.0).astype(BF16)
 
 
-def state_kernel(rows, chunks, x_ref, wk_ref, wv_ref, state_ref, v_hbm, v_ref, v_sem):
-    kt = project_transposed(wk_ref, x_ref, rows, chunks)
-    v = project(x_ref, wv_ref, rows, chunks).astype(BF16)
+def whole_rows(x_ref, rows, chunks):
+    return jnp.concatenate([x_ref[c * rows : (c + 1) * rows, :] for c in range(chunks)], axis=1)
+
+
+def state_kernel(rows, chunks, x_ref, wk_ref, wv_ref, state_ref, v_ref, left_ref):
+    x = whole_rows(x_ref, rows, chunks)
+    kt = lax.dot_general(wk_ref[...], x, NT, preferred_element_type=F32) * FK ** (-0.25)
+    v_ref[...] = dot(x, wv_ref[...]).astype(BF16)
     blocks = features(kt, 1.0, 1.0)
-    pairs = v.shape[1] // 128
-    lefts = [jnp.concatenate([b[32 * p : 32 * p + 32] for b in blocks], axis=0) for p in range(pairs)]
-    v_ref[...] = v
-    store = pltpu.make_async_copy(v_ref, v_hbm, v_sem)
-    store.start()
+    pairs = left_ref.shape[0]
     for p in range(pairs):
-        both = dot(lefts[p], v[:, 128 * p : 128 * p + 128]).reshape(BLOCKS, 2, FK, 128)
+        for n, block in enumerate(blocks):
+            left_ref[p, 32 * n : 32 * (n + 1), :] = block[32 * p : 32 * p + 32]
+    for p in range(pairs):
+        both = dot(left_ref[p], v_ref[:, 128 * p : 128 * p + 128]).reshape(BLOCKS, 2, FK, 128)
         one = jnp.where(low_half((BLOCKS, FK, 128)), both[:, 0], both[:, 1])
         state_ref[PAIR_ROWS * p : PAIR_ROWS * (p + 1), :] = one.reshape(PAIR_ROWS, 128).astype(BF16)
     used = PAIR_ROWS * pairs
     state_ref[used:, :] = jnp.zeros((state_ref.shape[0] - used, 128), BF16)
-    store.wait()
 
 
 def window_tiles(tiles, valid):
@@ -116,7 +119,8 @@
     return (col <= row + WIN) & (col > row), col
 
 
-def window_kernel(rows, chunks, x_ref, wq_ref, wk_ref, v_ref, out_ref, head_ref, halo_ref):
+def window_kernel(rows, chunks, x_ref, wq_ref, wk_ref, wv_ref, out_ref, head_ref, halo_ref, v_ref):
+    v_ref[...] = dot(whole_rows(x_ref, rows, chunks), wv_ref[...]).astype(BF16)
     keys = project(x_ref, wk_ref, rows, chunks).astype(BF16)
     queries = project(x_ref, wq_ref, rows, chunks).astype(BF16)
     width = keys.shape[1]
@@ -281,15 +285,15 @@
     (mean,) = call(mean_kernel, [((256, 128), BF16, vmem)], [], 200)
     hidden_states, mean, plane, first = lax.optimization_barrier((hidden_states, mean, plane, first))
     whole = lax.all_gather(hidden_states, "head", tiled=True)
-    state, v = call(
+    (state,) = call(
         functools.partial(state_kernel, rows, chunks),
-        [((held, 128), BF16, vmem), ((rows, width), BF16, hbm)],
+        [((held, 128), BF16, vmem)],
         [(whole, vmem), (feature_k.T, vmem), (value_w, vmem)],
         1500,
-        scratch=[pltpu.VMEM((rows, width), BF16), pltpu.SemaphoreType.DMA(())],
+        scratch=[pltpu.VMEM((rows, width), BF16), pltpu.VMEM((width // 128, 2 * PAIR_ROWS, rows), BF16)],
     )
     slices = exchange(state.reshape(members, held // members, 128), PLANE)
-    slices, v = lax.optimization_barrier((slices, v))
+    slices, whole = lax.optimization_barrier((slices, whole))
     piece_shape = slices.shape[1:]
     (totals,) = call(
         total_kernel,
@@ -299,11 +303,16 @@
         scratch=[pltpu.VMEM(piece_shape, BF16), pltpu.SemaphoreType.DMA((planes,))],
     )
     totals = exchange(totals, "seq_0")
-    window, head, halo = call(
+    window, head, halo, v = call(
         functools.partial(window_kernel, rows, chunks),
-        [((rows - WIN, width), F32, hbm), ((WIN, 3 * width), BF16, hbm), ((WIN, 2 * width), BF16, hbm)],
-        [(whole, vmem), (window_q, vmem), (window_k, vmem), (v, hbm)],
-        3500,
+        [
+            ((rows - WIN, width), F32, hbm),
+            ((WIN, 3 * width), BF16, hbm),
+            ((WIN, 2 * width), BF16, hbm),
+            ((rows, width), BF16, hbm),
+        ],
+        [(whole, vmem), (window_q, vmem), (window_k, vmem), (value_w, vmem)],
+        3900,
     )
     intra, phi = call(
         functools.partial(intra_kernel, rows, chunks),

time: 67.6 us -> 66.9 us (0.990)
  local copies, waits for them, and re-layouts: 0.04 us -> 1.29 us
  Pallas kernels: 10.6 us -> 9.58 us
  waiting for transfers between devices: 6.58 us -> 5.69 us
    unnamed x16, local copies, waits for them, and re-layouts: 0.04 us -> 1.29 us
    pallas_call x8, Pallas kernels: 10.6 us -> 9.58 us  [call(): pl.pallas_call(kernel, out_shape=[space(shape, dtype) for shape, dtype, s...]
    all_to_all x2, waiting for transfers between devices: 4.52 us -> 3.64 us  [exchange(): return lax.all_to_all(x, axis, split_axis=0, concat_axis=0, tiled=True)]
where the time goes in v10:
time: 66.9 us; the launch traced here: 66.5 us
  blocking collectives  32.2 us (48%)
  starting transfers between devices  17.7 us (26%)
  Pallas kernels  9.58 us (14%)
  waiting for transfers between devices  5.69 us (9%)
  local copies, waits for them, and re-layouts  1.29 us (2%)
    all_to_all x1, blocking collectives, exchange(): return lax.all_to_all(x, axis, split_axis=0, concat_axis=0, tiled=True)  20.2 us
    all_to_all x2, starting transfers between devices, exchange(): return lax.all_to_all(x, axis, split_axis=0, concat_axis=0, tiled=True)  14 us
    all_gather x1, blocking collectives, body(): whole = lax.all_gather(hidden_states, 'head', tiled=True)  11.9 us
    pallas_call x8, Pallas kernels, call(): pl.pallas_call(kernel, out_shape=[space(shape, dtype) for shape, dtype, s...  9.58 us
    ppermute x1, starting transfers between devices, body(): halo = lax.ppermute(halo, SEQ, [(i, i + 1) for i in range(devices - 1)])  3.68 us
    all_to_all x2, waiting for transfers between devices, exchange(): return lax.all_to_all(x, axis, split_axis=0, concat_axis=0, tiled=True)  3.64 us
    ppermute x1, waiting for transfers between devices, body(): halo = lax.ppermute(halo, SEQ, [(i, i + 1) for i in range(devices - 1)])  2.05 us
  transfers between devices with their start and end apart: 3, of which 3 were waited for; matrix products, arithmetic and copies ran while one was open for 0% of the time, Pallas kernels for 9%

profile of v10, /device:TPU:1, one launch (start us, length us, event | category | flops | bytes accessed | tf_op | source)
XLA Modules:
  0.0 66.5 jit_solution(17928568279354141045)
XLA Ops:
  0.0 0.0 copy-start.3
  0.0 0.0 copy-start
  0.0 11.9 %all_gather.3.x_ref = bf16[1024,384]{1,0:T(8,128)(2,1)S(1)} all-gather(bf16[256,384]{1,0:T(8,128)(2,1)} %param.7), channel_id=1, replica_groups=mesh['seq_0'=8,'seq_1'=8,'seq_2'=2,'head'=4] {'head'}, dimensions={0}, use_global_device_ids=true | all-gather | bytes 983040 | tf_op jit(solution)/shard_map/all_gather | solution.py:287
  12.0 0.0 copy-done.3
  12.0 0.0 copy-done
  12.0 1.1 %shard_map.74 = bf16[512,128]{1,0:T(8,128)(2,1)S(1)} custom-call(bf16[1024,384]{1,0:T(8,128)(2,1)S(1)} %all_gather.3.x_ref, bf16[96,1536]{1,0:T(8,128)(2,1)S(1)} %bitcast.9, bf16[1536,384]{1,0:T(8,128)(2,1)S(1)} %copy-done), custom_call_target="tpu_custom_call" | custom-call | flops 1500000000 | bytes 2260992 | tf_op jit(solution)/shard_map/pallas_call | solution.py:254
  13.0 20.2 %all_to_all.15.slices_ref = bf16[16,32,128]{2,1,0:T(8,128)(2,1)S(1)} all-to-all(bf16[16,32,128]{2,1,0:T(8,128)(2,1)S(1)} %bitcast.7), channel_id=1, replica_groups=mesh['seq_0'=8,'seq_1'=8,'seq_2'=2,'head'=4] {'seq_1','seq_2'}, dimensions={0} | all-to-all | bytes 262144 | tf_op jit(solution)/shard_map/all_to_all | solution.py:268
  33.2 0.0 copy-start.1
  33.2 0.7 %shard_map.75 = bf16[8,32,128]{2,1,0:T(8,128)(2,1)} custom-call(bf16[16,32,128]{2,1,0:T(8,128)(2,1)S(1)} %all_to_all.15.slices_ref), custom_call_target="tpu_custom_call" | custom-call | flops 600000000 | bytes 131072 | tf_op jit(solution)/shard_map/pallas_call | solution.py:254
  34.0 9.5 %all-to-all-start.1 = ((bf16[8,32,128]{2,1,0:T(8,128)(2,1)}), bf16[8,32,128]{2,1,0:T(8,128)(2,1)S(1)}, u32[]{:S(2)}, u32[]{:S(2)}) async-start(bf16[8,32,128]{2,1,0:T(8,128)(2,1)} %shard_map.75), calls=%async_computation.1 | async-start | bytes 131072 | tf_op jit(solution)/shard_map/all_to_all | solution.py:268
  43.4 0.0 copy-done.1
  43.5 0.0 copy-start.2
  43.5 1.3 %copy-done.2 = bf16[1536,384]{1,0:T(8,128)(2,1)S(1)} copy-done((bf16[1536,384]{1,0:T(8,128)(2,1)S(1)}, bf16[1536,384]{1,0:T(8,128)(2,1)}, u32[]{:S(2)}) %copy-start.2) | copy-done | bytes 1179672
  44.7 3.0 %shard_map.76 = (f32[192,384]{1,0:T(8,128)}, bf16[64,1152]{1,0:T(8,128)(2,1)}, bf16[64,768]{1,0:T(8,128)(2,1)}, bf16[256,384]{1,0:T(8,128)(2,1)}) custom-call(bf16[1024,384]{1,0:T(8,128)(2,1)S(1)} %all_gather.3.x_ref, bf16[1536,384]{1,0:T(8,128)(2,1)S(1)} %copy-done.1, bf16[1536,384]{1,0:T(8,128)(2,1)S(1)} %copy-done.2, bf16[1536,384]{1,0:T(8,128)(2,1)S(1)} %copy-done), custom_call_target="tpu_custom_call" | custom-call | flops 3900000000 | bytes 4325376 | tf_op jit(solution)/shard_map/pallas_call | solution.py:254
  47.8 2.4 %shard_map.77 = (f32[256,384]{1,0:T(8,128)S(1)}, bf16[256,1152]{1,0:T(8,128)(2,1)S(1)}) custom-call(bf16[1024,384]{1,0:T(8,128)(2,1)S(1)} %all_gather.3.x_ref, bf16[96,1536]{1,0:T(8,128)(2,1)} %bitcast.10, bf16[96,1536]{1,0:T(8,128)(2,1)} %bitcast.8, bf16[256,384]{1,0:T(8,128)(2,1)} %get-tuple-element.30.v_ref), custom_call_target="tpu_custom_call" | custom-call | flops 2200000000 | bytes 1572864 | tf_op jit(solution)/shard_map/pallas_call | solution.py:254
  50.2 0.7 %all-to-all-done.1.totals_ref = bf16[8,32,128]{2,1,0:T(8,128)(2,1)S(1)} async-done(((bf16[8,32,128]{2,1,0:T(8,128)(2,1)}), bf16[8,32,128]{2,1,0:T(8,128)(2,1)S(1)}, u32[]{:S(2)}, u32[]{:S(2)}) %all-to-all-start.1) | async-done | bytes 65568 | tf_op jit(solution)/shard_map/all_to_all | solution.py:268
  50.9 0.0 copy-start.7
  50.9 0.0 copy-start.6
  50.9 0.7 %shard_map.78 = bf16[16,32,128]{2,1,0:T(8,128)(2,1)} custom-call(s32[1]{0:T(128)} %bitcast.plane_ref, bf16[16,32,128]{2,1,0:T(8,128)(2,1)S(1)} %all_to_all.15.slices_ref, bf16[8,32,128]{2,1,0:T(8,128)(2,1)S(1)} %all-to-all-done.1.totals_ref), custom_call_target="tpu_custom_call" | custom-call | flops 1000000000 | bytes 196612 | tf_op jit(solution)/shard_map/pallas_call | solution.py:254
  51.6 4.5 %all-to-all-start.2 = ((bf16[16,32,128]{2,1,0:T(8,128)(2,1)}), bf16[16,32,128]{2,1,0:T(8,128)(2,1)S(1)}, u32[]{:S(2)}, u32[]{:S(2)}) async-start(bf16[16,32,128]{2,1,0:T(8,128)(2,1)} %shard_map.78), calls=%async_computation.2 | async-start | bytes 262144 | tf_op jit(solution)/shard_map/all_to_all | solution.py:268
  56.1 0.0 copy-done.7
  56.1 0.0 copy-start.4
  56.1 0.0 copy-start.5
  56.1 3.7 %collective-permute-start = (bf16[64,768]{1,0:T(8,128)(2,1)S(1)}, bf16[64,768]{1,0:T(8,128)(2,1)S(1)}, u32[]{:S(2)}, u32[]{:S(2)}) collective-permute-start(bf16[64,768]{1,0:T(8,128)(2,1)S(1)} %copy-done.7), channel_id=1, source_target_pairs={{0,4},{4,8},{8,12},{12,16},{16,20},{20,24},{24,28},{28,32},{32,36}... | collective-permute-start | bytes 294920 | tf_op jit(solution)/shard_map/ppermute | solution.py:335
  59.8 2.1 %collective-permute-done.halo_ref = bf16[64,768]{1,0:T(8,128)(2,1)S(1)} collective-permute-done((bf16[64,768]{1,0:T(8,128)(2,1)S(1)}, bf16[64,768]{1,0:T(8,128)(2,1)S(1)}, u32[]{:S(2)}, u32[]{:S(2)}) %collective-permute-start) | collective-permute-done | bytes 98336 | tf_op jit(solution)/shard_map/ppermute | solution.py:335
  61.9 0.0 copy-done.6
  61.9 0.5 shard_map.79.early_ref
  62.4 3.0 %all-to-all-done.2 = bf16[16,32,128]{2,1,0:T(8,128)(2,1)S(1)} async-done(((bf16[16,32,128]{2,1,0:T(8,128)(2,1)}), bf16[16,32,128]{2,1,0:T(8,128)(2,1)S(1)}, u32[]{:S(2)}, u32[]{:S(2)}) %all-to-all-start.2) | async-done | bytes 131104 | tf_op jit(solution)/shard_map/all_to_all | solution.py:268
  65.3 0.0 copy-done.4
  65.3 0.0 copy-done.5
  65.3 1.1 %shard_map.80 = bf16[256,384]{1,0:T(8,128)(2,1)} custom-call(bf16[512,128]{1,0:T(8,128)(2,1)S(1)} %bitcast.6, bf16[256,1152]{1,0:T(8,128)(2,1)S(1)} %get-tuple-element.34.phi_ref, f32[256,384]{1,0:T(8,128)S(1)} %get-tuple-element.35.intra_ref, f32[64,384]{1,0:T(8,128)S(1)} %shard_map.79.early_ref, f32[192,384]{1,0:T(8,128)S(1)} %copy-done.5, ...), custom_call_target="tpu_custom_call" | custom-call | flops 1400000000 | bytes 1574400 | tf_op jit(solution)/shard_map/pallas_call | solution.py:254
  (1 shorter events, 0.0 us)
Async XLA Ops:
  0.0 12.0 %copy-start.3 = (bf16[1536,96]{0,1:T(8,128)(2,1)S(1)}, bf16[1536,96]{0,1:T(8,128)(2,1)}, u32[]{:S(2)}) copy-start(bf16[1536,96]{0,1:T(8,128)(2,1)} %param.9) | copy-start | bytes 884740
  0.0 12.0 %copy-start = (bf16[1536,384]{1,0:T(8,128)(2,1)S(1)}, bf16[1536,384]{1,0:T(8,128)(2,1)}, u32[]{:S(2)}) copy-start(bf16[1536,384]{1,0:T(8,128)(2,1)} %wv_ref.3) | copy-start | bytes 3538948
  33.2 10.2 %copy-start.1 = (bf16[1536,384]{1,0:T(8,128)(2,1)S(1)}, bf16[1536,384]{1,0:T(8,128)(2,1)}, u32[]{:S(2)}) copy-start(bf16[1536,384]{1,0:T(8,128)(2,1)} %wq_ref.1) | copy-start | bytes 3538948
  34.0 16.9 %all-to-all-start.1 = ((bf16[8,32,128]{2,1,0:T(8,128)(2,1)}), bf16[8,32,128]{2,1,0:T(8,128)(2,1)S(1)}, u32[]{:S(2)}, u32[]{:S(2)}) async-start(bf16[8,32,128]{2,1,0:T(8,128)(2,1)} %shard_map.75), calls=%async_computation.1 | async-start | bytes 131072 | tf_op jit(solution)/shard_map/all_to_all | solution.py:268
  43.5 1.3 %copy-start.2 = (bf16[1536,384]{1,0:T(8,128)(2,1)S(1)}, bf16[1536,384]{1,0:T(8,128)(2,1)}, u32[]{:S(2)}) copy-start(bf16[1536,384]{1,0:T(8,128)(2,1)} %wk_ref.1) | copy-start | bytes 3538948
  50.9 5.2 %copy-start.7 = (bf16[64,768]{1,0:T(8,128)(2,1)S(1)}, bf16[64,768]{1,0:T(8,128)(2,1)}, u32[]{:S(2)}) copy-start(bf16[64,768]{1,0:T(8,128)(2,1)} %get-tuple-element.38) | copy-start | bytes 294916
  50.9 11.0 %copy-start.6 = (bf16[64,1152]{1,0:T(8,128)(2,1)S(1)}, bf16[64,1152]{1,0:T(8,128)(2,1)}, u32[]{:S(2)}) copy-start(bf16[64,1152]{1,0:T(8,128)(2,1)} %get-tuple-element.37.head_ref) | copy-start | bytes 442372
  51.6 13.7 %all-to-all-start.2 = ((bf16[16,32,128]{2,1,0:T(8,128)(2,1)}), bf16[16,32,128]{2,1,0:T(8,128)(2,1)S(1)}, u32[]{:S(2)}, u32[]{:S(2)}) async-start(bf16[16,32,128]{2,1,0:T(8,128)(2,1)} %shard_map.78), calls=%async_computation.2 | async-start | bytes 262144 | tf_op jit(solution)/shard_map/all_to_all | solution.py:268
  56.1 9.2 %copy-start.4 = (f32[384]{0:T(512)S(1)}, f32[384]{0:T(512)}, u32[]{:S(2)}) copy-start(f32[384]{0:T(512)} %gain_ref.1) | copy-start | bytes 4612
  56.1 9.2 %copy-start.5 = (f32[192,384]{1,0:T(8,128)S(1)}, f32[192,384]{1,0:T(8,128)}, u32[]{:S(2)}) copy-start(f32[192,384]{1,0:T(8,128)} %get-tuple-element.39.window_ref) | copy-start | bytes 884740
  56.1 5.7 %collective-permute-start = (bf16[64,768]{1,0:T(8,128)(2,1)S(1)}, bf16[64,768]{1,0:T(8,128)(2,1)S(1)}, u32[]{:S(2)}, u32[]{:S(2)}) collective-permute-start(bf16[64,768]{1,0:T(8,128)(2,1)S(1)} %copy-done.7), channel_id=1, source_target_pairs={{0,4},{4,8},{8,12},{12,16},{16,20},{20,24},{24,28},{28,32},{32,36}... | collective-permute-start | bytes 294920 | tf_op jit(solution)/shard_map/ppermute | solution.py:335

commit v11 on v10

--- a/solution.py
+++ b/solution.py
@@ -68,7 +68,9 @@
     return lax.broadcasted_iota(jnp.int32, shape, len(shape) - 1) < HV
 
 
-def mean_kernel(out_ref):
+def first_kernel(x_ref, copies_ref, out_ref):
+    for c in range(copies_ref.shape[0]):
+        copies_ref[c] = x_ref[...]
     i = lax.broadcasted_iota(jnp.int32, out_ref.shape, 0) % 128
     j = lax.broadcasted_iota(jnp.int32, out_ref.shape, 1)
     out_ref[...] = jnp.where((i < HV) == (j < HV), 1.0 / HV, 0.0).astype(BF16)
@@ -282,9 +284,14 @@
 
     vmem, hbm, smem = pltpu.VMEM, pltpu.HBM, pltpu.SMEM
 
-    (mean,) = call(mean_kernel, [((256, 128), BF16, vmem)], [], 200)
-    hidden_states, mean, plane, first = lax.optimization_barrier((hidden_states, mean, plane, first))
-    whole = lax.all_gather(hidden_states, "head", tiled=True)
+    copies, mean = call(
+        first_kernel,
+        [((chunks, *hidden_states.shape), BF16, vmem), ((256, 128), BF16, vmem)],
+        [(hidden_states, hbm)],
+        1000,
+    )
+    copies, mean, plane, first = lax.optimization_barrier((copies, mean, plane, first))
+    whole = exchange(copies, "head").reshape(chunks * rows, hidden_states.shape[1])
     (state,) = call(
         functools.partial(state_kernel, rows, chunks),
         [((held, 128), BF16, vmem)],

time: 66.9 us -> 70.4 us (1.052)
  blocking collectives: 32.2 us -> 34.1 us
  Pallas kernels: 9.58 us -> 10.6 us
    all_to_all x1 -> x2, blocking collectives: 20.2 us -> 34.1 us  [exchange(): return lax.all_to_all(x, axis, split_axis=0, concat_axis=0, tiled=True)]
    all_gather x1 -> x0, blocking collectives: 11.9 us -> none  [body(): whole = lax.all_gather(hidden_states, 'head', tiled=True)]
    pallas_call x8, Pallas kernels: 9.58 us -> 10.6 us  [call(): pl.pallas_call(kernel, out_shape=[space(shape, dtype) for shape, dtype, s...]
where the time goes in v11:
time: 70.4 us; the launch traced here: 70 us
  blocking collectives  34.1 us (48%)
  starting transfers between devices  18.2 us (26%)
  Pallas kernels  10.6 us (15%)
  waiting for transfers between devices  5.69 us (8%)
  local copies, waits for them, and re-layouts  1.3 us (2%)
    all_to_all x2, blocking collectives, exchange(): return lax.all_to_all(x, axis, split_axis=0, concat_axis=0, tiled=True)  34.1 us
    all_to_all x2, starting transfers between devices, exchange(): return lax.all_to_all(x, axis, split_axis=0, concat_axis=0, tiled=True)  14.5 us
    pallas_call x8, Pallas kernels, call(): pl.pallas_call(kernel, out_shape=[space(shape, dtype) for shape, dtype, s...  10.6 us
    ppermute x1, starting transfers between devices, body(): halo = lax.ppermute(halo, SEQ, [(i, i + 1) for i in range(devices - 1)])  3.68 us
    all_to_all x2, waiting for transfers between devices, exchange(): return lax.all_to_all(x, axis, split_axis=0, concat_axis=0, tiled=True)  3.64 us
    ppermute x1, waiting for transfers between devices, body(): halo = lax.ppermute(halo, SEQ, [(i, i + 1) for i in range(devices - 1)])  2.05 us
  transfers between devices with their start and end apart: 3, of which 3 were waited for; matrix products, arithmetic and copies ran while one was open for 0% of the time, Pallas kernels for 9%

profile of v11, /device:TPU:1, one launch (start us, length us, event | category | flops | bytes accessed | tf_op | source)
XLA Modules:
  0.0 70.0 jit_solution(5113360129260905884)
XLA Ops:
  0.0 1.0 %shard_map.73 = (bf16[4,256,384]{2,1,0:T(8,128)(2,1)S(1)}, bf16[256,128]{1,0:T(8,128)(2,1)S(1)}) custom-call(bf16[256,384]{1,0:T(8,128)(2,1)} %x_ref.1), custom_call_target="tpu_custom_call" | custom-call | flops 1000000000 | bytes 196608 | tf_op jit(solution)/shard_map/pallas_call | solution.py:256
  1.0 0.0 copy-start
  1.0 0.0 copy-start.3
  1.0 13.1 %all_to_all.20 = bf16[4,256,384]{2,1,0:T(8,128)(2,1)S(1)} all-to-all(bf16[4,256,384]{2,1,0:T(8,128)(2,1)S(1)} %get-tuple-element.28), channel_id=1, replica_groups=mesh['seq_0'=8,'seq_1'=8,'seq_2'=2,'head'=4] {'head'}, dimensions={0} | all-to-all | bytes 1572864 | tf_op jit(solution)/shard_map/all_to_all | solution.py:270
  14.1 0.0 copy-done
  14.1 0.0 copy-done.3
  14.1 1.1 %shard_map.74 = bf16[512,128]{1,0:T(8,128)(2,1)S(1)} custom-call(bf16[1024,384]{1,0:T(8,128)(2,1)S(1)} %bitcast.7, bf16[96,1536]{1,0:T(8,128)(2,1)S(1)} %bitcast.13, bf16[1536,384]{1,0:T(8,128)(2,1)S(1)} %copy-done), custom_call_target="tpu_custom_call" | custom-call | flops 1500000000 | bytes 2260992 | tf_op jit(solution)/shard_map/pallas_call | solution.py:256
  15.2 21.0 %all_to_all.21.slices_ref = bf16[16,32,128]{2,1,0:T(8,128)(2,1)S(1)} all-to-all(bf16[16,32,128]{2,1,0:T(8,128)(2,1)S(1)} %bitcast.11), channel_id=1, replica_groups=mesh['seq_0'=8,'seq_1'=8,'seq_2'=2,'head'=4] {'seq_1','seq_2'}, dimensions={0} | all-to-all | bytes 262144 | tf_op jit(solution)/shard_map/all_to_all | solution.py:270
  36.2 0.0 copy-start.1
  36.2 0.7 %shard_map.75 = bf16[8,32,128]{2,1,0:T(8,128)(2,1)} custom-call(bf16[16,32,128]{2,1,0:T(8,128)(2,1)S(1)} %all_to_all.21.slices_ref), custom_call_target="tpu_custom_call" | custom-call | flops 600000000 | bytes 131072 | tf_op jit(solution)/shard_map/pallas_call | solution.py:256
  36.9 10.0 %all-to-all-start.2 = ((bf16[8,32,128]{2,1,0:T(8,128)(2,1)}), bf16[8,32,128]{2,1,0:T(8,128)(2,1)S(1)}, u32[]{:S(2)}, u32[]{:S(2)}) async-start(bf16[8,32,128]{2,1,0:T(8,128)(2,1)} %shard_map.75), calls=%async_computation.2 | async-start | bytes 131072 | tf_op jit(solution)/shard_map/all_to_all | solution.py:270
  47.0 0.0 copy-done.1
  47.0 0.0 copy-start.2
  47.0 1.3 %copy-done.2 = bf16[1536,384]{1,0:T(8,128)(2,1)S(1)} copy-done((bf16[1536,384]{1,0:T(8,128)(2,1)S(1)}, bf16[1536,384]{1,0:T(8,128)(2,1)}, u32[]{:S(2)}) %copy-start.2) | copy-done | bytes 1179672
  48.2 3.0 %shard_map.76 = (f32[192,384]{1,0:T(8,128)}, bf16[64,1152]{1,0:T(8,128)(2,1)}, bf16[64,768]{1,0:T(8,128)(2,1)}, bf16[256,384]{1,0:T(8,128)(2,1)}) custom-call(bf16[1024,384]{1,0:T(8,128)(2,1)S(1)} %bitcast.8, bf16[1536,384]{1,0:T(8,128)(2,1)S(1)} %copy-done.1, bf16[1536,384]{1,0:T(8,128)(2,1)S(1)} %copy-done.2, bf16[1536,384]{1,0:T(8,128)(2,1)S(1)} %copy-done), custom_call_target="tpu_custom_call" | custom-call | flops 3900000000 | bytes 4325376 | tf_op jit(solution)/shard_map/pallas_call | solution.py:256
  51.3 2.4 %shard_map.77 = (f32[256,384]{1,0:T(8,128)S(1)}, bf16[256,1152]{1,0:T(8,128)(2,1)S(1)}) custom-call(bf16[1024,384]{1,0:T(8,128)(2,1)S(1)} %bitcast.9, bf16[96,1536]{1,0:T(8,128)(2,1)} %bitcast.14, bf16[96,1536]{1,0:T(8,128)(2,1)} %bitcast.12, bf16[256,384]{1,0:T(8,128)(2,1)} %get-tuple-element.34.v_ref), custom_call_target="tpu_custom_call" | custom-call | flops 2200000000 | bytes 1572864 | tf_op jit(solution)/shard_map/pallas_call | solution.py:256
  53.7 0.7 all-to-all-done.2.totals_ref
  54.4 0.0 copy-start.7
  54.4 0.0 copy-start.6
  54.4 0.7 %shard_map.78 = bf16[16,32,128]{2,1,0:T(8,128)(2,1)} custom-call(s32[1]{0:T(128)} %bitcast.plane_ref, bf16[16,32,128]{2,1,0:T(8,128)(2,1)S(1)} %all_to_all.21.slices_ref, bf16[8,32,128]{2,1,0:T(8,128)(2,1)S(1)} %all-to-all-done.2.totals_ref), custom_call_target="tpu_custom_call" | custom-call | flops 1000000000 | bytes 196612 | tf_op jit(solution)/shard_map/pallas_call | solution.py:256
  55.1 4.5 %all-to-all-start.3 = ((bf16[16,32,128]{2,1,0:T(8,128)(2,1)}), bf16[16,32,128]{2,1,0:T(8,128)(2,1)S(1)}, u32[]{:S(2)}, u32[]{:S(2)}) async-start(bf16[16,32,128]{2,1,0:T(8,128)(2,1)} %shard_map.78), calls=%async_computation.3 | async-start | bytes 262144 | tf_op jit(solution)/shard_map/all_to_all | solution.py:270
  59.6 0.0 copy-done.7
  59.6 0.0 copy-start.4
  59.6 0.0 copy-start.5
  59.6 3.7 %collective-permute-start = (bf16[64,768]{1,0:T(8,128)(2,1)S(1)}, bf16[64,768]{1,0:T(8,128)(2,1)S(1)}, u32[]{:S(2)}, u32[]{:S(2)}) collective-permute-start(bf16[64,768]{1,0:T(8,128)(2,1)S(1)} %copy-done.7), channel_id=1, source_target_pairs={{0,4},{4,8},{8,12},{12,16},{16,20},{20,24},{24,28},{28,32},{32,36}... | collective-permute-start | bytes 294920 | tf_op jit(solution)/shard_map/ppermute | solution.py:342
  63.3 2.1 %collective-permute-done.halo_ref = bf16[64,768]{1,0:T(8,128)(2,1)S(1)} collective-permute-done((bf16[64,768]{1,0:T(8,128)(2,1)S(1)}, bf16[64,768]{1,0:T(8,128)(2,1)S(1)}, u32[]{:S(2)}, u32[]{:S(2)}) %collective-permute-start) | collective-permute-done | bytes 98336 | tf_op jit(solution)/shard_map/ppermute | solution.py:342
  65.4 0.0 copy-done.6
  65.4 0.5 shard_map.79.early_ref
  65.9 3.0 %all-to-all-done.3 = bf16[16,32,128]{2,1,0:T(8,128)(2,1)S(1)} async-done(((bf16[16,32,128]{2,1,0:T(8,128)(2,1)}), bf16[16,32,128]{2,1,0:T(8,128)(2,1)S(1)}, u32[]{:S(2)}, u32[]{:S(2)}) %all-to-all-start.3) | async-done | bytes 131104 | tf_op jit(solution)/shard_map/all_to_all | solution.py:270
  68.8 0.0 copy-done.4
  68.8 0.0 copy-done.5
  68.9 1.1 %shard_map.80 = bf16[256,384]{1,0:T(8,128)(2,1)} custom-call(bf16[512,128]{1,0:T(8,128)(2,1)S(1)} %bitcast.10, bf16[256,1152]{1,0:T(8,128)(2,1)S(1)} %get-tuple-element.38.phi_ref, f32[256,384]{1,0:T(8,128)S(1)} %get-tuple-element.39.intra_ref, f32[64,384]{1,0:T(8,128)S(1)} %shard_map.79.early_ref, f32[192,384]{1,0:T(8,128)S(1)} %copy-done.5, ...), custom_call_target="tpu_custom_call" | custom-call | flops 1400000000 | bytes 1574400 | tf_op jit(solution)/shard_map/pallas_call | solution.py:256
Async XLA Ops:
  1.0 13.1 %copy-start = (bf16[1536,384]{1,0:T(8,128)(2,1)S(1)}, bf16[1536,384]{1,0:T(8,128)(2,1)}, u32[]{:S(2)}) copy-start(bf16[1536,384]{1,0:T(8,128)(2,1)} %wv_ref.3) | copy-start | bytes 3538948
  1.0 13.1 %copy-start.3 = (bf16[1536,96]{0,1:T(8,128)(2,1)S(1)}, bf16[1536,96]{0,1:T(8,128)(2,1)}, u32[]{:S(2)}) copy-start(bf16[1536,96]{0,1:T(8,128)(2,1)} %param.9) | copy-start | bytes 884740
  36.2 10.8 %copy-start.1 = (bf16[1536,384]{1,0:T(8,128)(2,1)S(1)}, bf16[1536,384]{1,0:T(8,128)(2,1)}, u32[]{:S(2)}) copy-start(bf16[1536,384]{1,0:T(8,128)(2,1)} %wq_ref.1) | copy-start | bytes 3538948
  36.9 17.5 %all-to-all-start.2 = ((bf16[8,32,128]{2,1,0:T(8,128)(2,1)}), bf16[8,32,128]{2,1,0:T(8,128)(2,1)S(1)}, u32[]{:S(2)}, u32[]{:S(2)}) async-start(bf16[8,32,128]{2,1,0:T(8,128)(2,1)} %shard_map.75), calls=%async_computation.2 | async-start | bytes 131072 | tf_op jit(solution)/shard_map/all_to_all | solution.py:270
  47.0 1.3 %copy-start.2 = (bf16[1536,384]{1,0:T(8,128)(2,1)S(1)}, bf16[1536,384]{1,0:T(8,128)(2,1)}, u32[]{:S(2)}) copy-start(bf16[1536,384]{1,0:T(8,128)(2,1)} %wk_ref.1) | copy-start | bytes 3538948
  54.4 5.2 %copy-start.7 = (bf16[64,768]{1,0:T(8,128)(2,1)S(1)}, bf16[64,768]{1,0:T(8,128)(2,1)}, u32[]{:S(2)}) copy-start(bf16[64,768]{1,0:T(8,128)(2,1)} %get-tuple-element.42) | copy-start | bytes 294916
  54.4 11.0 %copy-start.6 = (bf16[64,1152]{1,0:T(8,128)(2,1)S(1)}, bf16[64,1152]{1,0:T(8,128)(2,1)}, u32[]{:S(2)}) copy-start(bf16[64,1152]{1,0:T(8,128)(2,1)} %get-tuple-element.41.head_ref) | copy-start | bytes 442372
  55.1 13.7 %all-to-all-start.3 = ((bf16[16,32,128]{2,1,0:T(8,128)(2,1)}), bf16[16,32,128]{2,1,0:T(8,128)(2,1)S(1)}, u32[]{:S(2)}, u32[]{:S(2)}) async-start(bf16[16,32,128]{2,1,0:T(8,128)(2,1)} %shard_map.78), calls=%async_computation.3 | async-start | bytes 262144 | tf_op jit(solution)/shard_map/all_to_all | solution.py:270
  59.6 9.2 %copy-start.4 = (f32[384]{0:T(512)S(1)}, f32[384]{0:T(512)}, u32[]{:S(2)}) copy-start(f32[384]{0:T(512)} %gain_ref.1) | copy-start | bytes 4612
  59.6 9.2 %copy-start.5 = (f32[192,384]{1,0:T(8,128)S(1)}, f32[192,384]{1,0:T(8,128)}, u32[]{:S(2)}) copy-start(f32[192,384]{1,0:T(8,128)} %get-tuple-element.43.window_ref) | copy-start | bytes 884740
  59.6 5.7 %collective-permute-start = (bf16[64,768]{1,0:T(8,128)(2,1)S(1)}, bf16[64,768]{1,0:T(8,128)(2,1)S(1)}, u32[]{:S(2)}, u32[]{:S(2)}) collective-permute-start(bf16[64,768]{1,0:T(8,128)(2,1)S(1)} %copy-done.7), channel_id=1, source_target_pairs={{0,4},{4,8},{8,12},{12,16},{16,20},{20,24},{24,28},{28,32},{32,36}... | collective-permute-start | bytes 294920 | tf_op jit(solution)/shard_map/ppermute | solution.py:342

commit v12 on v10

--- a/solution.py
+++ b/solution.py
@@ -119,24 +119,41 @@
     return (col <= row + WIN) & (col > row), col
 
 
-def window_kernel(rows, chunks, x_ref, wq_ref, wk_ref, wv_ref, out_ref, head_ref, halo_ref, v_ref):
-    v_ref[...] = dot(whole_rows(x_ref, rows, chunks), wv_ref[...]).astype(BF16)
-    keys = project(x_ref, wk_ref, rows, chunks).astype(BF16)
-    queries = project(x_ref, wq_ref, rows, chunks).astype(BF16)
-    width = keys.shape[1]
-    halo_ref[:, :width] = keys[rows - WIN :]
+def window_kernel(
+    rows, chunks, x_ref, wq_hbm, wk_ref, wv_ref, out_hbm, head_hbm, halo_hbm, v_hbm,
+    wq_ref, out_ref, head_ref, halo_ref, v_ref, key_ref, sem
+):
+    load = pltpu.make_async_copy(wq_hbm, wq_ref, sem.at[0])
+    load.start()
+    x = whole_rows(x_ref, rows, chunks)
+    width = key_ref.shape[1]
+    v_ref[...] = dot(x, wv_ref[...]).astype(BF16)
+    stores = [pltpu.make_async_copy(v_ref, v_hbm, sem.at[1])]
+    stores[0].start()
+    key_ref[...] = dot(x, wk_ref[...]).astype(BF16)
+    halo_ref[:, :width] = key_ref[rows - WIN :, :]
     halo_ref[:, width:] = v_ref[rows - WIN :, :]
+    stores.append(pltpu.make_async_copy(halo_ref, halo_hbm, sem.at[2]))
+    stores[1].start()
+    load.wait()
+    queries = dot(x, wq_ref[...]).astype(BF16)
     head_ref[:, :width] = queries[:WIN]
-    head_ref[:, width : 2 * width] = keys[:WIN]
+    head_ref[:, width : 2 * width] = key_ref[:WIN, :]
     head_ref[:, 2 * width :] = v_ref[:WIN, :]
+    stores.append(pltpu.make_async_copy(head_ref, head_hbm, sem.at[3]))
+    stores[2].start()
     band, _ = window_band()
     places = [(t, p) for t in range(1, rows // WIN) for p in range(width // 128)]
     tiles = []
     for t, p in places:
         at, seen = slice(128 * p, 128 * p + 128), slice(WIN * (t - 1), WIN * (t + 1))
-        tiles.append((queries[WIN * t : WIN * (t + 1), at], keys[seen, at], v_ref[seen, at]))
+        tiles.append((queries[WIN * t : WIN * (t + 1), at], key_ref[seen, at], v_ref[seen, at]))
     for (t, p), out in zip(places, window_tiles(tiles, band)):
         out_ref[WIN * (t - 1) : WIN * t, 128 * p : 128 * p + 128] = out
+    stores.append(pltpu.make_async_copy(out_ref, out_hbm, sem.at[4]))
+    stores[3].start()
+    for store in stores:
+        store.wait()
 
 
 def first_window_kernel(first_ref, head_ref, halo_ref, out_ref):
@@ -311,8 +328,17 @@
             ((WIN, 2 * width), BF16, hbm),
             ((rows, width), BF16, hbm),
         ],
-        [(whole, vmem), (window_q, vmem), (window_k, vmem), (value_w, vmem)],
+        [(whole, vmem), (window_q, hbm), (window_k, vmem), (value_w, vmem)],
         3900,
+        scratch=[
+            pltpu.VMEM((model, width), BF16),
+            pltpu.VMEM((rows - WIN, width), F32),
+            pltpu.VMEM((WIN, 3 * width), BF16),
+            pltpu.VMEM((WIN, 2 * width), BF16),
+            pltpu.VMEM((rows, width), BF16),
+            pltpu.VMEM((rows, width), BF16),
+            pltpu.SemaphoreType.DMA((5,)),
+        ],
     )
     intra, phi = call(
         functools.partial(intra_kernel, rows, chunks),

time: 66.9 us -> 66.9 us (level)
  local copies, waits for them, and re-layouts: 1.29 us -> 0.03 us
  Pallas kernels: 9.58 us -> 10.7 us
    unnamed x16 -> x14, local copies, waits for them, and re-layouts: 1.29 us -> 0.03 us
    pallas_call x8, Pallas kernels: 9.58 us -> 10.7 us  [call(): pl.pallas_call(kernel, out_shape=[space(shape, dtype) for shape, dtype, s...]
  transfers between devices with their start and end apart: 3 -> 3, of which waited for: 3 -> 3; matrix products, arithmetic and copies ran while one was open for 0% -> 0% of each run, Pallas kernels for 9% -> 11%
where the time goes in v12:
time: 66.9 us; the launch traced here: 66.5 us
  blocking collectives  32.2 us (48%)
  starting transfers between devices  17.7 us (26%)
  Pallas kernels  10.7 us (16%)
  waiting for transfers between devices  5.81 us (9%)
    all_to_all x1, blocking collectives, exchange(): return lax.all_to_all(x, axis, split_axis=0, concat_axis=0, tiled=True)  20.2 us
    all_to_all x2, starting transfers between devices, exchange(): return lax.all_to_all(x, axis, split_axis=0, concat_axis=0, tiled=True)  14 us
    all_gather x1, blocking collectives, body(): whole = lax.all_gather(hidden_states, 'head', tiled=True)  11.9 us
    pallas_call x8, Pallas kernels, call(): pl.pallas_call(kernel, out_shape=[space(shape, dtype) for shape, dtype, s...  10.7 us
    all_to_all x2, waiting for transfers between devices, exchange(): return lax.all_to_all(x, axis, split_axis=0, concat_axis=0, tiled=True)  3.76 us
    ppermute x1, starting transfers between devices, body(): halo = lax.ppermute(halo, SEQ, [(i, i + 1) for i in range(devices - 1)])  3.68 us
    ppermute x1, waiting for transfers between devices, body(): halo = lax.ppermute(halo, SEQ, [(i, i + 1) for i in range(devices - 1)])  2.05 us
  transfers between devices with their start and end apart: 3, of which 3 were waited for; matrix products, arithmetic and copies ran while one was open for 0% of the time, Pallas kernels for 11%

profile of v12, /device:TPU:1, one launch (start us, length us, event | category | flops | bytes accessed | tf_op | source)
XLA Modules:
  0.0 66.5 jit_solution(17097791919035801137)
XLA Ops:
  0.0 0.0 copy-start.2
  0.0 0.0 copy-start
  0.0 11.9 %all_gather.3.x_ref = bf16[1024,384]{1,0:T(8,128)(2,1)S(1)} all-gather(bf16[256,384]{1,0:T(8,128)(2,1)} %param.7), channel_id=1, replica_groups=mesh['seq_0'=8,'seq_1'=8,'seq_2'=2,'head'=4] {'head'}, dimensions={0}, use_global_device_ids=true | all-gather | bytes 983040 | tf_op jit(solution)/shard_map/all_gather | solution.py:304
  12.0 0.0 copy-done.2
  12.0 0.0 copy-done
  12.0 1.1 %shard_map.74 = bf16[512,128]{1,0:T(8,128)(2,1)S(1)} custom-call(bf16[1024,384]{1,0:T(8,128)(2,1)S(1)} %all_gather.3.x_ref, bf16[96,1536]{1,0:T(8,128)(2,1)S(1)} %bitcast.9, bf16[1536,384]{1,0:T(8,128)(2,1)S(1)} %copy-done), custom_call_target="tpu_custom_call" | custom-call | flops 1500000000 | bytes 2260992 | tf_op jit(solution)/shard_map/pallas_call | solution.py:271
  13.0 20.2 %all_to_all.15.slices_ref = bf16[16,32,128]{2,1,0:T(8,128)(2,1)S(1)} all-to-all(bf16[16,32,128]{2,1,0:T(8,128)(2,1)S(1)} %bitcast.7), channel_id=1, replica_groups=mesh['seq_0'=8,'seq_1'=8,'seq_2'=2,'head'=4] {'seq_1','seq_2'}, dimensions={0} | all-to-all | bytes 262144 | tf_op jit(solution)/shard_map/all_to_all | solution.py:285
  33.2 0.0 copy-start.1
  33.2 0.7 %shard_map.75 = bf16[8,32,128]{2,1,0:T(8,128)(2,1)} custom-call(bf16[16,32,128]{2,1,0:T(8,128)(2,1)S(1)} %all_to_all.15.slices_ref), custom_call_target="tpu_custom_call" | custom-call | flops 600000000 | bytes 131072 | tf_op jit(solution)/shard_map/pallas_call | solution.py:271
  34.0 9.5 %all-to-all-start.1 = ((bf16[8,32,128]{2,1,0:T(8,128)(2,1)}), bf16[8,32,128]{2,1,0:T(8,128)(2,1)S(1)}, u32[]{:S(2)}, u32[]{:S(2)}) async-start(bf16[8,32,128]{2,1,0:T(8,128)(2,1)} %shard_map.75), calls=%async_computation.1 | async-start | bytes 131072 | tf_op jit(solution)/shard_map/all_to_all | solution.py:285
  43.5 0.0 copy-done.1
  43.5 4.2 %shard_map.76 = (f32[192,384]{1,0:T(8,128)}, bf16[64,1152]{1,0:T(8,128)(2,1)}, bf16[64,768]{1,0:T(8,128)(2,1)}, bf16[256,384]{1,0:T(8,128)(2,1)}) custom-call(bf16[1024,384]{1,0:T(8,128)(2,1)S(1)} %all_gather.3.x_ref, bf16[1536,384]{1,0:T(8,128)(2,1)} %wq_hbm.1, bf16[1536,384]{1,0:T(8,128)(2,1)S(1)} %copy-done.1, bf16[1536,384]{1,0:T(8,128)(2,1)S(1)} %copy-done), custom_call_target="tpu_custom_call" | custom-call | flops 3900000000 | bytes 4325376 | tf_op jit(solution)/shard_map/pallas_call | solution.py:271
  47.7 2.4 %shard_map.77 = (f32[256,384]{1,0:T(8,128)S(1)}, bf16[256,1152]{1,0:T(8,128)(2,1)S(1)}) custom-call(bf16[1024,384]{1,0:T(8,128)(2,1)S(1)} %all_gather.3.x_ref, bf16[96,1536]{1,0:T(8,128)(2,1)} %bitcast.10, bf16[96,1536]{1,0:T(8,128)(2,1)} %bitcast.8, bf16[256,384]{1,0:T(8,128)(2,1)} %get-tuple-element.30.v_ref), custom_call_target="tpu_custom_call" | custom-call | flops 2200000000 | bytes 1572864 | tf_op jit(solution)/shard_map/pallas_call | solution.py:271
  50.1 0.8 %all-to-all-done.1.totals_ref = bf16[8,32,128]{2,1,0:T(8,128)(2,1)S(1)} async-done(((bf16[8,32,128]{2,1,0:T(8,128)(2,1)}), bf16[8,32,128]{2,1,0:T(8,128)(2,1)S(1)}, u32[]{:S(2)}, u32[]{:S(2)}) %all-to-all-start.1) | async-done | bytes 65568 | tf_op jit(solution)/shard_map/all_to_all | solution.py:285
  50.9 0.0 copy-start.6
  50.9 0.0 copy-start.5
  50.9 0.7 %shard_map.78 = bf16[16,32,128]{2,1,0:T(8,128)(2,1)} custom-call(s32[1]{0:T(128)} %bitcast.plane_ref, bf16[16,32,128]{2,1,0:T(8,128)(2,1)S(1)} %all_to_all.15.slices_ref, bf16[8,32,128]{2,1,0:T(8,128)(2,1)S(1)} %all-to-all-done.1.totals_ref), custom_call_target="tpu_custom_call" | custom-call | flops 1000000000 | bytes 196612 | tf_op jit(solution)/shard_map/pallas_call | solution.py:271
  51.6 4.5 %all-to-all-start.2 = ((bf16[16,32,128]{2,1,0:T(8,128)(2,1)}), bf16[16,32,128]{2,1,0:T(8,128)(2,1)S(1)}, u32[]{:S(2)}, u32[]{:S(2)}) async-start(bf16[16,32,128]{2,1,0:T(8,128)(2,1)} %shard_map.78), calls=%async_computation.2 | async-start | bytes 262144 | tf_op jit(solution)/shard_map/all_to_all | solution.py:285
  56.1 0.0 copy-done.6
  56.1 0.0 copy-start.3
  56.1 0.0 copy-start.4
  56.1 3.7 %collective-permute-start = (bf16[64,768]{1,0:T(8,128)(2,1)S(1)}, bf16[64,768]{1,0:T(8,128)(2,1)S(1)}, u32[]{:S(2)}, u32[]{:S(2)}) collective-permute-start(bf16[64,768]{1,0:T(8,128)(2,1)S(1)} %copy-done.6), channel_id=1, source_target_pairs={{0,4},{4,8},{8,12},{12,16},{16,20},{20,24},{24,28},{28,32},{32,36}... | collective-permute-start | bytes 294920 | tf_op jit(solution)/shard_map/ppermute | solution.py:361
  59.8 2.1 %collective-permute-done.halo_ref = bf16[64,768]{1,0:T(8,128)(2,1)S(1)} collective-permute-done((bf16[64,768]{1,0:T(8,128)(2,1)S(1)}, bf16[64,768]{1,0:T(8,128)(2,1)S(1)}, u32[]{:S(2)}, u32[]{:S(2)}) %collective-permute-start) | collective-permute-done | bytes 98336 | tf_op jit(solution)/shard_map/ppermute | solution.py:361
  61.9 0.0 copy-done.5
  61.9 0.5 shard_map.79.early_ref
  62.4 3.0 %all-to-all-done.2 = bf16[16,32,128]{2,1,0:T(8,128)(2,1)S(1)} async-done(((bf16[16,32,128]{2,1,0:T(8,128)(2,1)}), bf16[16,32,128]{2,1,0:T(8,128)(2,1)S(1)}, u32[]{:S(2)}, u32[]{:S(2)}) %all-to-all-start.2) | async-done | bytes 131104 | tf_op jit(solution)/shard_map/all_to_all | solution.py:285
  65.3 0.0 copy-done.3
  65.3 0.0 copy-done.4
  65.3 1.1 %shard_map.80 = bf16[256,384]{1,0:T(8,128)(2,1)} custom-call(bf16[512,128]{1,0:T(8,128)(2,1)S(1)} %bitcast.6, bf16[256,1152]{1,0:T(8,128)(2,1)S(1)} %get-tuple-element.34.phi_ref, f32[256,384]{1,0:T(8,128)S(1)} %get-tuple-element.35.intra_ref, f32[64,384]{1,0:T(8,128)S(1)} %shard_map.79.early_ref, f32[192,384]{1,0:T(8,128)S(1)} %copy-done.4, ...), custom_call_target="tpu_custom_call" | custom-call | flops 1400000000 | bytes 1574400 | tf_op jit(solution)/shard_map/pallas_call | solution.py:271
  (1 shorter events, 0.0 us)
Async XLA Ops:
  0.0 12.0 %copy-start.2 = (bf16[1536,96]{0,1:T(8,128)(2,1)S(1)}, bf16[1536,96]{0,1:T(8,128)(2,1)}, u32[]{:S(2)}) copy-start(bf16[1536,96]{0,1:T(8,128)(2,1)} %param.9) | copy-start | bytes 884740
  0.0 12.0 %copy-start = (bf16[1536,384]{1,0:T(8,128)(2,1)S(1)}, bf16[1536,384]{1,0:T(8,128)(2,1)}, u32[]{:S(2)}) copy-start(bf16[1536,384]{1,0:T(8,128)(2,1)} %wv_ref.3) | copy-start | bytes 3538948
  33.2 10.2 %copy-start.1 = (bf16[1536,384]{1,0:T(8,128)(2,1)S(1)}, bf16[1536,384]{1,0:T(8,128)(2,1)}, u32[]{:S(2)}) copy-start(bf16[1536,384]{1,0:T(8,128)(2,1)} %wk_ref.1) | copy-start | bytes 3538948
  34.0 16.9 %all-to-all-start.1 = ((bf16[8,32,128]{2,1,0:T(8,128)(2,1)}), bf16[8,32,128]{2,1,0:T(8,128)(2,1)S(1)}, u32[]{:S(2)}, u32[]{:S(2)}) async-start(bf16[8,32,128]{2,1,0:T(8,128)(2,1)} %shard_map.75), calls=%async_computation.1 | async-start | bytes 131072 | tf_op jit(solution)/shard_map/all_to_all | solution.py:285
  50.9 5.2 %copy-start.6 = (bf16[64,768]{1,0:T(8,128)(2,1)S(1)}, bf16[64,768]{1,0:T(8,128)(2,1)}, u32[]{:S(2)}) copy-start(bf16[64,768]{1,0:T(8,128)(2,1)} %get-tuple-element.38) | copy-start | bytes 294916
  50.9 11.0 %copy-start.5 = (bf16[64,1152]{1,0:T(8,128)(2,1)S(1)}, bf16[64,1152]{1,0:T(8,128)(2,1)}, u32[]{:S(2)}) copy-start(bf16[64,1152]{1,0:T(8,128)(2,1)} %get-tuple-element.37.head_ref) | copy-start | bytes 442372
  51.6 13.7 %all-to-all-start.2 = ((bf16[16,32,128]{2,1,0:T(8,128)(2,1)}), bf16[16,32,128]{2,1,0:T(8,128)(2,1)S(1)}, u32[]{:S(2)}, u32[]{:S(2)}) async-start(bf16[16,32,128]{2,1,0:T(8,128)(2,1)} %shard_map.78), calls=%async_computation.2 | async-start | bytes 262144 | tf_op jit(solution)/shard_map/all_to_all | solution.py:285
  56.1 9.2 %copy-start.3 = (f32[384]{0:T(512)S(1)}, f32[384]{0:T(512)}, u32[]{:S(2)}) copy-start(f32[384]{0:T(512)} %gain_ref.1) | copy-start | bytes 4612
  56.1 9.2 %copy-start.4 = (f32[192,384]{1,0:T(8,128)S(1)}, f32[192,384]{1,0:T(8,128)}, u32[]{:S(2)}) copy-start(f32[192,384]{1,0:T(8,128)} %get-tuple-element.39.window_ref) | copy-start | bytes 884740
  56.1 5.7 %collective-permute-start = (bf16[64,768]{1,0:T(8,128)(2,1)S(1)}, bf16[64,768]{1,0:T(8,128)(2,1)S(1)}, u32[]{:S(2)}, u32[]{:S(2)}) collective-permute-start(bf16[64,768]{1,0:T(8,128)(2,1)S(1)} %copy-done.6), channel_id=1, source_target_pairs={{0,4},{4,8},{8,12},{12,16},{16,20},{20,24},{24,28},{28,32},{32,36}... | collective-permute-start | bytes 294920 | tf_op jit(solution)/shard_map/ppermute | solution.py:361

commit v13 on v12

--- a/solution.py
+++ b/solution.py
@@ -340,15 +340,7 @@
             pltpu.SemaphoreType.DMA((5,)),
         ],
     )
-    intra, phi = call(
-        functools.partial(intra_kernel, rows, chunks),
-        [((rows, width), F32, vmem), ((rows, 3 * width), BF16, vmem)],
-        [(whole, vmem), (feature_q.T, hbm), (feature_k.T, hbm), (v, hbm)],
-        2200,
-    )
-    totals, window, head, halo, intra, phi = lax.optimization_barrier(
-        (totals, window, head, halo, intra, phi)
-    )
+    totals, window, head, halo, v = lax.optimization_barrier((totals, window, head, halo, v))
     (before,) = call(
         prefix_kernel,
         [(slices.shape, BF16, hbm)],
@@ -359,6 +351,12 @@
     prefix = exchange(before, PLANE).reshape(held, 128)
     devices = lax.axis_size(SEQ)
     halo = lax.ppermute(halo, SEQ, [(i, i + 1) for i in range(devices - 1)])
+    intra, phi = call(
+        functools.partial(intra_kernel, rows, chunks),
+        [((rows, width), F32, vmem), ((rows, 3 * width), BF16, vmem)],
+        [(whole, vmem), (feature_q.T, hbm), (feature_k.T, hbm), (v, hbm)],
+        700,
+    )
     (early,) = call(
         first_window_kernel,
         [((WIN, width), F32, vmem)],

time: 66.9 us -> 66.9 us (level)
    all_to_all x2, waiting for transfers between devices: 3.76 us -> 5.88 us  [exchange(): return lax.all_to_all(x, axis, split_axis=0, concat_axis=0, tiled=True)]
    ppermute x1, waiting for transfers between devices: 2.05 us -> 0.01 us  [body(): halo = lax.ppermute(halo, SEQ, [(i, i + 1) for i in range(devices - 1)])]
  transfers between devices with their start and end apart: 3 -> 3, of which waited for: 3 -> 2; matrix products, arithmetic and copies ran while one was open for 0% -> 0% of each run, Pallas kernels for 11% -> 11%
where the time goes in v13:
time: 66.9 us; the launch traced here: 66.5 us
  blocking collectives  32.2 us (48%)
  starting transfers between devices  17.5 us (26%)
  Pallas kernels  10.8 us (16%)
  waiting for transfers between devices  5.89 us (9%)
    all_to_all x1, blocking collectives, exchange(): return lax.all_to_all(x, axis, split_axis=0, concat_axis=0, tiled=True)  20.2 us
    all_to_all x2, starting transfers between devices, exchange(): return lax.all_to_all(x, axis, split_axis=0, concat_axis=0, tiled=True)  14 us
    all_gather x1, blocking collectives, body(): whole = lax.all_gather(hidden_states, 'head', tiled=True)  11.9 us
    pallas_call x8, Pallas kernels, call(): pl.pallas_call(kernel, out_shape=[space(shape, dtype) for shape, dtype, s...  10.8 us
    all_to_all x2, waiting for transfers between devices, exchange(): return lax.all_to_all(x, axis, split_axis=0, concat_axis=0, tiled=True)  5.88 us
    ppermute x1, starting transfers between devices, body(): halo = lax.ppermute(halo, SEQ, [(i, i + 1) for i in range(devices - 1)])  3.55 us
  transfers between devices with their start and end apart: 3, of which 2 were waited for; matrix products, arithmetic and copies ran while one was open for 0% of the time, Pallas kernels for 11%

profile of v13, /device:TPU:1, one launch (start us, length us, event | category | flops | bytes accessed | tf_op | source)
XLA Modules:
  0.0 66.5 jit_solution(10280489098538466461)
XLA Ops:
  0.0 0.0 copy-start
  0.0 0.0 copy-start.2
  0.0 11.9 %all_gather.3.x_ref = bf16[1024,384]{1,0:T(8,128)(2,1)S(1)} all-gather(bf16[256,384]{1,0:T(8,128)(2,1)} %param.7), channel_id=1, replica_groups=mesh['seq_0'=8,'seq_1'=8,'seq_2'=2,'head'=4] {'head'}, dimensions={0}, use_global_device_ids=true | all-gather | bytes 983040 | tf_op jit(solution)/shard_map/all_gather | solution.py:304
  12.0 0.0 copy-done
  12.0 0.0 copy-done.2
  12.0 1.1 %shard_map.74 = bf16[512,128]{1,0:T(8,128)(2,1)S(1)} custom-call(bf16[1024,384]{1,0:T(8,128)(2,1)S(1)} %all_gather.3.x_ref, bf16[96,1536]{1,0:T(8,128)(2,1)S(1)} %bitcast.9, bf16[1536,384]{1,0:T(8,128)(2,1)S(1)} %copy-done), custom_call_target="tpu_custom_call" | custom-call | flops 1500000000 | bytes 2260992 | tf_op jit(solution)/shard_map/pallas_call | solution.py:271
  13.0 20.2 %all_to_all.15.slices_ref = bf16[16,32,128]{2,1,0:T(8,128)(2,1)S(1)} all-to-all(bf16[16,32,128]{2,1,0:T(8,128)(2,1)S(1)} %bitcast.7), channel_id=1, replica_groups=mesh['seq_0'=8,'seq_1'=8,'seq_2'=2,'head'=4] {'seq_1','seq_2'}, dimensions={0} | all-to-all | bytes 262144 | tf_op jit(solution)/shard_map/all_to_all | solution.py:285
  33.2 0.0 copy-start.1
  33.2 0.7 %shard_map.75 = bf16[8,32,128]{2,1,0:T(8,128)(2,1)} custom-call(bf16[16,32,128]{2,1,0:T(8,128)(2,1)S(1)} %all_to_all.15.slices_ref), custom_call_target="tpu_custom_call" | custom-call | flops 600000000 | bytes 131072 | tf_op jit(solution)/shard_map/pallas_call | solution.py:271
  34.0 9.5 %all-to-all-start.1 = ((bf16[8,32,128]{2,1,0:T(8,128)(2,1)}), bf16[8,32,128]{2,1,0:T(8,128)(2,1)S(1)}, u32[]{:S(2)}, u32[]{:S(2)}) async-start(bf16[8,32,128]{2,1,0:T(8,128)(2,1)} %shard_map.75), calls=%async_computation.1 | async-start | bytes 131072 | tf_op jit(solution)/shard_map/all_to_all | solution.py:285
  43.5 0.0 copy-done.1
  43.5 4.2 %shard_map.76 = (f32[192,384]{1,0:T(8,128)}, bf16[64,1152]{1,0:T(8,128)(2,1)}, bf16[64,768]{1,0:T(8,128)(2,1)}, bf16[256,384]{1,0:T(8,128)(2,1)}) custom-call(bf16[1024,384]{1,0:T(8,128)(2,1)S(1)} %all_gather.3.x_ref, bf16[1536,384]{1,0:T(8,128)(2,1)} %wq_hbm.1, bf16[1536,384]{1,0:T(8,128)(2,1)S(1)} %copy-done.1, bf16[1536,384]{1,0:T(8,128)(2,1)S(1)} %copy-done), custom_call_target="tpu_custom_call" | custom-call | flops 3900000000 | bytes 4325376 | tf_op jit(solution)/shard_map/pallas_call | solution.py:271
  47.7 3.2 %all-to-all-done.1.totals_ref = bf16[8,32,128]{2,1,0:T(8,128)(2,1)S(1)} async-done(((bf16[8,32,128]{2,1,0:T(8,128)(2,1)}), bf16[8,32,128]{2,1,0:T(8,128)(2,1)S(1)}, u32[]{:S(2)}, u32[]{:S(2)}) %all-to-all-start.1) | async-done | bytes 65568 | tf_op jit(solution)/shard_map/all_to_all | solution.py:285
  50.9 0.0 copy-start.6
  50.9 0.7 %shard_map.77 = bf16[16,32,128]{2,1,0:T(8,128)(2,1)} custom-call(s32[1]{0:T(128)} %bitcast.plane_ref, bf16[16,32,128]{2,1,0:T(8,128)(2,1)S(1)} %all_to_all.15.slices_ref, bf16[8,32,128]{2,1,0:T(8,128)(2,1)S(1)} %all-to-all-done.1.totals_ref), custom_call_target="tpu_custom_call" | custom-call | flops 1000000000 | bytes 196612 | tf_op jit(solution)/shard_map/pallas_call | solution.py:271
  51.6 4.5 %all-to-all-start.2 = ((bf16[16,32,128]{2,1,0:T(8,128)(2,1)}), bf16[16,32,128]{2,1,0:T(8,128)(2,1)S(1)}, u32[]{:S(2)}, u32[]{:S(2)}) async-start(bf16[16,32,128]{2,1,0:T(8,128)(2,1)} %shard_map.77), calls=%async_computation.2 | async-start | bytes 262144 | tf_op jit(solution)/shard_map/all_to_all | solution.py:285
  56.1 0.0 copy-done.6
  56.1 3.5 %collective-permute-start = (bf16[64,768]{1,0:T(8,128)(2,1)S(1)}, bf16[64,768]{1,0:T(8,128)(2,1)S(1)}, u32[]{:S(2)}, u32[]{:S(2)}) collective-permute-start(bf16[64,768]{1,0:T(8,128)(2,1)S(1)} %copy-done.6), channel_id=1, source_target_pairs={{0,4},{4,8},{8,12},{12,16},{16,20},{20,24},{24,28},{28,32},{32,36}... | collective-permute-start | bytes 294920 | tf_op jit(solution)/shard_map/ppermute | solution.py:353
  59.7 0.0 copy-start.5
  59.7 2.5 %shard_map.78 = (f32[256,384]{1,0:T(8,128)S(1)}, bf16[256,1152]{1,0:T(8,128)(2,1)S(1)}) custom-call(bf16[1024,384]{1,0:T(8,128)(2,1)S(1)} %all_gather.3.x_ref, bf16[96,1536]{1,0:T(8,128)(2,1)} %bitcast.10, bf16[96,1536]{1,0:T(8,128)(2,1)} %bitcast.8, bf16[256,384]{1,0:T(8,128)(2,1)} %get-tuple-element.31.v_ref), custom_call_target="tpu_custom_call" | custom-call | flops 700000000 | bytes 1572864 | tf_op jit(solution)/shard_map/pallas_call | solution.py:271
  62.1 0.0 copy-start.3
  62.2 0.0 copy-start.4
  62.2 0.0 collective-permute-done.halo_ref
  62.2 0.0 copy-done.5
  62.2 0.5 shard_map.79.early_ref
  62.7 2.7 %all-to-all-done.2 = bf16[16,32,128]{2,1,0:T(8,128)(2,1)S(1)} async-done(((bf16[16,32,128]{2,1,0:T(8,128)(2,1)}), bf16[16,32,128]{2,1,0:T(8,128)(2,1)S(1)}, u32[]{:S(2)}, u32[]{:S(2)}) %all-to-all-start.2) | async-done | bytes 131104 | tf_op jit(solution)/shard_map/all_to_all | solution.py:285
  65.3 0.0 copy-done.3
  65.3 0.0 copy-done.4
  65.4 1.1 %shard_map.80 = bf16[256,384]{1,0:T(8,128)(2,1)} custom-call(bf16[512,128]{1,0:T(8,128)(2,1)S(1)} %bitcast.6, bf16[256,1152]{1,0:T(8,128)(2,1)S(1)} %get-tuple-element.32.phi_ref, f32[256,384]{1,0:T(8,128)S(1)} %get-tuple-element.33.intra_ref, f32[64,384]{1,0:T(8,128)S(1)} %shard_map.79.early_ref, f32[192,384]{1,0:T(8,128)S(1)} %copy-done.4, ...), custom_call_target="tpu_custom_call" | custom-call | flops 1400000000 | bytes 1574400 | tf_op jit(solution)/shard_map/pallas_call | solution.py:271
  (1 shorter events, 0.0 us)
Async XLA Ops:
  0.0 12.0 %copy-start = (bf16[1536,384]{1,0:T(8,128)(2,1)S(1)}, bf16[1536,384]{1,0:T(8,128)(2,1)}, u32[]{:S(2)}) copy-start(bf16[1536,384]{1,0:T(8,128)(2,1)} %wv_ref.3) | copy-start | bytes 3538948
  0.0 12.0 %copy-start.2 = (bf16[1536,96]{0,1:T(8,128)(2,1)S(1)}, bf16[1536,96]{0,1:T(8,128)(2,1)}, u32[]{:S(2)}) copy-start(bf16[1536,96]{0,1:T(8,128)(2,1)} %param.9) | copy-start | bytes 884740
  33.2 10.2 %copy-start.1 = (bf16[1536,384]{1,0:T(8,128)(2,1)S(1)}, bf16[1536,384]{1,0:T(8,128)(2,1)}, u32[]{:S(2)}) copy-start(bf16[1536,384]{1,0:T(8,128)(2,1)} %wk_ref.1) | copy-start | bytes 3538948
  34.0 16.9 %all-to-all-start.1 = ((bf16[8,32,128]{2,1,0:T(8,128)(2,1)}), bf16[8,32,128]{2,1,0:T(8,128)(2,1)S(1)}, u32[]{:S(2)}, u32[]{:S(2)}) async-start(bf16[8,32,128]{2,1,0:T(8,128)(2,1)} %shard_map.75), calls=%async_computation.1 | async-start | bytes 131072 | tf_op jit(solution)/shard_map/all_to_all | solution.py:285
  50.9 5.2 %copy-start.6 = (bf16[64,768]{1,0:T(8,128)(2,1)S(1)}, bf16[64,768]{1,0:T(8,128)(2,1)}, u32[]{:S(2)}) copy-start(bf16[64,768]{1,0:T(8,128)(2,1)} %get-tuple-element.36) | copy-start | bytes 294916
  51.6 13.7 %all-to-all-start.2 = ((bf16[16,32,128]{2,1,0:T(8,128)(2,1)}), bf16[16,32,128]{2,1,0:T(8,128)(2,1)S(1)}, u32[]{:S(2)}, u32[]{:S(2)}) async-start(bf16[16,32,128]{2,1,0:T(8,128)(2,1)} %shard_map.77), calls=%async_computation.2 | async-start | bytes 262144 | tf_op jit(solution)/shard_map/all_to_all | solution.py:285
  56.1 6.1 %collective-permute-start = (bf16[64,768]{1,0:T(8,128)(2,1)S(1)}, bf16[64,768]{1,0:T(8,128)(2,1)S(1)}, u32[]{:S(2)}, u32[]{:S(2)}) collective-permute-start(bf16[64,768]{1,0:T(8,128)(2,1)S(1)} %copy-done.6), channel_id=1, source_target_pairs={{0,4},{4,8},{8,12},{12,16},{16,20},{20,24},{24,28},{28,32},{32,36}... | collective-permute-start | bytes 294920 | tf_op jit(solution)/shard_map/ppermute | solution.py:353
  59.7 2.5 %copy-start.5 = (bf16[64,1152]{1,0:T(8,128)(2,1)S(1)}, bf16[64,1152]{1,0:T(8,128)(2,1)}, u32[]{:S(2)}) copy-start(bf16[64,1152]{1,0:T(8,128)(2,1)} %get-tuple-element.35.head_ref) | copy-start | bytes 442372
  62.1 3.2 %copy-start.3 = (f32[384]{0:T(512)S(1)}, f32[384]{0:T(512)}, u32[]{:S(2)}) copy-start(f32[384]{0:T(512)} %gain_ref.1) | copy-start | bytes 4612
  62.2 3.2 %copy-start.4 = (f32[192,384]{1,0:T(8,128)S(1)}, f32[192,384]{1,0:T(8,128)}, u32[]{:S(2)}) copy-start(f32[192,384]{1,0:T(8,128)} %get-tuple-element.37.window_ref) | copy-start | bytes 884740

commit v14 on v12

--- a/solution.py
+++ b/solution.py
@@ -203,12 +203,12 @@
     total = slices_ref[0].astype(F32)
     for i in range(1, slices_ref.shape[0]):
         total = total + slices_ref[i].astype(F32)
-    total_ref[...] = total.astype(BF16)
-    stores = [pltpu.make_async_copy(total_ref, out_hbm.at[z], sem.at[z]) for z in range(out_hbm.shape[0])]
-    for store in stores:
-        store.start()
-    for store in stores:
-        store.wait()
+    total = total.astype(BF16)
+    for z in range(total_ref.shape[0]):
+        total_ref[z] = total
+    store = pltpu.make_async_copy(total_ref, out_hbm, sem)
+    store.start()
+    store.wait()
 
 
 def prefix_kernel(plane_ref, slices_ref, totals_ref, out_hbm, out_ref, sem):
@@ -317,7 +317,7 @@
         [((planes, *piece_shape), BF16, hbm)],
         [(slices, vmem)],
         600,
-        scratch=[pltpu.VMEM(piece_shape, BF16), pltpu.SemaphoreType.DMA((planes,))],
+        scratch=[pltpu.VMEM((planes, *piece_shape), BF16), pltpu.SemaphoreType.DMA(())],
     )
     totals = exchange(totals, "seq_0")
     window, head, halo, v = call(
@@ -354,7 +354,7 @@
         [(slices.shape, BF16, hbm)],
         [(plane, smem), (slices, vmem), (totals, vmem)],
         1000,
-        scratch=[pltpu.VMEM(slices.shape, BF16), pltpu.SemaphoreType.DMA((4,))],
+        scratch=[pltpu.VMEM(slices.shape, BF16), pltpu.SemaphoreType.DMA((2,))],
     )
     prefix = exchange(before, PLANE).reshape(held, 128)
     devices = lax.axis_size(SEQ)

time: 66.9 us -> 66.8 us (level)
  no operation moved by 1% of the time
where the time goes in v14:
time: 66.8 us; the launch traced here: 66.4 us
  blocking collectives  32.2 us (48%)
  starting transfers between devices  17.7 us (26%)
  Pallas kernels  10.6 us (16%)
  waiting for transfers between devices  5.81 us (9%)
    all_to_all x1, blocking collectives, exchange(): return lax.all_to_all(x, axis, split_axis=0, concat_axis=0, tiled=True)  20.2 us
    all_to_all x2, starting transfers between devices, exchange(): return lax.all_to_all(x, axis, split_axis=0, concat_axis=0, tiled=True)  14 us
    all_gather x1, blocking collectives, body(): whole = lax.all_gather(hidden_states, 'head', tiled=True)  11.9 us
    pallas_call x8, Pallas kernels, call(): pl.pallas_call(kernel, out_shape=[space(shape, dtype) for shape, dtype, s...  10.6 us
    all_to_all x2, waiting for transfers between devices, exchange(): return lax.all_to_all(x, axis, split_axis=0, concat_axis=0, tiled=True)  3.76 us
    ppermute x1, starting transfers between devices, body(): halo = lax.ppermute(halo, SEQ, [(i, i + 1) for i in range(devices - 1)])  3.68 us
    ppermute x1, waiting for transfers between devices, body(): halo = lax.ppermute(halo, SEQ, [(i, i + 1) for i in range(devices - 1)])  2.05 us
  transfers between devices with their start and end apart: 3, of which 3 were waited for; matrix products, arithmetic and copies ran while one was open for 0% of the time, Pallas kernels for 11%

profile of v14, /device:TPU:1, one launch (start us, length us, event | category | flops | bytes accessed | tf_op | source)
XLA Modules:
  0.0 66.4 jit_solution(10918610045293589856)
XLA Ops:
  0.0 0.0 copy-start.2
  0.0 0.0 copy-start
  0.0 11.9 %all_gather.3.x_ref = bf16[1024,384]{1,0:T(8,128)(2,1)S(1)} all-gather(bf16[256,384]{1,0:T(8,128)(2,1)} %param.7), channel_id=1, replica_groups=mesh['seq_0'=8,'seq_1'=8,'seq_2'=2,'head'=4] {'head'}, dimensions={0}, use_global_device_ids=true | all-gather | bytes 983040 | tf_op jit(solution)/shard_map/all_gather | solution.py:304
  12.0 0.0 copy-done.2
  12.0 0.0 copy-done
  12.0 1.1 %shard_map.74 = bf16[512,128]{1,0:T(8,128)(2,1)S(1)} custom-call(bf16[1024,384]{1,0:T(8,128)(2,1)S(1)} %all_gather.3.x_ref, bf16[96,1536]{1,0:T(8,128)(2,1)S(1)} %bitcast.9, bf16[1536,384]{1,0:T(8,128)(2,1)S(1)} %copy-done), custom_call_target="tpu_custom_call" | custom-call | flops 1500000000 | bytes 2260992 | tf_op jit(solution)/shard_map/pallas_call | solution.py:271
  13.0 20.2 %all_to_all.15.slices_ref = bf16[16,32,128]{2,1,0:T(8,128)(2,1)S(1)} all-to-all(bf16[16,32,128]{2,1,0:T(8,128)(2,1)S(1)} %bitcast.7), channel_id=1, replica_groups=mesh['seq_0'=8,'seq_1'=8,'seq_2'=2,'head'=4] {'seq_1','seq_2'}, dimensions={0} | all-to-all | bytes 262144 | tf_op jit(solution)/shard_map/all_to_all | solution.py:285
  33.2 0.0 copy-start.1
  33.2 0.6 shard_map.75
  33.9 9.5 %all-to-all-start.1 = ((bf16[8,32,128]{2,1,0:T(8,128)(2,1)}), bf16[8,32,128]{2,1,0:T(8,128)(2,1)S(1)}, u32[]{:S(2)}, u32[]{:S(2)}) async-start(bf16[8,32,128]{2,1,0:T(8,128)(2,1)} %shard_map.75), calls=%async_computation.1 | async-start | bytes 131072 | tf_op jit(solution)/shard_map/all_to_all | solution.py:285
  43.4 0.0 copy-done.1
  43.4 4.2 %shard_map.76 = (f32[192,384]{1,0:T(8,128)}, bf16[64,1152]{1,0:T(8,128)(2,1)}, bf16[64,768]{1,0:T(8,128)(2,1)}, bf16[256,384]{1,0:T(8,128)(2,1)}) custom-call(bf16[1024,384]{1,0:T(8,128)(2,1)S(1)} %all_gather.3.x_ref, bf16[1536,384]{1,0:T(8,128)(2,1)} %wq_hbm.1, bf16[1536,384]{1,0:T(8,128)(2,1)S(1)} %copy-done.1, bf16[1536,384]{1,0:T(8,128)(2,1)S(1)} %copy-done), custom_call_target="tpu_custom_call" | custom-call | flops 3900000000 | bytes 4325376 | tf_op jit(solution)/shard_map/pallas_call | solution.py:271
  47.6 2.4 %shard_map.77 = (f32[256,384]{1,0:T(8,128)S(1)}, bf16[256,1152]{1,0:T(8,128)(2,1)S(1)}) custom-call(bf16[1024,384]{1,0:T(8,128)(2,1)S(1)} %all_gather.3.x_ref, bf16[96,1536]{1,0:T(8,128)(2,1)} %bitcast.10, bf16[96,1536]{1,0:T(8,128)(2,1)} %bitcast.8, bf16[256,384]{1,0:T(8,128)(2,1)} %get-tuple-element.30.v_ref), custom_call_target="tpu_custom_call" | custom-call | flops 2200000000 | bytes 1572864 | tf_op jit(solution)/shard_map/pallas_call | solution.py:271
  50.0 0.8 %all-to-all-done.1.totals_ref = bf16[8,32,128]{2,1,0:T(8,128)(2,1)S(1)} async-done(((bf16[8,32,128]{2,1,0:T(8,128)(2,1)}), bf16[8,32,128]{2,1,0:T(8,128)(2,1)S(1)}, u32[]{:S(2)}, u32[]{:S(2)}) %all-to-all-start.1) | async-done | bytes 65568 | tf_op jit(solution)/shard_map/all_to_all | solution.py:285
  50.8 0.0 copy-start.6
  50.8 0.0 copy-start.5
  50.8 0.7 %shard_map.78 = bf16[16,32,128]{2,1,0:T(8,128)(2,1)} custom-call(s32[1]{0:T(128)} %bitcast.plane_ref, bf16[16,32,128]{2,1,0:T(8,128)(2,1)S(1)} %all_to_all.15.slices_ref, bf16[8,32,128]{2,1,0:T(8,128)(2,1)S(1)} %all-to-all-done.1.totals_ref), custom_call_target="tpu_custom_call" | custom-call | flops 1000000000 | bytes 196612 | tf_op jit(solution)/shard_map/pallas_call | solution.py:271
  51.5 4.5 %all-to-all-start.2 = ((bf16[16,32,128]{2,1,0:T(8,128)(2,1)}), bf16[16,32,128]{2,1,0:T(8,128)(2,1)S(1)}, u32[]{:S(2)}, u32[]{:S(2)}) async-start(bf16[16,32,128]{2,1,0:T(8,128)(2,1)} %shard_map.78), calls=%async_computation.2 | async-start | bytes 262144 | tf_op jit(solution)/shard_map/all_to_all | solution.py:285
  56.0 0.0 copy-done.6
  56.0 0.0 copy-start.3
  56.0 0.0 copy-start.4
  56.1 3.7 %collective-permute-start = (bf16[64,768]{1,0:T(8,128)(2,1)S(1)}, bf16[64,768]{1,0:T(8,128)(2,1)S(1)}, u32[]{:S(2)}, u32[]{:S(2)}) collective-permute-start(bf16[64,768]{1,0:T(8,128)(2,1)S(1)} %copy-done.6), channel_id=1, source_target_pairs={{0,4},{4,8},{8,12},{12,16},{16,20},{20,24},{24,28},{28,32},{32,36}... | collective-permute-start | bytes 294920 | tf_op jit(solution)/shard_map/ppermute | solution.py:361
  59.7 2.1 %collective-permute-done.halo_ref = bf16[64,768]{1,0:T(8,128)(2,1)S(1)} collective-permute-done((bf16[64,768]{1,0:T(8,128)(2,1)S(1)}, bf16[64,768]{1,0:T(8,128)(2,1)S(1)}, u32[]{:S(2)}, u32[]{:S(2)}) %collective-permute-start) | collective-permute-done | bytes 98336 | tf_op jit(solution)/shard_map/ppermute | solution.py:361
  61.8 0.0 copy-done.5
  61.8 0.5 shard_map.79.early_ref
  62.3 3.0 %all-to-all-done.2 = bf16[16,32,128]{2,1,0:T(8,128)(2,1)S(1)} async-done(((bf16[16,32,128]{2,1,0:T(8,128)(2,1)}), bf16[16,32,128]{2,1,0:T(8,128)(2,1)S(1)}, u32[]{:S(2)}, u32[]{:S(2)}) %all-to-all-start.2) | async-done | bytes 131104 | tf_op jit(solution)/shard_map/all_to_all | solution.py:285
  65.3 0.0 copy-done.3
  65.3 0.0 copy-done.4
  65.3 1.1 %shard_map.80 = bf16[256,384]{1,0:T(8,128)(2,1)} custom-call(bf16[512,128]{1,0:T(8,128)(2,1)S(1)} %bitcast.6, bf16[256,1152]{1,0:T(8,128)(2,1)S(1)} %get-tuple-element.34.phi_ref, f32[256,384]{1,0:T(8,128)S(1)} %get-tuple-element.35.intra_ref, f32[64,384]{1,0:T(8,128)S(1)} %shard_map.79.early_ref, f32[192,384]{1,0:T(8,128)S(1)} %copy-done.4, ...), custom_call_target="tpu_custom_call" | custom-call | flops 1400000000 | bytes 1574400 | tf_op jit(solution)/shard_map/pallas_call | solution.py:271
  (1 shorter events, 0.0 us)
Async XLA Ops:
  0.0 12.0 %copy-start.2 = (bf16[1536,96]{0,1:T(8,128)(2,1)S(1)}, bf16[1536,96]{0,1:T(8,128)(2,1)}, u32[]{:S(2)}) copy-start(bf16[1536,96]{0,1:T(8,128)(2,1)} %param.9) | copy-start | bytes 884740
  0.0 12.0 %copy-start = (bf16[1536,384]{1,0:T(8,128)(2,1)S(1)}, bf16[1536,384]{1,0:T(8,128)(2,1)}, u32[]{:S(2)}) copy-start(bf16[1536,384]{1,0:T(8,128)(2,1)} %wv_ref.3) | copy-start | bytes 3538948
  33.2 10.1 %copy-start.1 = (bf16[1536,384]{1,0:T(8,128)(2,1)S(1)}, bf16[1536,384]{1,0:T(8,128)(2,1)}, u32[]{:S(2)}) copy-start(bf16[1536,384]{1,0:T(8,128)(2,1)} %wk_ref.1) | copy-start | bytes 3538948
  33.9 16.9 %all-to-all-start.1 = ((bf16[8,32,128]{2,1,0:T(8,128)(2,1)}), bf16[8,32,128]{2,1,0:T(8,128)(2,1)S(1)}, u32[]{:S(2)}, u32[]{:S(2)}) async-start(bf16[8,32,128]{2,1,0:T(8,128)(2,1)} %shard_map.75), calls=%async_computation.1 | async-start | bytes 131072 | tf_op jit(solution)/shard_map/all_to_all | solution.py:285
  50.8 5.2 %copy-start.6 = (bf16[64,768]{1,0:T(8,128)(2,1)S(1)}, bf16[64,768]{1,0:T(8,128)(2,1)}, u32[]{:S(2)}) copy-start(bf16[64,768]{1,0:T(8,128)(2,1)} %get-tuple-element.38) | copy-start | bytes 294916
  50.8 11.0 %copy-start.5 = (bf16[64,1152]{1,0:T(8,128)(2,1)S(1)}, bf16[64,1152]{1,0:T(8,128)(2,1)}, u32[]{:S(2)}) copy-start(bf16[64,1152]{1,0:T(8,128)(2,1)} %get-tuple-element.37.head_ref) | copy-start | bytes 442372
  51.5 13.7 %all-to-all-start.2 = ((bf16[16,32,128]{2,1,0:T(8,128)(2,1)}), bf16[16,32,128]{2,1,0:T(8,128)(2,1)S(1)}, u32[]{:S(2)}, u32[]{:S(2)}) async-start(bf16[16,32,128]{2,1,0:T(8,128)(2,1)} %shard_map.78), calls=%async_computation.2 | async-start | bytes 262144 | tf_op jit(solution)/shard_map/all_to_all | solution.py:285
  56.0 9.2 %copy-start.3 = (f32[384]{0:T(512)S(1)}, f32[384]{0:T(512)}, u32[]{:S(2)}) copy-start(f32[384]{0:T(512)} %gain_ref.1) | copy-start | bytes 4612
  56.0 9.2 %copy-start.4 = (f32[192,384]{1,0:T(8,128)S(1)}, f32[192,384]{1,0:T(8,128)}, u32[]{:S(2)}) copy-start(f32[192,384]{1,0:T(8,128)} %get-tuple-element.39.window_ref) | copy-start | bytes 884740
  56.1 5.7 %collective-permute-start = (bf16[64,768]{1,0:T(8,128)(2,1)S(1)}, bf16[64,768]{1,0:T(8,128)(2,1)S(1)}, u32[]{:S(2)}, u32[]{:S(2)}) collective-permute-start(bf16[64,768]{1,0:T(8,128)(2,1)S(1)} %copy-done.6), channel_id=1, source_target_pairs={{0,4},{4,8},{8,12},{12,16},{16,20},{20,24},{24,28},{28,32},{32,36}... | collective-permute-start | bytes 294920 | tf_op jit(solution)/shard_map/ppermute | solution.py:361
